TPU v7x, 512 devices: a whole 4x8x8 slice. The times are simulated.
512 devices in a mesh: leaf: 64 (over z, y), sep: 8 (over x, core).
Axes of the slice: x: 4, y: 8, z: 8, core: 2. Of those that a mesh axis runs over, the one named last changes fastest.
Arguments:
- shot_columns: float32 [64, 8, 1536, 256], P('leaf', 'sep'), may hold values from -6 to 6
- factor_tiles: bfloat16 [64, 8, 12, 4, 128, 128], P('leaf', 'sep'), may hold values from -0.25 to 0.25
- factor_cols: int32 [64, 8, 12, 4], P('leaf', 'sep'), may hold values from 0 to 11, all different within a row
- boundary_rows: int32 [64, 8, 64], P('leaf', 'sep'), may hold values from 0 to 1535
- boundary_map: int32 [64, 8, 64], P('leaf', 'sep'), may hold values from 0 to 2047
- boundary_count: int32 [64, 8], P('leaf', 'sep'), may hold values from 16 to 64, as said below
- separator_load: float32 [8, 2048, 256], P('sep', 'leaf'), may hold values from -6 to 6
- inverse_tiles: bfloat16 [8, 2048, 8, 4, 128], P(None, 'leaf', 'sep'), may hold values from -0.09375 to 0.09375
- inverse_cols: int32 [8, 64, 8, 4], P(None, 'leaf', 'sep'), may hold values from 0 to 15, all different within a row
Outputs:
- leaf_solution: float32 [64, 8, 1536, 256], P('leaf', 'sep')
- separator_solution: float32 [8, 2048, 256], P('sep', 'leaf')
Inputs may be any that keep to these rules, and one draw needn't show every extreme that they name: `boundary_count`: some leaf section has exactly 64 live boundary rows in every draw.
All inputs are finite; a program needn't handle non-finite values.
Results may differ from a plain program's by a relative error of at most 0.0036.
Values may be sent and summed in bfloat16 or wider, within the bound.
No kernel may reach another device: no remote copies, remote signals or barrier semaphores. Data moves between devices by JAX's collectives and lax.ppermute only.
A program may use at most 64 MiB of HBM per device.

v0:
```python
import jax
import jax.numpy as jnp
from jax import lax
from jax.sharding import PartitionSpec as P

TILE = 128


def forward_local(tiles, tile_cols, vector):
    width = vector.shape[-1]
    tiled_rows = vector.astype(jnp.bfloat16).reshape(-1, TILE, width)
    picked = tiled_rows[tile_cols]
    product = jnp.einsum("tkab,tkbn->tan", tiles, picked, preferred_element_type=jnp.float32)
    return product.reshape(-1, width)


def flipped_local_block(tiles, tile_cols, vector):
    width = vector.shape[-1]
    count_rows = tiles.shape[0]
    tiled_rows = vector.astype(jnp.bfloat16).reshape(count_rows, TILE, width)
    addend_tiles = jnp.einsum(
        "tkab,tan->tkbn", tiles, tiled_rows, preferred_element_type=jnp.float32
    )
    picking_mask = (
        tile_cols[None, :, :] == jnp.arange(count_rows, dtype=jnp.int32)[:, None, None]
    ).astype(jnp.float32)
    reduced_total = jnp.einsum(
        "jia,iale->jle", picking_mask, addend_tiles, precision=lax.Precision.HIGHEST
    )
    return reduced_total.reshape(-1, width)


def body(
    shot_columns,
    factor_tiles,
    factor_cols,
    boundary_rows,
    boundary_map,
    boundary_count,
    separator_load,
    inverse_tiles,
    inverse_cols,
):
    tiles = factor_tiles[0, 0]
    tile_cols = factor_cols[0, 0]
    width = shot_columns.shape[-1]
    forward = forward_local(tiles, tile_cols, shot_columns[0, 0])
    own_rows = boundary_rows[0, 0]
    own_map = boundary_map[0, 0]
    live_mask = jnp.arange(own_rows.shape[0], dtype=jnp.int32) < boundary_count[0, 0]
    boundary_values = jnp.where(live_mask[:, None], forward[own_rows], jnp.float32(0.0))
    strip_count = separator_load.shape[1]
    section_rows = strip_count * lax.axis_size("leaf")
    leaf_index = lax.axis_index("leaf")
    desired_output = jnp.concatenate(
        [own_map, leaf_index * strip_count + jnp.arange(strip_count, dtype=jnp.int32)]
    )
    entries = jnp.concatenate([-boundary_values, separator_load[0]], axis=0)
    partial_value = jax.ops.segment_sum(entries, desired_output, num_segments=section_rows)
    residual = lax.psum(partial_value, "leaf").astype(jnp.bfloat16)
    column_tiles = residual.reshape(-1, TILE, width)
    picked = column_tiles[inverse_cols[:, 0, 0, :]]
    strip_tiles = inverse_tiles[:, :, 0]
    own_block = lax.psum_scatter(
        jnp.einsum("qikc,qkcn->qin", strip_tiles, picked, preferred_element_type=jnp.float32),
        "sep",
        scatter_dimension=0,
        tiled=True,
    )
    section_solution = lax.all_gather(own_block[0], "leaf", axis=0, tiled=True)
    needed = jnp.where(live_mask[:, None], section_solution[own_map], jnp.float32(0.0))
    corrected = forward.at[own_rows].add(-needed)
    leaf_solution = flipped_local_block(tiles, tile_cols, corrected)
    return (leaf_solution[None, None], own_block)


def solution(mesh):
    placed = (
        P("leaf", "sep", None, None),
        P("leaf", "sep", None, None, None, None),
        P("leaf", "sep", None, None),
        P("leaf", "sep", None),
        P("leaf", "sep", None),
        P("leaf", "sep"),
        P("sep", "leaf", None),
        P(None, "leaf", "sep", None, None),
        P(None, "leaf", "sep", None),
    )
    return jax.shard_map(
        body,
        mesh=mesh,
        in_specs=placed,
        out_specs=(P("leaf", "sep", None, None), P("sep", "leaf", None)),
        check_vma=False,
    )
```

profile of v0, /device:TPU:4, one launch (start us, length us, event | category | flops | bytes accessed | tf_op | source)
XLA Modules:
  0.0 481.6 jit_solution(15578592426343926049)
XLA Ops:
  8.0 0.7 fusion.23
  8.7 0.7 compare_select_fusion
  9.4 0.1 copy.15
  9.4 0.1 reshape.154
  9.5 0.7 compare_select_fusion.1
  10.2 0.1 copy.14
  10.3 0.1 reshape.138
  10.4 1.5 convert_element_type.14
  12.0 2.5 gather_fusion
  14.5 2.6 fusion.7
  17.1 0.7 gather_fusion.1
  17.8 0.1 select_negate_fusion
  17.9 2.5 scatter_custom_fusion
  20.4 309.6 %all-reduce.1 = bf16[2048,256]{1,0:T(8,128)(2,1)} all-reduce(f32[2048,256]{1,0:T(8,128)} %scatter_custom_fusion), channel_id=1, replica_groups=mesh['leaf'=64,'sep'=8] {'leaf'}, use_global_device_ids=true, to_apply=%region_1.2 | all-reduce | flops 524288 | bytes 3145728 | tf_op jit(solution)/shard_map/psum | solution.py:60
  329.9 3.3 gather_fusion.2
  333.2 2.7 convolution_bitcast_fusion
  336.1 23.2 %reduce-scatter.2.cloned.1.call-done = f32[1,32,256]{2,1,0:T(8,128)} async-done(((f32[8,32,256]{2,1,0:T(8,128)}), f32[1,32,256]{2,1,0:T(8,128)}) %reduce-scatter.2.cloned.1.call-update) | async-done | bytes 32784 | tf_op jit(solution)/shard_map/reduce_scatter | solution.py:64
  359.3 90.9 %all-gather.3.cloned.1.call-done = f32[1,2048,256]{2,1,0:T(8,128)} async-done(((f32[1,32,256]{2,1,0:T(8,128)}), f32[1,2048,256]{2,1,0:T(8,128)}) %all-gather.3.cloned.1.call-update) | async-done | bytes 2097168 | tf_op jit(solution)/shard_map/all_gather | solution.py:70
  450.2 2.6 scatter_custom_fusion.1
  452.8 0.1 convert_element_type.17
  452.9 3.7 fusion.5
  456.6 9.5 %copy.21 = f32[12,256,4,128]{1,0,2,3:T(8,128)} copy(f32[12,256,4,128]{3,1,2,0:T(8,128)} %fusion.5) | data formatting | bytes 12582912 | tf_op jit(solution)/shard_map/tkab,tan->tkbn/dot_general | solution.py:21
  466.1 6.6 %fusion.2 = f32[12,128,256]{2,0,1:T(8,128)S(1)} fusion(f32[12,256,4,128]{1,0,2,3:T(8,128)} %copy.21, s32[12,4]{0,1:T(4,128)S(1)} %bitcast.74), kind=kOutput, calls=%fused_computation.8 | convolution fusion | flops 226492992 | bytes 7864512 | tf_op jit(solution)/shard_map/jia,iale->jle/dot_general | solution.py:27
  472.7 2.1 copy.17
  (22 shorter events, 0.3 us)
Async XLA Ops:
  7.2 7.4 %copy-start = (bf16[1,1,12,4,128,128]{5,4,3,2,1,0:T(8,128)(2,1)S(1)}, bf16[1,1,12,4,128,128]{5,4,3,2,1,0:T(8,128)(2,1)}, u32[]{:S(2)}) copy-start(bf16[1,1,12,4,128,128]{5,4,3,2,1,0:T(8,128)(2,1)} %param.10) | copy-start | bytes 4718596
  7.2 4.7 copy-start.4
  7.2 352.0 %reduce-scatter.2.cloned.1.call-start = ((), (), s32[]{:S(2)}) async-start(), calls=%async_computation.1 | async-start | bytes 294912 | tf_op jit(solution)/shard_map/reduce_scatter | solution.py:64
  14.5 3.3 copy-start.2
  329.9 3.3 copy-start.1
  336.0 114.2 %all-gather.3.cloned.1.call-start = ((), (), s32[]{:S(2)}) async-start(), calls=%async_computation.2 | async-start | bytes 2129920 | tf_op jit(solution)/shard_map/all_gather | solution.py:70
  456.6 9.5 %copy-start.3 = (s32[1,1,12,4]{2,3,1,0:T(4,128)S(1)}, s32[1,1,12,4]{2,3,1,0:T(4,128)}, u32[]{:S(2)}) copy-start(s32[1,1,12,4]{2,3,1,0:T(4,128)} %param.11) | copy-start | bytes 580
Sparse Core Ops, SparseCore 0:
  336.1 23.0 reduce-scatter.1
  362.9 87.3 all-gather.2
where the time goes:
time: 482 us
  blocking collectives  310 us (64%)
  waiting for transfers between devices  114 us (24%)
  local copies, waits for them, and re-layouts  18.4 us (4%)
  matrix products  15.6 us (3%)
  between operations  14.9 us (3%)
  other arithmetic  8.89 us (2%)
    psum x1, blocking collectives, body(): residual = lax.psum(partial_value, 'leaf').astype(jnp.bfloat16)  310 us
    all_gather x1, waiting for transfers between devices, body(): section_solution = lax.all_gather(own_block[0], 'leaf', axis=0, tiled=True)  90.9 us
    reduce_scatter x1, waiting for transfers between devices, body(): lax.psum_scatter(jnp.einsum('qikc,qkcn->qin', strip_tiles, picked, prefer...  23.2 us
  transfers between devices with their start and end apart: 2, of which 2 were waited for; matrix products, arithmetic and copies ran while one was open for 0% of the time, Pallas kernels for 0%

commit v1 on v0

v1 whole, which is shorter than its diff:
```python
import functools

import jax
import jax.numpy as jnp
from jax import lax
from jax.experimental import pallas as pl
from jax.experimental.pallas import tpu as pltpu
from jax.sharding import Mesh, PartitionSpec as P

TILE = 128
HI_SHIFT = 7
DEAD = 255
MAP_ROWS = 8
F32 = jnp.float32
BF16 = jnp.bfloat16

SMEM = functools.partial(pl.BlockSpec, memory_space=pltpu.SMEM)
VMEM = functools.partial(pl.BlockSpec, memory_space=pltpu.VMEM)


def call(kernel, out_shape, in_specs, scratch=()):
    single = not isinstance(out_shape, (tuple, list))
    return pl.pallas_call(
        kernel,
        out_shape=out_shape,
        in_specs=in_specs,
        out_specs=VMEM() if single else tuple(VMEM() for _ in out_shape),
        scratch_shapes=list(scratch),
    )


def exchange(value, axes):
    return lax.all_to_all(value, axes, split_axis=0, concat_axis=0, tiled=True)


def forward_kernel(cols, rows, count, shots, tiles, own_map, forward, sent, rounded, picked):
    count_rows, per_row = tiles.shape[0], tiles.shape[1]
    peers, _, width = sent.shape
    kmax = picked.shape[0] - MAP_ROWS
    rounded[...] = shots[...].astype(BF16)
    for t in range(count_rows):
        total = None
        for k in range(0, per_row, 2):
            left = jnp.concatenate([tiles[t, k], tiles[t, k + 1]], axis=1)
            starts = [pl.multiple_of(cols[t, k + i] * TILE, TILE) for i in range(2)]
            right = jnp.concatenate([rounded[pl.ds(s, TILE), :] for s in starts], axis=0)
            term = jnp.dot(left, right, preferred_element_type=F32)
            total = term if total is None else total + term
        forward[pl.ds(t * TILE, TILE), :] = total
    live = count[0, 0]
    for k in range(kmax):
        row = forward[pl.ds(rows[0, k], 1), :]
        picked[pl.ds(k, 1), :] = jnp.where(k < live, row, 0.0)
    target = own_map[...]
    lane = lax.broadcasted_iota(jnp.int32, target.shape, 1)
    high = jnp.where(lane < live, target >> HI_SHIFT, DEAD).astype(F32)
    low = (target & (TILE - 1)).astype(F32)
    picked[pl.ds(kmax, MAP_ROWS), :] = jnp.zeros((MAP_ROWS, width), F32)
    picked[pl.ds(kmax, 1), pl.ds(0, kmax)] = high
    picked[pl.ds(kmax + 1, 1), pl.ds(0, kmax)] = low
    whole = picked[...].astype(BF16)
    for p in range(peers):
        sent[p] = whole


def combine_kernel(got, partial, chosen, *, n_y, strip):
    y = lax.axis_index("y")
    peers, held, width = got.shape
    kmax = held - MAP_ROWS
    n_rows = chosen.shape[0]
    r = lax.broadcasted_iota(jnp.int32, (n_rows, kmax), 0)
    row_id = ((r // strip) * n_y + y) * strip + r % strip
    row_id = row_id.astype(F32)
    total = None
    for p in range(peers):
        targets = got[p, pl.ds(kmax, MAP_ROWS), :].astype(F32)[:, :kmax]
        target = targets[0:1] * float(TILE) + targets[1:2]
        hot = jnp.where(row_id == target, 1.0, 0.0).astype(BF16)
        chosen[:, pl.ds(p * kmax, kmax)] = hot
        term = jnp.dot(hot, got[p, pl.ds(0, kmax), :], preferred_element_type=F32)
        total = term if total is None else total + term
    partial[...] = total.reshape(partial.shape)


def residual_kernel(load, got, sent):
    total = got[0]
    for p in range(1, got.shape[0]):
        total = total + got[p]
    value = (load[...] - total).astype(BF16)
    for p in range(sent.shape[0]):
        sent[p] = value


def separator_kernel(cols, strips, residual, product):
    sections, per_row = cols.shape
    for q in range(sections):
        total = None
        for k in range(0, per_row, 2):
            starts = [pl.multiple_of(cols[q, k + i] * TILE, TILE) for i in range(2)]
            right = jnp.concatenate([residual[pl.ds(s, TILE), :] for s in starts], axis=0)
            term = jnp.dot(strips[q, :, pl.ds(k * TILE, 2 * TILE)], right, preferred_element_type=F32)
            total = term if total is None else total + term
        product[q] = total


def solution_kernel(got, own, sent):
    total = got[0]
    for p in range(1, got.shape[0]):
        total = total + got[p]
    own[...] = total
    value = total.astype(BF16)
    for p in range(sent.shape[0]):
        sent[p] = value


def pick_kernel(chosen, strips, sent):
    peers, kmax, width = sent.shape
    picked = lax.dot_general(chosen[...], strips[...], (((0,), (0,)), ((), ())), preferred_element_type=F32)
    sent[...] = picked.astype(BF16).reshape(peers, kmax, width)


def transposed_kernel(cols, rows, got, forward, tiles, out, corrected, needed):
    count_rows, per_row = tiles.shape[0], tiles.shape[1]
    peers, kmax, width = got.shape
    total = got[0].astype(F32)
    for p in range(1, peers):
        total = total + got[p].astype(F32)
    needed[...] = total
    corrected[...] = forward[...]
    for k in range(kmax):
        at = pl.ds(rows[0, k], 1)
        corrected[at, :] = corrected[at, :] - needed[pl.ds(k, 1), :]
    out[...] = jnp.zeros_like(out)
    for t in range(count_rows):
        block = corrected[pl.ds(t * TILE, TILE), :].astype(BF16)
        for k in range(per_row):
            term = lax.dot_general(tiles[t, k], block, (((0,), (0,)), ((), ())), preferred_element_type=F32)
            at = pl.ds(pl.multiple_of(cols[t, k] * TILE, TILE), TILE)
            out[at, :] = out[at, :] + term


def body(
    shot_columns,
    factor_tiles,
    factor_cols,
    boundary_rows,
    boundary_map,
    boundary_count,
    separator_load,
    inverse_tiles,
    inverse_cols,
):
    n_z, n_y = lax.axis_size("z"), lax.axis_size("y")
    n_sep = lax.axis_size("sep")
    shots, tiles, cols = shot_columns[0, 0], factor_tiles[0, 0], factor_cols[0, 0]
    rows, own_map, load = boundary_rows[0], boundary_map[0], separator_load[0]
    leaf_rows, width = shots.shape
    kmax = rows.shape[1]
    strip = load.shape[0]
    shape = jax.ShapeDtypeStruct
    forward, sent = call(
        forward_kernel,
        (shape((leaf_rows, width), F32), shape((n_y, kmax + MAP_ROWS, width), BF16)),
        [SMEM(), SMEM(), SMEM(), VMEM(), VMEM(), VMEM()],
        [pltpu.VMEM((leaf_rows, width), BF16), pltpu.VMEM((kmax + MAP_ROWS, width), F32)],
    )(cols, rows, boundary_count, shots, tiles, own_map)
    got = exchange(sent, "y")
    partial, chosen = call(
        functools.partial(combine_kernel, n_y=n_y, strip=strip),
        (shape((n_z, strip, width), F32), shape((n_z * strip, n_y * kmax), BF16)),
        [VMEM()],
    )(got)
    got = exchange(partial, "z")
    sent = call(residual_kernel, shape((n_z * n_y, strip, width), BF16), [VMEM(), VMEM()])(load, got)
    residual = exchange(sent, ("z", "y")).reshape(-1, width)
    strips = inverse_tiles[:, :, 0].reshape(n_sep, strip, -1)
    product = call(separator_kernel, shape((n_sep, strip, width), F32), [SMEM(), VMEM(), VMEM()])(
        inverse_cols[:, 0, 0], strips, residual
    )
    got = exchange(product, "sep")
    own, sent = call(
        solution_kernel, (shape((strip, width), F32), shape((n_z, strip, width), BF16)), [VMEM()]
    )(got)
    solved = exchange(sent, "z").reshape(-1, width)
    sent = call(pick_kernel, shape((n_y, kmax, width), BF16), [VMEM(), VMEM()])(chosen, solved)
    got = exchange(sent, "y")
    leaf_solution = call(
        transposed_kernel,
        shape((leaf_rows, width), F32),
        [SMEM(), SMEM(), VMEM(), VMEM(), VMEM()],
        [pltpu.VMEM((leaf_rows, width), F32), pltpu.VMEM((kmax, width), F32)],
    )(cols, rows, got, forward, tiles)
    return leaf_solution[None, None], own[None]


def solution(mesh):
    n_leaf, n_sep = mesh.shape["leaf"], mesh.shape["sep"]
    n_y = 8
    torus = Mesh(mesh.devices.reshape(n_leaf // n_y, n_y, n_sep), ("z", "y", "sep"))
    leaf = ("z", "y")
    placed = (
        P(leaf, "sep", None, None),
        P(leaf, "sep", None, None, None, None),
        P(leaf, "sep", None, None),
        P(leaf, "sep", None),
        P(leaf, "sep", None),
        P(leaf, "sep"),
        P("sep", leaf, None),
        P(None, leaf, "sep", None, None),
        P(None, leaf, "sep", None),
    )
    return jax.shard_map(
        body,
        mesh=torus,
        in_specs=placed,
        out_specs=(P(leaf, "sep", None, None), P("sep", leaf, None)),
        check_vma=False,
    )
```

time: 482 us -> 136 us (0.28)
  the two profiles are of different devices: /device:TPU:4 before, /device:TPU:2 now
where the time goes in v1:
time: 136 us; the launch traced here: 135 us
  blocking collectives  79.8 us (59%)
  waiting for transfers between devices  26.9 us (20%)
  Pallas kernels  18.7 us (14%)
  starting transfers between devices  4.79 us (4%)
  local copies, waits for them, and re-layouts  3.81 us (3%)
    all_to_all x5, blocking collectives, exchange(): return lax.all_to_all(value, axes, split_axis=0, concat_axis=0, tiled=True)  79.8 us
    all_to_all x1, waiting for transfers between devices, exchange(): return lax.all_to_all(value, axes, split_axis=0, concat_axis=0, tiled=True)  26.9 us
    all_to_all x1, starting transfers between devices, exchange(): return lax.all_to_all(value, axes, split_axis=0, concat_axis=0, tiled=True)  4.79 us
    pallas_call x1, Pallas kernels, body(): call(transposed_kernel, shape((leaf_rows, width), F32), [SMEM(), SMEM(),...  4.54 us
    pallas_call x1, Pallas kernels, body(): call(forward_kernel, (shape((leaf_rows, width), F32), shape((n_y, kmax +...  3.8 us
  transfers between devices with their start and end apart: 1, of which 1 were waited for; matrix products, arithmetic and copies ran while one was open for 1% of the time, Pallas kernels for 0%

profile of v1, /device:TPU:2, one launch (start us, length us, event | category | flops | bytes accessed | tf_op | source)
XLA Modules:
  0.0 135.3 jit_solution(11193069930242918386)
XLA Ops:
  0.6 1.4 %copy.13.cols = s32[12,4]{1,0:T(8,128)} copy(s32[12,4]{0,1:T(4,128)} %bitcast.20) | data formatting | bytes 384 | tf_op jit(solution)/shard_map/squeeze | solution.py:155
  2.6 3.8 %shard_map.104 = (f32[1536,256]{1,0:T(8,128)}, bf16[8,72,256]{2,1,0:T(8,128)(2,1)}) custom-call(s32[12,4]{1,0:T(8,128)} %copy.13.cols, s32[1,64]{1,0:T(1,128)} %bitcast.18, s32[1,1]{1,0:T(1,128)S(6)} %copy.14.count, f32[1536,256]{1,0:T(8,128)} %bitcast.15, bf16[12,4,128,128]{3,2,1,0:T(8,128)(2,1)} %bitcast.11, s32[1,64]{1,0:T(1,128)} %bitcast.22), custom_call_target="tpu_custom_call" | custom-call | tf_op jit(solution)/shard_map/pallas_call | solution.py:161
  6.4 19.8 %all_to_all.30.got = bf16[8,72,256]{2,1,0:T(8,128)(2,1)} all-to-all(bf16[8,72,256]{2,1,0:T(8,128)(2,1)} %get-tuple-element.8), channel_id=1, replica_groups=mesh['z'=8,'y'=8,'sep'=8] {'y'}, dimensions={0} | all-to-all | bytes 589824 | tf_op jit(solution)/shard_map/all_to_all | solution.py:33
  26.2 2.2 %shard_map.105 = (f32[8,32,256]{2,1,0:T(8,128)}, bf16[256,512]{1,0:T(8,128)(2,1)}) custom-call(bf16[8,72,256]{2,1,0:T(8,128)(2,1)} %all_to_all.30.got), custom_call_target="tpu_custom_call" | custom-call | tf_op jit(solution)/shard_map/pallas_call | solution.py:168
  28.4 20.9 %all_to_all.31.got = f32[8,32,256]{2,1,0:T(8,128)} all-to-all(f32[8,32,256]{2,1,0:T(8,128)} %get-tuple-element.10), channel_id=1, replica_groups=mesh['z'=8,'y'=8,'sep'=8] {'z'}, dimensions={0} | all-to-all | bytes 524288 | tf_op jit(solution)/shard_map/all_to_all | solution.py:33
  49.3 0.0 copy-start.1
  49.3 2.1 %shard_map.106 = bf16[64,32,256]{2,1,0:T(8,128)(2,1)} custom-call(f32[32,256]{1,0:T(8,128)} %bitcast.17, f32[8,32,256]{2,1,0:T(8,128)} %all_to_all.31.got), custom_call_target="tpu_custom_call" | custom-call | tf_op jit(solution)/shard_map/pallas_call | solution.py:174
  51.4 0.0 copy-start.2
  51.4 4.8 %all-to-all-start.2 = ((bf16[64,32,256]{2,1,0:T(8,128)(2,1)}), bf16[64,32,256]{2,1,0:T(8,128)(2,1)S(1)}, u32[]{:S(2)}, u32[]{:S(2)}) async-start(bf16[64,32,256]{2,1,0:T(8,128)(2,1)} %shard_map.106), calls=%async_computation.2 | async-start | bytes 2097152 | tf_op jit(solution)/shard_map/all_to_all | solution.py:33
  56.2 0.0 copy-done.1
  56.2 0.8 reshape_squeeze.3.strips
  57.0 0.0 copy-done.2
  57.0 0.7 copy.12.cols
  57.7 26.9 %all-to-all-done.2 = bf16[64,32,256]{2,1,0:T(8,128)(2,1)S(1)} async-done(((bf16[64,32,256]{2,1,0:T(8,128)(2,1)}), bf16[64,32,256]{2,1,0:T(8,128)(2,1)S(1)}, u32[]{:S(2)}, u32[]{:S(2)}) %all-to-all-start.2) | async-done | bytes 1048608 | tf_op jit(solution)/shard_map/all_to_all | solution.py:33
  84.6 0.0 copy-start
  84.6 1.0 copy-done
  85.5 2.5 %shard_map.107 = f32[8,32,256]{2,1,0:T(8,128)} custom-call(s32[8,4]{1,0:T(8,128)} %copy.12.cols, bf16[8,32,512]{2,1,0:T(8,128)(2,1)} %reshape_squeeze.3.strips, bf16[2048,256]{1,0:T(8,128)(2,1)} %bitcast.13), custom_call_target="tpu_custom_call" | custom-call | tf_op jit(solution)/shard_map/pallas_call | solution.py:177
  88.0 11.0 %all_to_all.32.got = f32[8,32,256]{2,1,0:T(8,128)} all-to-all(f32[8,32,256]{2,1,0:T(8,128)} %shard_map.107), channel_id=1, replica_groups=mesh['z'=8,'y'=8,'sep'=8] {'sep'}, dimensions={0} | all-to-all | bytes 524288 | tf_op jit(solution)/shard_map/all_to_all | solution.py:33
  99.0 1.6 %shard_map.108 = (f32[32,256]{1,0:T(8,128)}, bf16[8,32,256]{2,1,0:T(8,128)(2,1)}) custom-call(f32[8,32,256]{2,1,0:T(8,128)} %all_to_all.32.got), custom_call_target="tpu_custom_call" | custom-call | tf_op jit(solution)/shard_map/pallas_call | solution.py:181
  100.7 13.4 %all_to_all.33 = bf16[8,32,256]{2,1,0:T(8,128)(2,1)} all-to-all(bf16[8,32,256]{2,1,0:T(8,128)(2,1)} %get-tuple-element.11), channel_id=1, replica_groups=mesh['z'=8,'y'=8,'sep'=8] {'z'}, dimensions={0} | all-to-all | bytes 262144 | tf_op jit(solution)/shard_map/all_to_all | solution.py:33
  114.1 2.0 %shard_map.109 = bf16[8,64,256]{2,1,0:T(8,128)(2,1)} custom-call(bf16[256,512]{1,0:T(8,128)(2,1)} %get-tuple-element.9.chosen, bf16[256,256]{1,0:T(8,128)(2,1)} %bitcast.16), custom_call_target="tpu_custom_call" | custom-call | tf_op jit(solution)/shard_map/pallas_call | solution.py:185
  116.0 14.7 %all_to_all.34.got = bf16[8,64,256]{2,1,0:T(8,128)(2,1)} all-to-all(bf16[8,64,256]{2,1,0:T(8,128)(2,1)} %shard_map.109), channel_id=1, replica_groups=mesh['z'=8,'y'=8,'sep'=8] {'y'}, dimensions={0} | all-to-all | bytes 524288 | tf_op jit(solution)/shard_map/all_to_all | solution.py:33
  130.8 4.5 %shard_map.110 = f32[1536,256]{1,0:T(8,128)} custom-call(s32[12,4]{1,0:T(8,128)} %copy.13.cols, s32[1,64]{1,0:T(1,128)} %bitcast.19, bf16[8,64,256]{2,1,0:T(8,128)(2,1)} %all_to_all.34.got, f32[1536,256]{1,0:T(8,128)} %get-tuple-element.12.forward, bf16[12,4,128,128]{3,2,1,0:T(8,128)(2,1)} %bitcast.12), custom_call_target="tpu_custom_call" | custom-call | tf_op jit(solution)/shard_map/pallas_call | solution.py:187
Async XLA Ops:
  49.3 6.9 %copy-start.1 = (bf16[8,32,1,4,128]{4,3,2,1,0:T(4,128)(2,1)S(1)}, bf16[8,32,1,4,128]{4,3,2,1,0:T(4,128)(2,1)}, u32[]{:S(2)}) copy-start(bf16[8,32,1,4,128]{4,3,2,1,0:T(4,128)(2,1)} %param.16) | copy-start | bytes 786436
  51.4 5.6 %copy-start.2 = (s32[8,1,1,4]{0,3,2,1:T(4,128)S(1)}, s32[8,1,1,4]{0,3,2,1:T(4,128)}, u32[]{:S(2)}) copy-start(s32[8,1,1,4]{0,3,2,1:T(4,128)} %param.17) | copy-start | bytes 388
  51.4 33.2 %all-to-all-start.2 = ((bf16[64,32,256]{2,1,0:T(8,128)(2,1)}), bf16[64,32,256]{2,1,0:T(8,128)(2,1)S(1)}, u32[]{:S(2)}, u32[]{:S(2)}) async-start(bf16[64,32,256]{2,1,0:T(8,128)(2,1)} %shard_map.106), calls=%async_computation.2 | async-start | bytes 2097152 | tf_op jit(solution)/shard_map/all_to_all | solution.py:33
  84.6 1.0 copy-start

commit v2 on v1

v2 whole, which is shorter than its diff:
```python
import functools

import jax
import jax.numpy as jnp
from jax import lax
from jax.experimental import pallas as pl
from jax.experimental.pallas import tpu as pltpu
from jax.sharding import Mesh, PartitionSpec as P

TILE = 128
SHIFT = 7
DEAD = 255
SLOTS = 8
EXTRA = 8
F32 = jnp.float32
BF16 = jnp.bfloat16

SMEM = functools.partial(pl.BlockSpec, memory_space=pltpu.SMEM)
VMEM = functools.partial(pl.BlockSpec, memory_space=pltpu.VMEM)


def near(value):
    return pltpu.with_memory_space_constraint(value, pltpu.VMEM)


def call(kernel, out_shape, in_specs, scratch=(), out_specs=None):
    single = not isinstance(out_shape, (tuple, list))
    if out_specs is None:
        out_specs = VMEM() if single else tuple(VMEM() for _ in out_shape)
    return pl.pallas_call(
        kernel,
        out_shape=out_shape,
        in_specs=in_specs,
        out_specs=out_specs,
        scratch_shapes=list(scratch),
    )


def exchange(value, axes):
    return lax.all_to_all(value, axes, split_axis=0, concat_axis=0, tiled=True)


def over_rows(left, right):
    return lax.dot_general(left, right, (((0,), (0,)), ((), ())), preferred_element_type=F32)


def over_lanes(left, right):
    return lax.dot_general(left, right, (((1,), (1,)), ((), ())), preferred_element_type=F32)


def forward_kernel(
    cols, rows, targets, count, shots, tiles, own_map,
    forward, sent, taken, slots,
    rounded, exact, picked, filled, *, strip,
):
    count_rows, per_row = tiles.shape[0], tiles.shape[1]
    peers, _, width = sent.shape
    kmax = taken.shape[0]
    rounded[...] = shots[...].astype(BF16)
    for t in range(count_rows):
        total = None
        for k in range(0, per_row, 2):
            left = jnp.concatenate([tiles[t, k], tiles[t, k + 1]], axis=1)
            starts = [pl.multiple_of(cols[k + i, t] * TILE, TILE) for i in range(2)]
            right = jnp.concatenate([rounded[pl.ds(s, TILE), :] for s in starts], axis=0)
            term = jnp.dot(left, right, preferred_element_type=F32)
            total = term if total is None else total + term
        exact[pl.ds(t * TILE, TILE), :] = total
        forward[pl.ds(t * TILE, TILE), :] = total.astype(BF16)
    live = count[0, 0]
    for s in range(filled.shape[0]):
        filled[s] = 0
    lane = lax.broadcasted_iota(jnp.int32, own_map.shape, 1)
    place = jnp.zeros(own_map.shape, jnp.int32)
    most = 0
    for k in range(kmax):
        row = exact[pl.ds(rows[0, k], 1), :]
        taken[pl.ds(k, 1), :] = row
        picked[pl.ds(k, 1), :] = jnp.where(k < live, row, 0.0)
        owner = targets[0, k] // strip
        slot = filled[owner]
        alive = (k < live).astype(jnp.int32)
        filled[owner] = slot + alive
        most = jnp.maximum(most, alive * (slot + 1))
        place = jnp.where(lane == k, slot, place)
        slots[0, k] = jnp.where(k < live, owner * SLOTS + jnp.minimum(slot, SLOTS - 1), -1)
    target = own_map[...]
    high = jnp.where(lane < live, target >> SHIFT, DEAD).astype(F32)
    low = (target & (TILE - 1)).astype(F32)
    picked[pl.ds(kmax, EXTRA), :] = jnp.zeros((EXTRA, width), F32)
    picked[pl.ds(kmax, 1), pl.ds(0, kmax)] = high
    picked[pl.ds(kmax + 1, 1), pl.ds(0, kmax)] = low
    picked[pl.ds(kmax + 2, 1), pl.ds(0, kmax)] = place.astype(F32)
    over = jnp.where(most > SLOTS, 1.0, 0.0)
    picked[pl.ds(kmax + 3, 1), :] = jnp.full((1, width), over, F32)
    whole = picked[...].astype(BF16)
    for p in range(peers):
        sent[p] = whole


def ring_targets(got, n_rows, n_y, strip):
    y = lax.axis_index("y")
    kmax = got.shape[1] - EXTRA
    r = lax.broadcasted_iota(jnp.int32, (n_rows, kmax), 0)
    row_id = ((r // strip) * n_y + y) * strip + r % strip
    row_id = row_id.astype(F32)
    for p in range(got.shape[0]):
        info = got[p, pl.ds(kmax, EXTRA), :].astype(F32)
        target = info[0:1, :kmax] * float(TILE) + info[1:2, :kmax]
        yield p, info, jnp.where(row_id == target, 1.0, 0.0).astype(BF16)


def combine_kernel(got, sent, *, n_y, strip):
    peers, _, width = got.shape
    n_z = sent.shape[0]
    kmax = got.shape[1] - EXTRA
    total, wanted, over = None, [], None
    for p, info, hot in ring_targets(got, n_z * strip, n_y, strip):
        term = jnp.dot(hot, got[p, pl.ds(0, kmax), :], preferred_element_type=F32)
        total = term if total is None else total + term
        slot = lax.broadcasted_iota(jnp.int32, (TILE, kmax), 0)
        place = info[2:3, :kmax].astype(jnp.int32)
        mine = jnp.where(slot == place + p * SLOTS, 1.0, 0.0)
        mine = jnp.where(place < SLOTS, mine, 0.0).astype(BF16)
        wanted.append(over_lanes(hot, mine))
        flag = info[3:4, :TILE]
        over = flag if over is None else jnp.maximum(over, flag)
    asked = wanted[0]
    for w in wanted[1:]:
        asked = asked + w
    lane = lax.broadcasted_iota(jnp.int32, asked.shape, 1)
    asked = jnp.where(lane < peers * SLOTS, asked, jnp.broadcast_to(over, asked.shape))
    sent[:, :, pl.ds(0, width)] = total.astype(BF16).reshape(n_z, strip, width)
    sent[:, :, pl.ds(width, TILE)] = asked.astype(BF16).reshape(n_z, strip, TILE)


def residual_kernel(load, got, sent):
    width = load.shape[1]
    total = got[0, :, pl.ds(0, width)].astype(F32)
    for p in range(1, got.shape[0]):
        total = total + got[p, :, pl.ds(0, width)].astype(F32)
    value = (load[...] - total).astype(BF16)
    for p in range(sent.shape[0]):
        sent[p] = value


def separator_kernel(cols, strips, residual, got, product):
    per_row, sections = cols.shape
    _, strip, width = residual.shape
    per_tile = TILE // strip
    for q in range(sections):
        total = None
        for k in range(0, per_row, 2):
            right = jnp.concatenate(
                [
                    residual[pl.ds(cols[k + i, q] * per_tile, per_tile)].reshape(TILE, width)
                    for i in range(2)
                ],
                axis=0,
            )
            term = jnp.dot(strips[q, :, pl.ds(k * TILE, 2 * TILE)], right, preferred_element_type=F32)
            total = term if total is None else total + term
        product[q, pl.ds(0, strip), :] = total
    over = got[0, pl.ds(0, EXTRA), pl.ds(width, TILE)].astype(F32)
    for p in range(1, got.shape[0]):
        over = jnp.maximum(over, got[p, pl.ds(0, EXTRA), pl.ds(width, TILE)].astype(F32))
    over = jnp.concatenate([over] * (width // TILE), axis=1)
    for q in range(sections):
        product[q, pl.ds(strip, EXTRA), :] = over


def solution_kernel(got, asked, own, sent, over):
    strip, width = own.shape
    total = got[0]
    for p in range(1, got.shape[0]):
        total = total + got[p]
    own[...] = total[:strip]
    most = got[0, pl.ds(strip, EXTRA), pl.ds(0, TILE)]
    for p in range(1, got.shape[0]):
        most = jnp.maximum(most, got[p, pl.ds(strip, EXTRA), pl.ds(0, TILE)])
    over[...] = most
    value = total[:strip].astype(BF16)
    n_z = asked.shape[0]
    per = sent.shape[0] // n_z
    for p in range(n_z):
        rows = over_rows(asked[p, :, pl.ds(width, TILE)], value)[: per * SLOTS]
        sent[pl.ds(p * per, per)] = rows.astype(BF16).reshape(per, SLOTS, width)


def pick_kernel(got, strips, sent, *, n_y, strip):
    n_rows = strips.shape[0]
    for p, _, hot in ring_targets(got, n_rows, n_y, strip):
        sent[p] = over_rows(hot, strips[...]).astype(BF16)


def transposed_kernel(cols, count, forward, tiles, row_lanes, base, reach, same, wide):
    count_rows, per_row = tiles.shape[0], tiles.shape[1]
    leaf_rows, width = forward.shape
    kmax = same.shape[0]
    wide[...] = jnp.zeros_like(wide)
    lanes = row_lanes[...]
    sums = None
    for t in range(count_rows):
        r = lax.broadcasted_iota(jnp.int32, (TILE, TILE), 0) + t * TILE
        hot = jnp.where(r == lanes, 1.0, 0.0).astype(BF16)
        term = over_rows(hot, hot)
        sums = term if sums is None else sums + term
        block = jnp.concatenate([forward[pl.ds(t * TILE, TILE), :], hot], axis=1)
        for k in range(per_row):
            at = pl.ds(pl.multiple_of(cols[k, t] * TILE, TILE), TILE)
            wide[at, :] = wide[at, :] + over_rows(tiles[t, k], block)
    base[...] = wide[:, pl.ds(0, width)]
    reach[...] = wide[:, pl.ds(width, TILE)].astype(BF16)
    same[...] = sums[:kmax]


def finish(needed, count, taken, same, base, reach, out, change):
    @pl.when(pl.program_id(0) == 0)
    def _():
        kmax = taken.shape[0]
        equal = same[...][:, :kmax]
        k = lax.broadcasted_iota(jnp.int32, equal.shape, 1)
        mine = lax.broadcasted_iota(jnp.int32, equal.shape, 0)
        earlier = jnp.sum(jnp.where(k < mine, equal, 0.0), axis=1, keepdims=True)
        live = jnp.where(k < count[0, 0], equal, 0.0).astype(BF16)
        term = jnp.dot(live, needed().astype(BF16), preferred_element_type=F32)
        before = taken[...]
        delta = (before - term).astype(BF16).astype(F32) - before.astype(BF16).astype(F32)
        delta = jnp.where(earlier == 0.0, delta, 0.0)
        high = delta.astype(BF16)
        change[pl.ds(0, kmax), :] = high
        change[pl.ds(kmax, kmax), :] = (delta - high.astype(F32)).astype(BF16)

    out[...] = base[...] + jnp.dot(reach[...], change[...], preferred_element_type=F32)


def slot_finish_kernel(slots, count, got, taken, same, base, reach, out, change, plain, rows):
    kmax = taken.shape[0]

    def needed():
        plain[...] = got[...].reshape(plain.shape).astype(F32)
        for k in range(kmax):
            at = slots[0, k]
            row = plain[pl.ds(jnp.maximum(at, 0), 1), :]
            rows[pl.ds(k, 1), :] = jnp.where(at >= 0, row, 0.0)
        return rows[...]

    finish(needed, count, taken, same, base, reach, out, change)


def ring_finish_kernel(count, got, taken, same, base, reach, out, change):
    def needed():
        total = got[0].astype(F32)
        for p in range(1, got.shape[0]):
            total = total + got[p].astype(F32)
        return total

    finish(needed, count, taken, same, base, reach, out, change)


def body(
    shot_columns,
    factor_tiles,
    factor_cols,
    boundary_rows,
    boundary_map,
    boundary_count,
    separator_load,
    inverse_tiles,
    inverse_cols,
):
    n_z, n_y = lax.axis_size("z"), lax.axis_size("y")
    n_sep, n_leaf = lax.axis_size("sep"), n_z * n_y
    shots, tiles, cols = shot_columns[0, 0], factor_tiles[0, 0], factor_cols[0, 0].T
    rows, own_map, load = boundary_rows[0], boundary_map[0], separator_load[0]
    leaf_rows, width = shots.shape
    kmax = rows.shape[1]
    strip = load.shape[0]
    shape = jax.ShapeDtypeStruct
    forward, sent, taken, slots = call(
        functools.partial(forward_kernel, strip=strip),
        (
            shape((leaf_rows, width), BF16),
            shape((n_y, kmax + EXTRA, width), BF16),
            shape((kmax, width), F32),
            shape((1, kmax), jnp.int32),
        ),
        [SMEM(), SMEM(), SMEM(), SMEM(), VMEM(), VMEM(), VMEM()],
        [
            pltpu.VMEM((leaf_rows, width), BF16),
            pltpu.VMEM((leaf_rows, width), F32),
            pltpu.VMEM((kmax + EXTRA, width), F32),
            pltpu.SMEM((n_leaf,), jnp.int32),
        ],
        (VMEM(), VMEM(), VMEM(), SMEM()),
    )(cols, rows, own_map, boundary_count, shots, tiles, own_map)
    ring = exchange(sent, "y")
    sent = call(
        functools.partial(combine_kernel, n_y=n_y, strip=strip),
        shape((n_z, strip, width + TILE), BF16),
        [VMEM()],
    )(near(ring))
    asked = exchange(sent, "z")
    sent = call(residual_kernel, shape((n_leaf, strip, width), BF16), [VMEM(), VMEM()])(load, near(asked))
    residual = exchange(sent, ("z", "y"))
    held_rows, _ = lax.optimization_barrier((rows, asked[0, 0, 0]))
    base, reach, same = call(
        transposed_kernel,
        (shape((leaf_rows, width), F32), shape((leaf_rows, TILE), BF16), shape((kmax, TILE), F32)),
        [SMEM(), SMEM(), VMEM(), VMEM(), VMEM()],
        [pltpu.VMEM((leaf_rows, width + TILE), F32)],
    )(cols, boundary_count, forward, tiles, jnp.concatenate([held_rows, held_rows], axis=1))
    strips = inverse_tiles[:, :, 0].reshape(n_sep, strip, -1)
    product = call(
        separator_kernel,
        shape((n_sep, strip + EXTRA, width), F32),
        [SMEM(), VMEM(), VMEM(), VMEM()],
    )(inverse_cols[:, 0, 0].T, near(strips), near(residual), near(asked))
    got = exchange(product, "sep")
    own, sent, over = call(
        solution_kernel,
        (shape((strip, width), F32), shape((n_leaf, SLOTS, width), BF16), shape((EXTRA, TILE), F32)),
        [VMEM(), VMEM()],
    )(near(got), near(asked))

    pieces = 4
    part = leaf_rows // pieces
    whole = lambda *dims: pl.BlockSpec(dims, lambda i: (0,) * len(dims))
    tail = [
        whole(kmax, width),
        whole(kmax, TILE),
        pl.BlockSpec((part, width), lambda i: (i, 0)),
        pl.BlockSpec((part, TILE), lambda i: (i, 0)),
    ]

    def finished(kernel, lead, scratch):
        return pl.pallas_call(
            kernel,
            grid=(pieces,),
            out_shape=shape((leaf_rows, width), F32),
            in_specs=lead + tail,
            out_specs=pl.BlockSpec((part, width), lambda i: (i, 0)),
            scratch_shapes=[pltpu.VMEM((2 * kmax, width), BF16)] + scratch,
        )

    def by_slots():
        got = exchange(sent, ("z", "y"))
        return finished(
            slot_finish_kernel,
            [SMEM(), SMEM(), whole(n_leaf, SLOTS, width)],
            [pltpu.VMEM((n_leaf * SLOTS, width), F32), pltpu.VMEM((kmax, width), F32)],
        )(slots, boundary_count, got, taken, same, base, reach)

    def by_rings():
        value = jnp.broadcast_to(own.astype(BF16)[None], (n_z, strip, width))
        solved = exchange(value, "z").reshape(-1, width)
        picked = call(
            functools.partial(pick_kernel, n_y=n_y, strip=strip),
            shape((n_y, kmax, width), BF16),
            [VMEM(), VMEM()],
        )(ring, solved)
        got = exchange(picked, "y")
        return finished(ring_finish_kernel, [SMEM(), whole(n_y, kmax, width)], [])(
            boundary_count, got, taken, same, base, reach
        )

    leaf_solution = lax.cond(jnp.max(over) > 0.0, by_rings, by_slots)
    return leaf_solution[None, None], own[None]


def solution(mesh):
    n_leaf, n_sep = mesh.shape["leaf"], mesh.shape["sep"]
    n_y = 8
    torus = Mesh(mesh.devices.reshape(n_leaf // n_y, n_y, n_sep), ("z", "y", "sep"))
    leaf = ("z", "y")
    placed = (
        P(leaf, "sep", None, None),
        P(leaf, "sep", None, None, None, None),
        P(leaf, "sep", None, None),
        P(leaf, "sep", None),
        P(leaf, "sep", None),
        P(leaf, "sep"),
        P("sep", leaf, None),
        P(None, leaf, "sep", None, None),
        P(None, leaf, "sep", None),
    )
    return jax.shard_map(
        body,
        mesh=torus,
        in_specs=placed,
        out_specs=(P(leaf, "sep", None, None), P("sep", leaf, None)),
        check_vma=False,
    )
```

time: 136 us -> 131 us (0.963)
  blocking collectives: 79.8 us -> 67.4 us
  starting transfers between devices: 4.79 us -> 9.48 us
  local copies, waits for them, and re-layouts: 3.81 us -> 0.13 us
  waiting for transfers between devices: 26.9 us -> 30.2 us
  other arithmetic: 0 us -> 1.92 us
    all_to_all x5 -> x4, blocking collectives: 79.8 us -> 67.4 us  [exchange(): return lax.all_to_all(value, axes, split_axis=0, concat_axis=0, tiled=True)]
    all_to_all x1 -> x2, starting transfers between devices: 4.79 us -> 9.48 us  [exchange(): return lax.all_to_all(value, axes, split_axis=0, concat_axis=0, tiled=True)]
    all_to_all x1 -> x2, waiting for transfers between devices: 26.9 us -> 30.2 us  [exchange(): return lax.all_to_all(value, axes, split_axis=0, concat_axis=0, tiled=True)]
    squeeze x2 -> x0, local copies, waits for them, and re-layouts: 2.03 us -> none  [the longest x1 1.36 us: body(): factor_cols[0, 0]]
    pallas_call x7 -> x8, Pallas kernels: 18.7 us -> 18.9 us  [the longest x1 3.88 us: by_rings(): finished(ring_finish_kernel, [SMEM(), whole(n_y, kmax, width)], [])]
  transfers between devices with their start and end apart: 1 -> 2, of which waited for: 1 -> 2; matrix products, arithmetic and copies ran while one was open for 1% -> 1% of each run, Pallas kernels for 0% -> 3%
where the time goes in v2:
time: 131 us; the launch traced here: 130 us
  blocking collectives  67.4 us (51%)
  waiting for transfers between devices  30.2 us (23%)
  Pallas kernels  18.9 us (14%)
  starting transfers between devices  9.48 us (7%)
  between operations  1.98 us (2%)
  other arithmetic  1.92 us (1%)
    all_to_all x4, blocking collectives, exchange(): return lax.all_to_all(value, axes, split_axis=0, concat_axis=0, tiled=True)  67.4 us
    all_to_all x2, waiting for transfers between devices, exchange(): return lax.all_to_all(value, axes, split_axis=0, concat_axis=0, tiled=True)  30.2 us
    all_to_all x2, starting transfers between devices, exchange(): return lax.all_to_all(value, axes, split_axis=0, concat_axis=0, tiled=True)  9.48 us
    pallas_call x1, Pallas kernels, by_rings(): finished(ring_finish_kernel, [SMEM(), whole(n_y, kmax, width)], [])  3.88 us
    pallas_call x1, Pallas kernels, body(): call(functools.partial(forward_kernel, strip=strip), (shape((leaf_rows, w...  3.74 us
    pallas_call x1, Pallas kernels, body(): call(transposed_kernel, (shape((leaf_rows, width), F32), shape((leaf_rows...  3.41 us
  transfers between devices with their start and end apart: 2, of which 2 were waited for; matrix products, arithmetic and copies ran while one was open for 1% of the time, Pallas kernels for 3%

profile of v2, /device:TPU:2, one launch (start us, length us, event | category | flops | bytes accessed | tf_op | source)
XLA Modules:
  0.0 130.0 jit_solution(9595969408863855387)
XLA Ops:
  1.3 3.7 %shard_map.104 = (bf16[1536,256]{1,0:T(8,128)(2,1)}, bf16[8,72,256]{2,1,0:T(8,128)(2,1)}, f32[64,256]{1,0:T(8,128)S(1)}, s32[1,64]{1,0:T(1,128)S(1)}) custom-call(s32[4,12]{1,0:T(4,128)} %bitcast.23, s32[1,64]{1,0:T(1,128)} %bitcast.28, s32[1,64]{1,0:T(1,128)} %bitcast.25, s32[1,1]{1,0:T(1,128)S(6)} %copy.13.count, f32[1536,256]{1,0:T(8,128)} %bitcast.17, ...), custom_call_target="tpu_custom_call" | custom-call | tf_op jit(solution)/shard_map/pallas_call | solution.py:280
  5.0 19.7 %all_to_all.35.got = bf16[8,72,256]{2,1,0:T(8,128)(2,1)S(1)} all-to-all(bf16[8,72,256]{2,1,0:T(8,128)(2,1)} %get-tuple-element.58), channel_id=1, replica_groups=mesh['z'=8,'y'=8,'sep'=8] {'y'}, dimensions={0} | all-to-all | bytes 589824 | tf_op jit(solution)/shard_map/all_to_all | solution.py:40
  24.7 1.2 shard_map.105
  26.0 20.1 %all_to_all.36.got.asked = bf16[8,32,384]{2,1,0:T(8,128)(2,1)S(1)} all-to-all(bf16[8,32,384]{2,1,0:T(8,128)(2,1)} %shard_map.105), channel_id=1, replica_groups=mesh['z'=8,'y'=8,'sep'=8] {'z'}, dimensions={0} | all-to-all | bytes 393216 | tf_op jit(solution)/shard_map/all_to_all | solution.py:40
  46.1 1.9 %shard_map.106 = bf16[64,32,256]{2,1,0:T(8,128)(2,1)} custom-call(f32[32,256]{1,0:T(8,128)} %bitcast.21, bf16[8,32,384]{2,1,0:T(8,128)(2,1)S(1)} %all_to_all.36.got.asked), custom_call_target="tpu_custom_call" | custom-call | tf_op jit(solution)/shard_map/pallas_call | solution.py:304
  48.0 4.7 %all-to-all-start.5 = ((bf16[64,32,256]{2,1,0:T(8,128)(2,1)}), bf16[64,32,256]{2,1,0:T(8,128)(2,1)S(1)}, u32[]{:S(2)}, u32[]{:S(2)}) async-start(bf16[64,32,256]{2,1,0:T(8,128)(2,1)} %shard_map.106), calls=%async_computation.5 | async-start | bytes 2097152 | tf_op jit(solution)/shard_map/all_to_all | solution.py:40
  52.6 0.0 copy-done
  52.6 0.0 copy-start.2
  52.6 0.1 reshape_squeeze.3.strips
  52.8 27.5 %all-to-all-done.5.residual = bf16[64,32,256]{2,1,0:T(8,128)(2,1)S(1)} async-done(((bf16[64,32,256]{2,1,0:T(8,128)(2,1)}), bf16[64,32,256]{2,1,0:T(8,128)(2,1)S(1)}, u32[]{:S(2)}, u32[]{:S(2)}) %all-to-all-start.5) | async-done | bytes 1048608 | tf_op jit(solution)/shard_map/all_to_all | solution.py:40
  80.2 1.9 %shard_map.107 = f32[8,40,256]{2,1,0:T(8,128)} custom-call(s32[4,8]{1,0:T(4,128)} %bitcast.27, bf16[8,32,512]{2,1,0:T(8,128)(2,1)S(1)} %reshape_squeeze.3.strips, bf16[64,32,256]{2,1,0:T(8,128)(2,1)S(1)} %all-to-all-done.5.residual, bf16[8,32,384]{2,1,0:T(8,128)(2,1)S(1)} %all_to_all.36.got.asked), custom_call_target="tpu_custom_call" | custom-call | tf_op jit(solution)/shard_map/pallas_call | solution.py:314
  82.1 4.8 %all-to-all-start.6 = ((f32[8,40,256]{2,1,0:T(8,128)}), f32[8,40,256]{2,1,0:T(8,128)S(1)}, u32[]{:S(2)}, u32[]{:S(2)}) async-start(f32[8,40,256]{2,1,0:T(8,128)} %shard_map.107), calls=%async_computation.6 | async-start | bytes 655360 | tf_op jit(solution)/shard_map/all_to_all | solution.py:40
  86.9 0.0 copy-done.2
  86.9 0.6 pad_add_fusion.row_lanes
  87.5 3.4 %shard_map.109 = (f32[1536,256]{1,0:T(8,128)S(1)}, bf16[1536,128]{1,0:T(8,128)(2,1)S(1)}, f32[64,128]{1,0:T(8,128)S(1)}) custom-call(s32[4,12]{1,0:T(4,128)} %bitcast.24, s32[1,1]{1,0:T(1,128)S(6)} %copy.13.count, bf16[1536,256]{1,0:T(8,128)(2,1)} %get-tuple-element.63.forward, bf16[12,4,128,128]{3,2,1,0:T(8,128)(2,1)} %bitcast.16, ...), custom_call_target="tpu_custom_call" | custom-call | tf_op jit(solution)/shard_map/pallas_call | solution.py:307
  90.9 2.7 %all-to-all-done.6.got = f32[8,40,256]{2,1,0:T(8,128)S(1)} async-done(((f32[8,40,256]{2,1,0:T(8,128)}), f32[8,40,256]{2,1,0:T(8,128)S(1)}, u32[]{:S(2)}, u32[]{:S(2)}) %all-to-all-start.6) | async-done | bytes 327712 | tf_op jit(solution)/shard_map/all_to_all | solution.py:40
  93.7 0.8 shard_map.108
  94.5 1.3 %reduce_max.9 = f32[]{:T(128)} reduce(f32[8,128]{1,0:T(8,128)} %get-tuple-element.59, f32[]{:T(128)} %constant.0.clone.1), dimensions={0,1}, to_apply=%region_0.0 | reduce | flops 1023 | bytes 4104 | tf_op jit(solution)/shard_map/reduce_max | solution.py:367
  96.5 0.0 copy-done.1
  96.5 33.6 %conditional.1 = (f32[1,1,1536,256]{3,2,1,0:T(8,128)}) conditional(s32[]{:T(128)} %convert_element_type.6, (bf16[64,8,256]{2,1,0:T(8,128)(2,1)S(1)}, s32[1,64]{1,0:T(1,128)S(1)}, s32[1,1]{1,0:T(1,128)}, f32[64,256]{1,0:T(8,128)S(1)}, f32[64,128]{1,0:T(8,128)S(1)}, /*index=5*/f32[1536,256]{1,0:T(8,128)S(1)}, ...), branch_computations={%region_1.0_spmd, %region_2.0_spmd} | conditional | flops 8192 | bytes 983048 | solution.py:367
  96.5 13.1 %all_to_all.33 = bf16[8,32,256]{2,1,0:T(8,128)(2,1)} all-to-all(bf16[8,32,256]{2,1,0:T(8,128)(2,1)S(1)} %broadcast_in_dim.13), channel_id=1, replica_groups=mesh['z'=8,'y'=8,'sep'=8] {'z'}, dimensions={0} | all-to-all | bytes 262144 | tf_op jit(solution)/shard_map/cond/branch_1_fun/all_to_all | solution.py:40
  109.6 2.0 %branch_1_fun.2 = bf16[8,64,256]{2,1,0:T(8,128)(2,1)} custom-call(bf16[8,72,256]{2,1,0:T(8,128)(2,1)S(1)} %get-tuple-element.40.got, bf16[256,256]{1,0:T(8,128)(2,1)} %bitcast.20), custom_call_target="tpu_custom_call" | custom-call | tf_op jit(solution)/shard_map/cond/branch_1_fun/pallas_call | solution.py:357
  111.6 14.5 %all_to_all.34.got = bf16[8,64,256]{2,1,0:T(8,128)(2,1)} all-to-all(bf16[8,64,256]{2,1,0:T(8,128)(2,1)} %branch_1_fun.2), channel_id=1, replica_groups=mesh['z'=8,'y'=8,'sep'=8] {'y'}, dimensions={0} | all-to-all | bytes 524288 | tf_op jit(solution)/shard_map/cond/branch_1_fun/all_to_all | solution.py:40
  126.1 3.9 %branch_1_fun.3 = f32[1536,256]{1,0:T(8,128)} custom-call(s32[1,1]{1,0:T(1,128)} %get-tuple-element.39.count, bf16[8,64,256]{2,1,0:T(8,128)(2,1)} %all_to_all.34.got, f32[64,256]{1,0:T(8,128)S(1)} %get-tuple-element.42.taken, f32[64,128]{1,0:T(8,128)S(1)} %get-tuple-element.43.same, f32[1536,256]{1,0:T(8,128)S(1)} %get-tuple-element.44.base, ...), custom_call_target="tpu_custom_call" | custom-call | tf_op jit(solution)/shard_map/cond/branch_1_fun/pallas_call | solution.py:363
  (4 shorter events, 0.0 us)
Async XLA Ops:
  46.0 6.6 %copy-start = (bf16[8,32,1,4,128]{4,3,2,1,0:T(4,128)(2,1)S(1)}, bf16[8,32,1,4,128]{4,3,2,1,0:T(4,128)(2,1)}, u32[]{:S(2)}) copy-start(bf16[8,32,1,4,128]{4,3,2,1,0:T(4,128)(2,1)} %param.18) | copy-start | bytes 786436
  48.0 32.2 %all-to-all-start.5 = ((bf16[64,32,256]{2,1,0:T(8,128)(2,1)}), bf16[64,32,256]{2,1,0:T(8,128)(2,1)S(1)}, u32[]{:S(2)}, u32[]{:S(2)}) async-start(bf16[64,32,256]{2,1,0:T(8,128)(2,1)} %shard_map.106), calls=%async_computation.5 | async-start | bytes 2097152 | tf_op jit(solution)/shard_map/all_to_all | solution.py:40
  52.6 34.3 %copy-start.2 = (s32[1,1,64]{2,1,0:T(1,128)S(1)}, s32[1,1,64]{2,1,0:T(1,128)}, u32[]{:S(2)}) copy-start(s32[1,1,64]{2,1,0:T(1,128)} %param.14) | copy-start | bytes 772
  82.1 11.6 %all-to-all-start.6 = ((f32[8,40,256]{2,1,0:T(8,128)}), f32[8,40,256]{2,1,0:T(8,128)S(1)}, u32[]{:S(2)}, u32[]{:S(2)}) async-start(f32[8,40,256]{2,1,0:T(8,128)} %shard_map.107), calls=%async_computation.6 | async-start | bytes 655360 | tf_op jit(solution)/shard_map/all_to_all | solution.py:40
  94.5 2.0 %copy-start.1 = (f32[32,256]{1,0:T(8,128)}, f32[32,256]{1,0:T(8,128)S(1)}, u32[]{:S(2)}) copy-start(f32[32,256]{1,0:T(8,128)S(1)} %get-tuple-element.67) | copy-start | bytes 98308

commit v3 on v2

--- a/solution.py
+++ b/solution.py
@@ -178,7 +178,8 @@
     most = got[0, pl.ds(strip, EXTRA), pl.ds(0, TILE)]
     for p in range(1, got.shape[0]):
         most = jnp.maximum(most, got[p, pl.ds(strip, EXTRA), pl.ds(0, TILE)])
-    over[...] = most
+    lane = lax.broadcasted_iota(jnp.int32, most.shape, 1)
+    over[0, 0] = (jnp.max(jnp.where(lane == TILE - 1, most, 0.0)) > 0.0).astype(jnp.int32)
     value = total[:strip].astype(BF16)
     n_z = asked.shape[0]
     per = sent.shape[0] // n_z
@@ -215,22 +216,19 @@
 
 
 def finish(needed, count, taken, same, base, reach, out, change):
-    @pl.when(pl.program_id(0) == 0)
-    def _():
-        kmax = taken.shape[0]
-        equal = same[...][:, :kmax]
-        k = lax.broadcasted_iota(jnp.int32, equal.shape, 1)
-        mine = lax.broadcasted_iota(jnp.int32, equal.shape, 0)
-        earlier = jnp.sum(jnp.where(k < mine, equal, 0.0), axis=1, keepdims=True)
-        live = jnp.where(k < count[0, 0], equal, 0.0).astype(BF16)
-        term = jnp.dot(live, needed().astype(BF16), preferred_element_type=F32)
-        before = taken[...]
-        delta = (before - term).astype(BF16).astype(F32) - before.astype(BF16).astype(F32)
-        delta = jnp.where(earlier == 0.0, delta, 0.0)
-        high = delta.astype(BF16)
-        change[pl.ds(0, kmax), :] = high
-        change[pl.ds(kmax, kmax), :] = (delta - high.astype(F32)).astype(BF16)
-
+    kmax = taken.shape[0]
+    equal = same[...][:, :kmax]
+    k = lax.broadcasted_iota(jnp.int32, equal.shape, 1)
+    mine = lax.broadcasted_iota(jnp.int32, equal.shape, 0)
+    earlier = jnp.sum(jnp.where(k < mine, equal, 0.0), axis=1, keepdims=True)
+    live = jnp.where(k < count[0, 0], equal, 0.0).astype(BF16)
+    term = jnp.dot(live, needed().astype(BF16), preferred_element_type=F32)
+    before = taken[...]
+    delta = (before - term).astype(BF16).astype(F32) - before.astype(BF16).astype(F32)
+    delta = jnp.where(earlier == 0.0, delta, 0.0)
+    high = delta.astype(BF16)
+    change[pl.ds(0, kmax), :] = high
+    change[pl.ds(kmax, kmax), :] = (delta - high.astype(F32)).astype(BF16)
     out[...] = base[...] + jnp.dot(reach[...], change[...], preferred_element_type=F32)
 
 
@@ -319,37 +317,26 @@
     got = exchange(product, "sep")
     own, sent, over = call(
         solution_kernel,
-        (shape((strip, width), F32), shape((n_leaf, SLOTS, width), BF16), shape((EXTRA, TILE), F32)),
+        (shape((strip, width), F32), shape((n_leaf, SLOTS, width), BF16), shape((1, 1), jnp.int32)),
         [VMEM(), VMEM()],
+        out_specs=(VMEM(), VMEM(), SMEM()),
     )(near(got), near(asked))
 
-    pieces = 4
-    part = leaf_rows // pieces
-    whole = lambda *dims: pl.BlockSpec(dims, lambda i: (0,) * len(dims))
-    tail = [
-        whole(kmax, width),
-        whole(kmax, TILE),
-        pl.BlockSpec((part, width), lambda i: (i, 0)),
-        pl.BlockSpec((part, TILE), lambda i: (i, 0)),
-    ]
-
     def finished(kernel, lead, scratch):
-        return pl.pallas_call(
+        return call(
             kernel,
-            grid=(pieces,),
-            out_shape=shape((leaf_rows, width), F32),
-            in_specs=lead + tail,
-            out_specs=pl.BlockSpec((part, width), lambda i: (i, 0)),
-            scratch_shapes=[pltpu.VMEM((2 * kmax, width), BF16)] + scratch,
+            shape((leaf_rows, width), F32),
+            lead + [VMEM(), VMEM(), VMEM(), VMEM()],
+            [pltpu.VMEM((2 * kmax, width), BF16)] + scratch,
         )
 
     def by_slots():
         got = exchange(sent, ("z", "y"))
         return finished(
             slot_finish_kernel,
-            [SMEM(), SMEM(), whole(n_leaf, SLOTS, width)],
+            [SMEM(), SMEM(), VMEM()],
             [pltpu.VMEM((n_leaf * SLOTS, width), F32), pltpu.VMEM((kmax, width), F32)],
-        )(slots, boundary_count, got, taken, same, base, reach)
+        )(slots, boundary_count, near(got), taken, same, near(base), near(reach))
 
     def by_rings():
         value = jnp.broadcast_to(own.astype(BF16)[None], (n_z, strip, width))
@@ -360,11 +347,11 @@
             [VMEM(), VMEM()],
         )(ring, solved)
         got = exchange(picked, "y")
-        return finished(ring_finish_kernel, [SMEM(), whole(n_y, kmax, width)], [])(
-            boundary_count, got, taken, same, base, reach
+        return finished(ring_finish_kernel, [SMEM(), VMEM()], [])(
+            boundary_count, near(got), taken, same, near(base), near(reach)
         )
 
-    leaf_solution = lax.cond(jnp.max(over) > 0.0, by_rings, by_slots)
+    leaf_solution = lax.cond(over[0, 0] > 0, by_rings, by_slots)
     return leaf_solution[None, None], own[None]
 
 

time: 131 us -> 121 us (0.924)
  the two profiles are of different devices: /device:TPU:2 before, /device:TPU:8 now
where the time goes in v3:
time: 121 us; the launch traced here: 120 us
  blocking collectives  58.8 us (49%)
  waiting for transfers between devices  30.6 us (25%)
  Pallas kernels  17.1 us (14%)
  starting transfers between devices  9.83 us (8%)
  between operations  2.01 us (2%)
  local copies, waits for them, and re-layouts  1.53 us (1%)
    all_to_all x3, blocking collectives, exchange(): return lax.all_to_all(value, axes, split_axis=0, concat_axis=0, tiled=True)  58.8 us
    all_to_all x2, waiting for transfers between devices, exchange(): return lax.all_to_all(value, axes, split_axis=0, concat_axis=0, tiled=True)  30.6 us
    all_to_all x2, starting transfers between devices, exchange(): return lax.all_to_all(value, axes, split_axis=0, concat_axis=0, tiled=True)  9.83 us
    pallas_call x1, Pallas kernels, body(): call(transposed_kernel, (shape((leaf_rows, width), F32), shape((leaf_rows...  4.55 us
    pallas_call x1, Pallas kernels, body(): call(functools.partial(forward_kernel, strip=strip), (shape((leaf_rows, w...  3.74 us
    pallas_call x1, Pallas kernels, by_slots(): finished(slot_finish_kernel, [SMEM(), SMEM(), VMEM()], [pltpu.VMEM((n_lea...  3.01 us
  transfers between devices with their start and end apart: 2, of which 2 were waited for; matrix products, arithmetic and copies ran while one was open for 1% of the time, Pallas kernels for 4%

profile of v3, /device:TPU:8, one launch (start us, length us, event | category | flops | bytes accessed | tf_op | source)
XLA Modules:
  0.0 120.5 jit_solution(13795394318823340674)
XLA Ops:
  1.3 3.7 %shard_map.104 = (bf16[1536,256]{1,0:T(8,128)(2,1)}, bf16[8,72,256]{2,1,0:T(8,128)(2,1)}, f32[64,256]{1,0:T(8,128)S(1)}, s32[1,64]{1,0:T(1,128)S(1)}) custom-call(s32[4,12]{1,0:T(4,128)} %bitcast.24, s32[1,64]{1,0:T(1,128)} %bitcast.29, s32[1,64]{1,0:T(1,128)} %bitcast.26, s32[1,1]{1,0:T(1,128)S(6)} %copy.13.count, f32[1536,256]{1,0:T(8,128)} %bitcast.18, ...), custom_call_target="tpu_custom_call" | custom-call | tf_op jit(solution)/shard_map/pallas_call | solution.py:278
  5.0 18.7 %all_to_all.35.got = bf16[8,72,256]{2,1,0:T(8,128)(2,1)S(1)} all-to-all(bf16[8,72,256]{2,1,0:T(8,128)(2,1)} %get-tuple-element.58), channel_id=1, replica_groups=mesh['z'=8,'y'=8,'sep'=8] {'y'}, dimensions={0} | all-to-all | bytes 589824 | tf_op jit(solution)/shard_map/all_to_all | solution.py:40
  23.7 1.2 %shard_map.105 = bf16[8,32,384]{2,1,0:T(8,128)(2,1)} custom-call(bf16[8,72,256]{2,1,0:T(8,128)(2,1)S(1)} %all_to_all.35.got), custom_call_target="tpu_custom_call" | custom-call | tf_op jit(solution)/shard_map/pallas_call | solution.py:296
  24.9 20.1 %all_to_all.36.got.asked = bf16[8,32,384]{2,1,0:T(8,128)(2,1)S(1)} all-to-all(bf16[8,32,384]{2,1,0:T(8,128)(2,1)} %shard_map.105), channel_id=1, replica_groups=mesh['z'=8,'y'=8,'sep'=8] {'z'}, dimensions={0} | all-to-all | bytes 393216 | tf_op jit(solution)/shard_map/all_to_all | solution.py:40
  45.0 0.0 copy-start.2
  45.0 1.9 %shard_map.106 = bf16[64,32,256]{2,1,0:T(8,128)(2,1)} custom-call(f32[32,256]{1,0:T(8,128)} %bitcast.22, bf16[8,32,384]{2,1,0:T(8,128)(2,1)S(1)} %all_to_all.36.got.asked), custom_call_target="tpu_custom_call" | custom-call | tf_op jit(solution)/shard_map/pallas_call | solution.py:302
  47.0 5.5 %all-to-all-start.5 = ((bf16[64,32,256]{2,1,0:T(8,128)(2,1)}), bf16[64,32,256]{2,1,0:T(8,128)(2,1)S(1)}, u32[]{:S(2)}, u32[]{:S(2)}) async-start(bf16[64,32,256]{2,1,0:T(8,128)(2,1)} %shard_map.106), calls=%async_computation.5 | async-start | bytes 2097152 | tf_op jit(solution)/shard_map/all_to_all | solution.py:40
  52.5 0.0 copy-done.2
  52.5 0.0 copy-start.4
  52.5 0.1 reshape_squeeze.3.strips
  52.6 27.6 %all-to-all-done.5.residual = bf16[64,32,256]{2,1,0:T(8,128)(2,1)S(1)} async-done(((bf16[64,32,256]{2,1,0:T(8,128)(2,1)}), bf16[64,32,256]{2,1,0:T(8,128)(2,1)S(1)}, u32[]{:S(2)}, u32[]{:S(2)}) %all-to-all-start.5) | async-done | bytes 1048608 | tf_op jit(solution)/shard_map/all_to_all | solution.py:40
  80.2 1.9 %shard_map.107 = f32[8,40,256]{2,1,0:T(8,128)} custom-call(s32[4,8]{1,0:T(4,128)} %bitcast.28, bf16[8,32,512]{2,1,0:T(8,128)(2,1)S(1)} %reshape_squeeze.3.strips, bf16[64,32,256]{2,1,0:T(8,128)(2,1)S(1)} %all-to-all-done.5.residual, bf16[8,32,384]{2,1,0:T(8,128)(2,1)S(1)} %all_to_all.36.got.asked), custom_call_target="tpu_custom_call" | custom-call | tf_op jit(solution)/shard_map/pallas_call | solution.py:312
  82.1 4.3 %all-to-all-start.6 = ((f32[8,40,256]{2,1,0:T(8,128)}), f32[8,40,256]{2,1,0:T(8,128)S(1)}, u32[]{:S(2)}, u32[]{:S(2)}) async-start(f32[8,40,256]{2,1,0:T(8,128)} %shard_map.107), calls=%async_computation.6 | async-start | bytes 655360 | tf_op jit(solution)/shard_map/all_to_all | solution.py:40
  86.4 0.0 copy-done.4
  86.4 0.6 pad_add_fusion.row_lanes
  87.0 4.5 %shard_map.109 = (f32[1536,256]{1,0:T(8,128)}, bf16[1536,128]{1,0:T(8,128)(2,1)S(1)}, f32[64,128]{1,0:T(8,128)S(1)}) custom-call(s32[4,12]{1,0:T(4,128)} %bitcast.25, s32[1,1]{1,0:T(1,128)S(6)} %copy.13.count, bf16[1536,256]{1,0:T(8,128)(2,1)} %get-tuple-element.63.forward, bf16[12,4,128,128]{3,2,1,0:T(8,128)(2,1)} %bitcast.17, s32[1,128]{1,0:T(1,128)} %pad_add_fusion.row_lanes), custom_call_target="tpu_custom_call" | custom-call | tf_op jit(solution)/shard_map/pallas_call | solution.py:305
  91.5 3.1 %all-to-all-done.6.got = f32[8,40,256]{2,1,0:T(8,128)S(1)} async-done(((f32[8,40,256]{2,1,0:T(8,128)}), f32[8,40,256]{2,1,0:T(8,128)S(1)}, u32[]{:S(2)}, u32[]{:S(2)}) %all-to-all-start.6) | async-done | bytes 327712 | tf_op jit(solution)/shard_map/all_to_all | solution.py:40
  94.6 0.8 shard_map.108
  95.3 0.0 copy-start.3
  96.0 0.0 copy-done.3
  96.0 24.4 %conditional.1 = (f32[1,1,1536,256]{3,2,1,0:T(8,128)}) conditional(s32[]{:T(128)} %bitcast.12, (bf16[64,8,256]{2,1,0:T(8,128)(2,1)S(1)}, s32[1,64]{1,0:T(1,128)S(1)}, s32[1,1]{1,0:T(1,128)}, f32[64,256]{1,0:T(8,128)S(1)}, f32[64,128]{1,0:T(8,128)S(1)}, /*index=5*/f32[1536,256]{1,0:T(8,128)}, bf16[1536,128]{1,0:T(8,128)(2,1)S(1)}) %tuple.17, ...), branch_computations={%region_0.0_spmd, %region_1.0_spmd} | conditional | flops 8192 | bytes 7274532 | solution.py:354
  96.0 20.0 %all_to_all.32.got = bf16[64,8,256]{2,1,0:T(8,128)(2,1)S(1)} all-to-all(bf16[64,8,256]{2,1,0:T(8,128)(2,1)S(1)} %get-tuple-element.34), channel_id=1, replica_groups=mesh['z'=8,'y'=8,'sep'=8] {'z','y'}, dimensions={0} | all-to-all | bytes 524288 | tf_op jit(solution)/shard_map/cond/branch_0_fun/all_to_all | solution.py:40
  116.0 1.4 %copy-done = f32[1536,256]{1,0:T(8,128)S(1)} copy-done((f32[1536,256]{1,0:T(8,128)S(1)}, f32[1536,256]{1,0:T(8,128)}, u32[]{:S(2)}) %copy-start) | copy-done | bytes 1572888 | tf_op jit(solution)/shard_map/cond
  117.4 3.0 %branch_0_fun.1 = f32[1536,256]{1,0:T(8,128)} custom-call(s32[1,64]{1,0:T(1,128)S(1)} %get-tuple-element.32.slots, s32[1,1]{1,0:T(1,128)} %get-tuple-element.33.count, bf16[64,8,256]{2,1,0:T(8,128)(2,1)S(1)} %all_to_all.32.got, f32[64,256]{1,0:T(8,128)S(1)} %get-tuple-element.35.taken, f32[64,128]{1,0:T(8,128)S(1)} %get-tuple-element.36.same, ...), custom_call_target="tpu_custom_call" | custom-call | tf_op jit(solution)/shard_map/cond/branch_0_fun/pallas_call | solution.py:335
  (1 shorter events, 0.0 us)
Async XLA Ops:
  45.0 7.5 %copy-start.2 = (bf16[8,32,1,4,128]{4,3,2,1,0:T(4,128)(2,1)S(1)}, bf16[8,32,1,4,128]{4,3,2,1,0:T(4,128)(2,1)}, u32[]{:S(2)}) copy-start(bf16[8,32,1,4,128]{4,3,2,1,0:T(4,128)(2,1)} %param.18) | copy-start | bytes 786436
  47.0 33.2 %all-to-all-start.5 = ((bf16[64,32,256]{2,1,0:T(8,128)(2,1)}), bf16[64,32,256]{2,1,0:T(8,128)(2,1)S(1)}, u32[]{:S(2)}, u32[]{:S(2)}) async-start(bf16[64,32,256]{2,1,0:T(8,128)(2,1)} %shard_map.106), calls=%async_computation.5 | async-start | bytes 2097152 | tf_op jit(solution)/shard_map/all_to_all | solution.py:40
  52.5 33.9 %copy-start.4 = (s32[1,1,64]{2,1,0:T(1,128)S(1)}, s32[1,1,64]{2,1,0:T(1,128)}, u32[]{:S(2)}) copy-start(s32[1,1,64]{2,1,0:T(1,128)} %param.14) | copy-start | bytes 772
  82.1 12.5 %all-to-all-start.6 = ((f32[8,40,256]{2,1,0:T(8,128)}), f32[8,40,256]{2,1,0:T(8,128)S(1)}, u32[]{:S(2)}, u32[]{:S(2)}) async-start(f32[8,40,256]{2,1,0:T(8,128)} %shard_map.107), calls=%async_computation.6 | async-start | bytes 655360 | tf_op jit(solution)/shard_map/all_to_all | solution.py:40
  95.3 0.7 copy-start.3
  116.0 1.4 %copy-start = (f32[1536,256]{1,0:T(8,128)S(1)}, f32[1536,256]{1,0:T(8,128)}, u32[]{:S(2)}) copy-start(f32[1536,256]{1,0:T(8,128)} %get-tuple-element.37.base) | copy-start | bytes 4718596 | tf_op jit(solution)/shard_map/cond

commit v4 on v3

--- a/solution.py
+++ b/solution.py
@@ -110,81 +110,93 @@
         yield p, info, jnp.where(row_id == target, 1.0, 0.0).astype(BF16)
 
 
-def combine_kernel(got, sent, *, n_y, strip):
+def combine_kernel(got, load, sent, summed, *, n_y, strip):
     peers, _, width = got.shape
-    n_z = sent.shape[0]
+    n_z, _, half = sent.shape
+    n_rows = n_z * strip
     kmax = got.shape[1] - EXTRA
-    total, wanted, over = None, [], None
-    for p, info, hot in ring_targets(got, n_z * strip, n_y, strip):
+    total, asked, over = None, None, None
+    for p, info, hot in ring_targets(got, n_rows, n_y, strip):
         term = jnp.dot(hot, got[p, pl.ds(0, kmax), :], preferred_element_type=F32)
         total = term if total is None else total + term
         slot = lax.broadcasted_iota(jnp.int32, (TILE, kmax), 0)
         place = info[2:3, :kmax].astype(jnp.int32)
         mine = jnp.where(slot == place + p * SLOTS, 1.0, 0.0)
         mine = jnp.where(place < SLOTS, mine, 0.0).astype(BF16)
-        wanted.append(over_lanes(hot, mine))
+        wanted = over_lanes(hot, mine)
+        asked = wanted if asked is None else asked + wanted
         flag = info[3:4, :TILE]
         over = flag if over is None else jnp.maximum(over, flag)
-    asked = wanted[0]
-    for w in wanted[1:]:
-        asked = asked + w
     lane = lax.broadcasted_iota(jnp.int32, asked.shape, 1)
-    asked = jnp.where(lane < peers * SLOTS, asked, jnp.broadcast_to(over, asked.shape))
-    sent[:, :, pl.ds(0, width)] = total.astype(BF16).reshape(n_z, strip, width)
-    sent[:, :, pl.ds(width, TILE)] = asked.astype(BF16).reshape(n_z, strip, TILE)
-
-
-def residual_kernel(load, got, sent):
-    width = load.shape[1]
-    total = got[0, :, pl.ds(0, width)].astype(F32)
+    asked = jnp.where(lane < peers * SLOTS, asked, jnp.broadcast_to(over, asked.shape)).astype(BF16)
+    summed[...] = -total
+    z = lax.axis_index("zh") * 2 + lax.axis_index("zl")
+    own = pl.ds(pl.multiple_of(z * strip, strip), strip)
+    summed[own, :] = summed[own, :] + load[...]
+    halves = [summed[:, pl.ds(h * half, half)].astype(BF16) for h in range(2)]
+    for p in range(n_z):
+        sent[p, pl.ds(0, n_rows), :] = halves[p % 2]
+        sent[p, pl.ds(n_rows, strip), :] = asked[p * strip : (p + 1) * strip]
+
+
+def residual_kernel(got, sent):
+    n_rows = sent.shape[1]
+    total = got[0, pl.ds(0, n_rows), :].astype(F32)
     for p in range(1, got.shape[0]):
-        total = total + got[p, :, pl.ds(0, width)].astype(F32)
-    value = (load[...] - total).astype(BF16)
+        total = total + got[p, pl.ds(0, n_rows), :].astype(F32)
+    value = total.astype(BF16)
     for p in range(sent.shape[0]):
         sent[p] = value
 
 
-def separator_kernel(cols, strips, residual, got, product):
+def separator_kernel(cols, near_cols, strips, near_strips, residual, got, product):
     per_row, sections = cols.shape
-    _, strip, width = residual.shape
+    n_y, n_rows, half = residual.shape
+    strip = product.shape[1] - EXTRA
     per_tile = TILE // strip
-    for q in range(sections):
-        total = None
-        for k in range(0, per_row, 2):
-            right = jnp.concatenate(
-                [
-                    residual[pl.ds(cols[k + i, q] * per_tile, per_tile)].reshape(TILE, width)
-                    for i in range(2)
-                ],
-                axis=0,
-            )
-            term = jnp.dot(strips[q, :, pl.ds(k * TILE, 2 * TILE)], right, preferred_element_type=F32)
-            total = term if total is None else total + term
-        product[q, pl.ds(0, strip), :] = total
-    over = got[0, pl.ds(0, EXTRA), pl.ds(width, TILE)].astype(F32)
+    zl = lax.axis_index("zl")
+
+    def tile(c):
+        parts = n_y // per_tile
+        y = (c % parts) * per_tile
+        at = pl.multiple_of((c // parts) * strip, strip)
+        return residual[pl.ds(y, per_tile), pl.ds(at, strip), :].reshape(TILE, half)
+
+    over = got[0, pl.ds(n_rows, EXTRA), :].astype(F32)
     for p in range(1, got.shape[0]):
-        over = jnp.maximum(over, got[p, pl.ds(0, EXTRA), pl.ds(width, TILE)].astype(F32))
-    over = jnp.concatenate([over] * (width // TILE), axis=1)
-    for q in range(sections):
-        product[q, pl.ds(strip, EXTRA), :] = over
+        over = jnp.maximum(over, got[p, pl.ds(n_rows, EXTRA), :].astype(F32))
+    for which, wanted, rows in ((zl, cols, strips), (1 - zl, near_cols, near_strips)):
+        for q in range(sections):
+            total = None
+            for k in range(0, per_row, 2):
+                right = jnp.concatenate([tile(wanted[k, q]), tile(wanted[k + 1, q])], axis=0)
+                left = rows[q, pl.ds(0, strip), pl.ds(k * TILE, 2 * TILE)]
+                term = jnp.dot(left, right, preferred_element_type=F32)
+                total = term if total is None else total + term
+            product[which * sections + q, pl.ds(0, strip), :] = total
+            product[which * sections + q, pl.ds(strip, EXTRA), :] = over
 
 
 def solution_kernel(got, asked, own, sent, over):
     strip, width = own.shape
-    total = got[0]
-    for p in range(1, got.shape[0]):
-        total = total + got[p]
-    own[...] = total[:strip]
-    most = got[0, pl.ds(strip, EXTRA), pl.ds(0, TILE)]
-    for p in range(1, got.shape[0]):
-        most = jnp.maximum(most, got[p, pl.ds(strip, EXTRA), pl.ds(0, TILE)])
+    half = got.shape[2]
+    sections = got.shape[0] // 2
+    most = None
+    for h in range(2):
+        total = None
+        for p in range(h * sections, (h + 1) * sections):
+            term = got[p, pl.ds(0, strip), :]
+            total = term if total is None else total + term
+            flag = got[p, pl.ds(strip, EXTRA), :]
+            most = flag if most is None else jnp.maximum(most, flag)
+        own[:, pl.ds(h * half, half)] = total
     lane = lax.broadcasted_iota(jnp.int32, most.shape, 1)
     over[0, 0] = (jnp.max(jnp.where(lane == TILE - 1, most, 0.0)) > 0.0).astype(jnp.int32)
-    value = total[:strip].astype(BF16)
-    n_z = asked.shape[0]
+    value = own[...].astype(BF16)
+    n_z, held, _ = asked.shape
     per = sent.shape[0] // n_z
     for p in range(n_z):
-        rows = over_rows(asked[p, :, pl.ds(width, TILE)], value)[: per * SLOTS]
+        rows = over_rows(asked[p, pl.ds(held - strip, strip), :], value)[: per * SLOTS]
         sent[pl.ds(p * per, per)] = rows.astype(BF16).reshape(per, SLOTS, width)
 
 
@@ -267,7 +279,8 @@
     inverse_tiles,
     inverse_cols,
 ):
-    n_z, n_y = lax.axis_size("z"), lax.axis_size("y")
+    z_axes = ("zh", "zl")
+    n_z, n_y = lax.axis_size(z_axes), lax.axis_size("y")
     n_sep, n_leaf = lax.axis_size("sep"), n_z * n_y
     shots, tiles, cols = shot_columns[0, 0], factor_tiles[0, 0], factor_cols[0, 0].T
     rows, own_map, load = boundary_rows[0], boundary_map[0], separator_load[0]
@@ -275,6 +288,15 @@
     kmax = rows.shape[1]
     strip = load.shape[0]
     shape = jax.ShapeDtypeStruct
+    tile_cols = inverse_cols[:, 0, 0]
+    strips = inverse_tiles[:, :, 0].reshape(n_sep, strip, -1)
+    noted = jnp.pad(
+        tile_cols.astype(BF16)[:, None],
+        ((0, 0), (0, EXTRA - 1), (0, strips.shape[2] - tile_cols.shape[1])),
+    )
+    bundle = jnp.concatenate([strips, noted], axis=1)
+    near_bundle = lax.ppermute(bundle, "zl", [(0, 1), (1, 0)])
+    near_cols = near_bundle[:, strip, : tile_cols.shape[1]].astype(jnp.int32)
     forward, sent, taken, slots = call(
         functools.partial(forward_kernel, strip=strip),
         (
@@ -293,14 +315,16 @@
         (VMEM(), VMEM(), VMEM(), SMEM()),
     )(cols, rows, own_map, boundary_count, shots, tiles, own_map)
     ring = exchange(sent, "y")
+    half = width // 2
     sent = call(
         functools.partial(combine_kernel, n_y=n_y, strip=strip),
-        shape((n_z, strip, width + TILE), BF16),
-        [VMEM()],
-    )(near(ring))
-    asked = exchange(sent, "z")
-    sent = call(residual_kernel, shape((n_leaf, strip, width), BF16), [VMEM(), VMEM()])(load, near(asked))
-    residual = exchange(sent, ("z", "y"))
+        shape((n_z, n_z * strip + strip, half), BF16),
+        [VMEM(), VMEM()],
+        [pltpu.VMEM((n_z * strip, width), F32)],
+    )(near(ring), load)
+    asked = exchange(sent, z_axes)
+    sent = call(residual_kernel, shape((n_y, n_z * strip, half), BF16), [VMEM()])(near(asked))
+    residual = exchange(sent, "y")
     held_rows, _ = lax.optimization_barrier((rows, asked[0, 0, 0]))
     base, reach, same = call(
         transposed_kernel,
@@ -308,13 +332,12 @@
         [SMEM(), SMEM(), VMEM(), VMEM(), VMEM()],
         [pltpu.VMEM((leaf_rows, width + TILE), F32)],
     )(cols, boundary_count, forward, tiles, jnp.concatenate([held_rows, held_rows], axis=1))
-    strips = inverse_tiles[:, :, 0].reshape(n_sep, strip, -1)
     product = call(
         separator_kernel,
-        shape((n_sep, strip + EXTRA, width), F32),
-        [SMEM(), VMEM(), VMEM(), VMEM()],
-    )(inverse_cols[:, 0, 0].T, near(strips), near(residual), near(asked))
-    got = exchange(product, "sep")
+        shape((2 * n_sep, strip + EXTRA, half), F32),
+        [SMEM(), SMEM(), VMEM(), VMEM(), VMEM(), VMEM()],
+    )(tile_cols.T, near_cols.T, near(bundle), near(near_bundle), near(residual), near(asked))
+    got = exchange(product, ("zl", "sep"))
     own, sent, over = call(
         solution_kernel,
         (shape((strip, width), F32), shape((n_leaf, SLOTS, width), BF16), shape((1, 1), jnp.int32)),
@@ -331,16 +354,16 @@
         )
 
     def by_slots():
-        got = exchange(sent, ("z", "y"))
+        got = exchange(sent, z_axes + ("y",))
         return finished(
             slot_finish_kernel,
             [SMEM(), SMEM(), VMEM()],
             [pltpu.VMEM((n_leaf * SLOTS, width), F32), pltpu.VMEM((kmax, width), F32)],
-        )(slots, boundary_count, near(got), taken, same, near(base), near(reach))
+        )(slots, boundary_count, near(got), taken, same, base, reach)
 
     def by_rings():
         value = jnp.broadcast_to(own.astype(BF16)[None], (n_z, strip, width))
-        solved = exchange(value, "z").reshape(-1, width)
+        solved = exchange(value, z_axes).reshape(-1, width)
         picked = call(
             functools.partial(pick_kernel, n_y=n_y, strip=strip),
             shape((n_y, kmax, width), BF16),
@@ -348,7 +371,7 @@
         )(ring, solved)
         got = exchange(picked, "y")
         return finished(ring_finish_kernel, [SMEM(), VMEM()], [])(
-            boundary_count, near(got), taken, same, near(base), near(reach)
+            boundary_count, near(got), taken, same, base, reach
         )
 
     leaf_solution = lax.cond(over[0, 0] > 0, by_rings, by_slots)
@@ -358,8 +381,8 @@
 def solution(mesh):
     n_leaf, n_sep = mesh.shape["leaf"], mesh.shape["sep"]
     n_y = 8
-    torus = Mesh(mesh.devices.reshape(n_leaf // n_y, n_y, n_sep), ("z", "y", "sep"))
-    leaf = ("z", "y")
+    torus = Mesh(mesh.devices.reshape(n_leaf // n_y // 2, 2, n_y, n_sep), ("zh", "zl", "y", "sep"))
+    leaf = ("zh", "zl", "y")
     placed = (
         P(leaf, "sep", None, None),
         P(leaf, "sep", None, None, None, None),

time: 121 us -> 113 us (0.934)
  waiting for transfers between devices: 30.6 us -> 15.5 us
  blocking collectives: 58.8 us -> 64.3 us
  starting transfers between devices: 9.83 us -> 12.6 us
    all_to_all x2, waiting for transfers between devices: 30.6 us -> 8.98 us  [exchange(): return lax.all_to_all(value, axes, split_axis=0, concat_axis=0, tiled=True)]
    ppermute x0 -> x1, waiting for transfers between devices: none -> 6.49 us  [body(): near_bundle = lax.ppermute(bundle, 'zl', [(0, 1), (1, 0)])]
    all_to_all x3, blocking collectives: 58.8 us -> 64.3 us  [exchange(): return lax.all_to_all(value, axes, split_axis=0, concat_axis=0, tiled=True)]
    ppermute x0 -> x1, starting transfers between devices: none -> 2.47 us  [body(): near_bundle = lax.ppermute(bundle, 'zl', [(0, 1), (1, 0)])]
    cond x2 -> x0, local copies, waits for them, and re-layouts: 1.41 us -> none
  transfers between devices with their start and end apart: 2 -> 3, of which waited for: 2 -> 3; matrix products, arithmetic and copies ran while one was open for 1% -> 1% of each run, Pallas kernels for 4% -> 3%
where the time goes in v4:
time: 113 us; the launch traced here: 112 us
  blocking collectives  64.3 us (57%)
  Pallas kernels  16.1 us (14%)
  waiting for transfers between devices  15.5 us (14%)
  starting transfers between devices  12.6 us (11%)
  between operations  2 us (2%)
    all_to_all x3, blocking collectives, exchange(): return lax.all_to_all(value, axes, split_axis=0, concat_axis=0, tiled=True)  64.3 us
    all_to_all x2, starting transfers between devices, exchange(): return lax.all_to_all(value, axes, split_axis=0, concat_axis=0, tiled=True)  10.1 us
    all_to_all x2, waiting for transfers between devices, exchange(): return lax.all_to_all(value, axes, split_axis=0, concat_axis=0, tiled=True)  8.98 us
    ppermute x1, waiting for transfers between devices, body(): near_bundle = lax.ppermute(bundle, 'zl', [(0, 1), (1, 0)])  6.49 us
    pallas_call x1, Pallas kernels, body(): call(functools.partial(forward_kernel, strip=strip), (shape((leaf_rows, w...  3.74 us
    pallas_call x1, Pallas kernels, body(): call(transposed_kernel, (shape((leaf_rows, width), F32), shape((leaf_rows...  3.44 us
    pallas_call x1, Pallas kernels, by_slots(): finished(slot_finish_kernel, [SMEM(), SMEM(), VMEM()], [pltpu.VMEM((n_lea...  3.01 us
    ppermute x1, starting transfers between devices, body(): near_bundle = lax.ppermute(bundle, 'zl', [(0, 1), (1, 0)])  2.47 us
  transfers between devices with their start and end apart: 3, of which 3 were waited for; matrix products, arithmetic and copies ran while one was open for 1% of the time, Pallas kernels for 3%

profile of v4, /device:TPU:8, one launch (start us, length us, event | category | flops | bytes accessed | tf_op | source)
XLA Modules:
  0.0 111.9 jit_solution(1491807834031457954)
XLA Ops:
  1.3 3.7 %shard_map.104 = (bf16[1536,256]{1,0:T(8,128)(2,1)}, bf16[8,72,256]{2,1,0:T(8,128)(2,1)}, f32[64,256]{1,0:T(8,128)S(1)}, s32[1,64]{1,0:T(1,128)S(1)}) custom-call(s32[4,12]{1,0:T(4,128)} %bitcast.29, s32[1,64]{1,0:T(1,128)} %bitcast.35, s32[1,64]{1,0:T(1,128)} %bitcast.33, s32[1,1]{1,0:T(1,128)S(6)} %copy.17.count, f32[1536,256]{1,0:T(8,128)} %bitcast.23, ...), custom_call_target="tpu_custom_call" | custom-call | tf_op jit(solution)/shard_map/pallas_call | solution.py:300
  5.0 18.7 %all_to_all.35.got = bf16[8,72,256]{2,1,0:T(8,128)(2,1)S(1)} all-to-all(bf16[8,72,256]{2,1,0:T(8,128)(2,1)} %get-tuple-element.58), channel_id=1, replica_groups=mesh['zh'=4,'zl'=2,'y'=8,'sep'=8] {'y'}, dimensions={0} | all-to-all | bytes 589824 | tf_op jit(solution)/shard_map/all_to_all | solution.py:40
  23.7 2.2 %shard_map.105 = bf16[8,288,128]{2,1,0:T(8,128)(2,1)} custom-call(bf16[8,72,256]{2,1,0:T(8,128)(2,1)S(1)} %all_to_all.35.got, f32[32,256]{1,0:T(8,128)} %bitcast.27), custom_call_target="tpu_custom_call" | custom-call | tf_op jit(solution)/shard_map/pallas_call | solution.py:319
  25.9 26.6 %all_to_all.36.got.asked = bf16[8,288,128]{2,1,0:T(8,128)(2,1)S(1)} all-to-all(bf16[8,288,128]{2,1,0:T(8,128)(2,1)} %shard_map.105), channel_id=1, replica_groups=mesh['zh'=4,'zl'=2,'y'=8,'sep'=8] {'zh','zl'}, dimensions={0} | all-to-all | bytes 1179648 | tf_op jit(solution)/shard_map/all_to_all | solution.py:40
  52.4 0.9 shard_map.106
  53.3 5.7 %all-to-all-start.5 = ((bf16[8,256,128]{2,1,0:T(8,128)(2,1)}), bf16[8,256,128]{2,1,0:T(8,128)(2,1)S(1)}, u32[]{:S(2)}, u32[]{:S(2)}) async-start(bf16[8,256,128]{2,1,0:T(8,128)(2,1)} %shard_map.106), calls=%async_computation.5 | async-start | bytes 1048576 | tf_op jit(solution)/shard_map/all_to_all | solution.py:40
  59.1 0.0 copy-done.1
  59.1 0.1 copy.13
  59.2 0.1 reshape_squeeze.3
  59.3 0.0 copy-start.2
  59.3 2.5 %collective-permute-start = (bf16[8,40,512]{2,1,0:T(8,128)(2,1)S(1)}, bf16[8,40,512]{2,1,0:T(8,128)(2,1)S(1)}, u32[]{:S(2)}, u32[]{:S(2)}) collective-permute-start(bf16[8,40,512]{2,1,0:T(8,128)(2,1)S(1)} %fusion.1.strips), channel_id=1, source_target_pairs={{0,64},{64,0},{1,65},{65,1},{2,66},{66,2},{3,67},{67,3},{4,68},{68... | collective-permute-start | bytes 983048 | tf_op jit(solution)/shard_map/ppermute | solution.py:298
  61.8 6.5 %collective-permute-done.near_strips = bf16[8,40,512]{2,1,0:T(8,128)(2,1)S(1)} collective-permute-done((bf16[8,40,512]{2,1,0:T(8,128)(2,1)S(1)}, bf16[8,40,512]{2,1,0:T(8,128)(2,1)S(1)}, u32[]{:S(2)}, u32[]{:S(2)}) %collective-permute-start) | collective-permute-done | bytes 327712 | tf_op jit(solution)/shard_map/ppermute | solution.py:298
  68.3 0.7 copy.14
  69.0 4.3 %all-to-all-done.5.residual = bf16[8,256,128]{2,1,0:T(8,128)(2,1)S(1)} async-done(((bf16[8,256,128]{2,1,0:T(8,128)(2,1)}), bf16[8,256,128]{2,1,0:T(8,128)(2,1)S(1)}, u32[]{:S(2)}, u32[]{:S(2)}) %all-to-all-start.5) | async-done | bytes 524320 | tf_op jit(solution)/shard_map/all_to_all | solution.py:40
  73.3 2.1 %shard_map.107 = f32[16,40,128]{2,1,0:T(8,128)} custom-call(s32[4,8]{1,0:T(4,128)} %bitcast.32, s32[4,8]{1,0:T(4,128)} %bitcast.31, bf16[8,40,512]{2,1,0:T(8,128)(2,1)S(1)} %fusion.1.strips, bf16[8,40,512]{2,1,0:T(8,128)(2,1)S(1)} %collective-permute-done.near_strips, bf16[8,256,128]{2,1,0:T(8,128)(2,1)S(1)} %all-to-all-done.5.residual, ...), custom_call_target="tpu_custom_call" | custom-call | tf_op jit(solution)/shard_map/pallas_call | solution.py:335
  75.3 4.4 %all-to-all-start.6 = ((f32[16,40,128]{2,1,0:T(8,128)}), f32[16,40,128]{2,1,0:T(8,128)S(1)}, u32[]{:S(2)}, u32[]{:S(2)}) async-start(f32[16,40,128]{2,1,0:T(8,128)} %shard_map.107), calls=%async_computation.6 | async-start | bytes 655360 | tf_op jit(solution)/shard_map/all_to_all | solution.py:40
  79.7 0.0 copy-done.2
  79.7 0.6 pad_add_fusion.row_lanes
  80.3 3.4 %shard_map.109 = (f32[1536,256]{1,0:T(8,128)S(1)}, bf16[1536,128]{1,0:T(8,128)(2,1)S(1)}, f32[64,128]{1,0:T(8,128)S(1)}) custom-call(s32[4,12]{1,0:T(4,128)} %bitcast.30, s32[1,1]{1,0:T(1,128)S(6)} %copy.17.count, bf16[1536,256]{1,0:T(8,128)(2,1)} %get-tuple-element.63.forward, bf16[12,4,128,128]{3,2,1,0:T(8,128)(2,1)} %bitcast.22, ...), custom_call_target="tpu_custom_call" | custom-call | tf_op jit(solution)/shard_map/pallas_call | solution.py:329
  83.8 4.7 %all-to-all-done.6.got = f32[16,40,128]{2,1,0:T(8,128)S(1)} async-done(((f32[16,40,128]{2,1,0:T(8,128)}), f32[16,40,128]{2,1,0:T(8,128)S(1)}, u32[]{:S(2)}, u32[]{:S(2)}) %all-to-all-start.6) | async-done | bytes 327712 | tf_op jit(solution)/shard_map/all_to_all | solution.py:40
  88.5 0.7 shard_map.108
  89.9 22.1 %conditional.1 = (f32[1,1,1536,256]{3,2,1,0:T(8,128)}) conditional(s32[]{:T(128)} %bitcast.15, (bf16[64,8,256]{2,1,0:T(8,128)(2,1)S(1)}, s32[1,64]{1,0:T(1,128)S(1)}, s32[1,1]{1,0:T(1,128)}, f32[64,256]{1,0:T(8,128)S(1)}, f32[64,128]{1,0:T(8,128)S(1)}, /*index=5*/f32[1536,256]{1,0:T(8,128)S(1)}, bf16[1536,128]{1,0:T(8,128)(2,1)S(1)}) %tuple.17, ...), branch_computations={%region_0.1_spmd, %region_1.2_spmd} | conditional | flops 8192 | bytes 983048 | solution.py:377
  89.9 19.1 %all_to_all.32.got = bf16[64,8,256]{2,1,0:T(8,128)(2,1)S(1)} all-to-all(bf16[64,8,256]{2,1,0:T(8,128)(2,1)S(1)} %get-tuple-element.34), channel_id=1, replica_groups=mesh['zh'=4,'zl'=2,'y'=8,'sep'=8] {'zh','zl','y'}, dimensions={0} | all-to-all | bytes 524288 | tf_op jit(solution)/shard_map/cond/branch_0_fun/all_to_all | solution.py:40
  108.9 3.0 %branch_0_fun.1 = f32[1536,256]{1,0:T(8,128)} custom-call(s32[1,64]{1,0:T(1,128)S(1)} %get-tuple-element.32.slots, s32[1,1]{1,0:T(1,128)} %get-tuple-element.33.count, bf16[64,8,256]{2,1,0:T(8,128)(2,1)S(1)} %all_to_all.32.got, f32[64,256]{1,0:T(8,128)S(1)} %get-tuple-element.35.taken, f32[64,128]{1,0:T(8,128)S(1)} %get-tuple-element.36.same, ...), custom_call_target="tpu_custom_call" | custom-call | tf_op jit(solution)/shard_map/cond/branch_0_fun/pallas_call | solution.py:358
  (6 shorter events, 0.0 us)
Async XLA Ops:
  25.9 33.2 %copy-start.1 = (s32[8,1,1,4]{0,3,2,1:T(4,128)S(1)}, s32[8,1,1,4]{0,3,2,1:T(4,128)}, u32[]{:S(2)}) copy-start(s32[8,1,1,4]{0,3,2,1:T(4,128)} %param.19) | copy-start | bytes 388
  25.9 33.3 %copy-start = (bf16[8,32,1,4,128]{4,3,2,1,0:T(4,128)(2,1)S(1)}, bf16[8,32,1,4,128]{4,3,2,1,0:T(4,128)(2,1)}, u32[]{:S(2)}) copy-start(bf16[8,32,1,4,128]{4,3,2,1,0:T(4,128)(2,1)} %param.18) | copy-start | bytes 786436
  53.3 19.9 %all-to-all-start.5 = ((bf16[8,256,128]{2,1,0:T(8,128)(2,1)}), bf16[8,256,128]{2,1,0:T(8,128)(2,1)S(1)}, u32[]{:S(2)}, u32[]{:S(2)}) async-start(bf16[8,256,128]{2,1,0:T(8,128)(2,1)} %shard_map.106), calls=%async_computation.5 | async-start | bytes 1048576 | tf_op jit(solution)/shard_map/all_to_all | solution.py:40
  59.3 20.5 %copy-start.2 = (s32[1,1,64]{2,1,0:T(1,128)S(1)}, s32[1,1,64]{2,1,0:T(1,128)}, u32[]{:S(2)}) copy-start(s32[1,1,64]{2,1,0:T(1,128)} %param.14) | copy-start | bytes 772
  59.3 9.0 %collective-permute-start = (bf16[8,40,512]{2,1,0:T(8,128)(2,1)S(1)}, bf16[8,40,512]{2,1,0:T(8,128)(2,1)S(1)}, u32[]{:S(2)}, u32[]{:S(2)}) collective-permute-start(bf16[8,40,512]{2,1,0:T(8,128)(2,1)S(1)} %fusion.1.strips), channel_id=1, source_target_pairs={{0,64},{64,0},{1,65},{65,1},{2,66},{66,2},{3,67},{67,3},{4,68},{68... | collective-permute-start | bytes 983048 | tf_op jit(solution)/shard_map/ppermute | solution.py:298
  75.3 13.1 %all-to-all-start.6 = ((f32[16,40,128]{2,1,0:T(8,128)}), f32[16,40,128]{2,1,0:T(8,128)S(1)}, u32[]{:S(2)}, u32[]{:S(2)}) async-start(f32[16,40,128]{2,1,0:T(8,128)} %shard_map.107), calls=%async_computation.6 | async-start | bytes 655360 | tf_op jit(solution)/shard_map/all_to_all | solution.py:40

commit v5 on v4

--- a/solution.py
+++ b/solution.py
@@ -12,11 +12,13 @@
 DEAD = 255
 SLOTS = 8
 EXTRA = 8
+PIECES = 4
 F32 = jnp.float32
 BF16 = jnp.bfloat16
 
 SMEM = functools.partial(pl.BlockSpec, memory_space=pltpu.SMEM)
 VMEM = functools.partial(pl.BlockSpec, memory_space=pltpu.VMEM)
+ANY = functools.partial(pl.BlockSpec, memory_space=pl.ANY)
 
 
 def near(value):
@@ -40,6 +42,16 @@
     return lax.all_to_all(value, axes, split_axis=0, concat_axis=0, tiled=True)
 
 
+def chunks(source, target, sems):
+    n = sems.shape[0]
+    size = source.shape[0] // n
+    made = []
+    for i in range(n):
+        at = pl.ds(i * size, size)
+        made.append((at, pltpu.make_async_copy(source.at[at], target.at[at], sems.at[i])))
+    return made
+
+
 def over_rows(left, right):
     return lax.dot_general(left, right, (((0,), (0,)), ((), ())), preferred_element_type=F32)
 
@@ -49,15 +61,38 @@
 
 
 def forward_kernel(
-    cols, rows, targets, count, shots, tiles, own_map,
+    cols, rows, targets, count, far_shots, far_tiles, own_map,
     forward, sent, taken, slots,
-    rounded, exact, picked, filled, *, strip,
+    shots, tiles, shot_sems, tile_sems, rounded, exact, picked, filled, *, strip,
 ):
     count_rows, per_row = tiles.shape[0], tiles.shape[1]
+    shot_copies = chunks(far_shots, shots, shot_sems)
+    tile_copies = chunks(far_tiles, tiles, tile_sems)
+    for _, copy in shot_copies + tile_copies:
+        copy.start()
     peers, _, width = sent.shape
     kmax = taken.shape[0]
-    rounded[...] = shots[...].astype(BF16)
+    live = count[0, 0]
+    for s in range(filled.shape[0]):
+        filled[s] = 0
+    lane = lax.broadcasted_iota(jnp.int32, own_map.shape, 1)
+    place = jnp.zeros(own_map.shape, jnp.int32)
+    most = 0
+    for k in range(kmax):
+        owner = targets[0, k] // strip
+        slot = filled[owner]
+        alive = (k < live).astype(jnp.int32)
+        filled[owner] = slot + alive
+        most = jnp.maximum(most, alive * (slot + 1))
+        place = jnp.where(lane == k, slot, place)
+        slots[0, k] = jnp.where(k < live, owner * SLOTS + jnp.minimum(slot, SLOTS - 1), -1)
+    for at, copy in shot_copies:
+        copy.wait()
+        rounded[at] = shots[at].astype(BF16)
+    span = count_rows // len(tile_copies)
     for t in range(count_rows):
+        if t % span == 0:
+            tile_copies[t // span][1].wait()
         total = None
         for k in range(0, per_row, 2):
             left = jnp.concatenate([tiles[t, k], tiles[t, k + 1]], axis=1)
@@ -67,23 +102,10 @@
             total = term if total is None else total + term
         exact[pl.ds(t * TILE, TILE), :] = total
         forward[pl.ds(t * TILE, TILE), :] = total.astype(BF16)
-    live = count[0, 0]
-    for s in range(filled.shape[0]):
-        filled[s] = 0
-    lane = lax.broadcasted_iota(jnp.int32, own_map.shape, 1)
-    place = jnp.zeros(own_map.shape, jnp.int32)
-    most = 0
     for k in range(kmax):
         row = exact[pl.ds(rows[0, k], 1), :]
         taken[pl.ds(k, 1), :] = row
         picked[pl.ds(k, 1), :] = jnp.where(k < live, row, 0.0)
-        owner = targets[0, k] // strip
-        slot = filled[owner]
-        alive = (k < live).astype(jnp.int32)
-        filled[owner] = slot + alive
-        most = jnp.maximum(most, alive * (slot + 1))
-        place = jnp.where(lane == k, slot, place)
-        slots[0, k] = jnp.where(k < live, owner * SLOTS + jnp.minimum(slot, SLOTS - 1), -1)
     target = own_map[...]
     high = jnp.where(lane < live, target >> SHIFT, DEAD).astype(F32)
     low = (target & (TILE - 1)).astype(F32)
@@ -227,7 +249,11 @@
     same[...] = sums[:kmax]
 
 
-def finish(needed, count, taken, same, base, reach, out, change):
+def finish(needed, count, taken, same, base, reach, out, change, held, in_sems, out_sems):
+    arrivals = chunks(base, held, in_sems)
+    leaves = chunks(held, out, out_sems)
+    for _, copy in arrivals:
+        copy.start()
     kmax = taken.shape[0]
     equal = same[...][:, :kmax]
     k = lax.broadcasted_iota(jnp.int32, equal.shape, 1)
@@ -241,10 +267,15 @@
     high = delta.astype(BF16)
     change[pl.ds(0, kmax), :] = high
     change[pl.ds(kmax, kmax), :] = (delta - high.astype(F32)).astype(BF16)
-    out[...] = base[...] + jnp.dot(reach[...], change[...], preferred_element_type=F32)
-
-
-def slot_finish_kernel(slots, count, got, taken, same, base, reach, out, change, plain, rows):
+    for (at, arrive), (_, leave) in zip(arrivals, leaves, strict=True):
+        arrive.wait()
+        held[at] = held[at] + jnp.dot(reach[at], change[...], preferred_element_type=F32)
+        leave.start()
+    for _, leave in leaves:
+        leave.wait()
+
+
+def slot_finish_kernel(slots, count, got, taken, same, base, reach, out, change, held, in_sems, out_sems, plain, rows):
     kmax = taken.shape[0]
 
     def needed():
@@ -255,17 +286,17 @@
             rows[pl.ds(k, 1), :] = jnp.where(at >= 0, row, 0.0)
         return rows[...]
 
-    finish(needed, count, taken, same, base, reach, out, change)
-
-
-def ring_finish_kernel(count, got, taken, same, base, reach, out, change):
+    finish(needed, count, taken, same, base, reach, out, change, held, in_sems, out_sems)
+
+
+def ring_finish_kernel(count, got, taken, same, base, reach, out, change, held, in_sems, out_sems):
     def needed():
         total = got[0].astype(F32)
         for p in range(1, got.shape[0]):
             total = total + got[p].astype(F32)
         return total
 
-    finish(needed, count, taken, same, base, reach, out, change)
+    finish(needed, count, taken, same, base, reach, out, change, held, in_sems, out_sems)
 
 
 def body(
@@ -296,7 +327,6 @@
     )
     bundle = jnp.concatenate([strips, noted], axis=1)
     near_bundle = lax.ppermute(bundle, "zl", [(0, 1), (1, 0)])
-    near_cols = near_bundle[:, strip, : tile_cols.shape[1]].astype(jnp.int32)
     forward, sent, taken, slots = call(
         functools.partial(forward_kernel, strip=strip),
         (
@@ -305,8 +335,12 @@
             shape((kmax, width), F32),
             shape((1, kmax), jnp.int32),
         ),
-        [SMEM(), SMEM(), SMEM(), SMEM(), VMEM(), VMEM(), VMEM()],
+        [SMEM(), SMEM(), SMEM(), SMEM(), ANY(), ANY(), VMEM()],
         [
+            pltpu.VMEM(shots.shape, F32),
+            pltpu.VMEM(tiles.shape, BF16),
+            pltpu.SemaphoreType.DMA((PIECES,)),
+            pltpu.SemaphoreType.DMA((PIECES,)),
             pltpu.VMEM((leaf_rows, width), BF16),
             pltpu.VMEM((leaf_rows, width), F32),
             pltpu.VMEM((kmax + EXTRA, width), F32),
@@ -315,6 +349,8 @@
         (VMEM(), VMEM(), VMEM(), SMEM()),
     )(cols, rows, own_map, boundary_count, shots, tiles, own_map)
     ring = exchange(sent, "y")
+    ring, near_bundle = lax.optimization_barrier((ring, near_bundle))
+    near_cols = near_bundle[:, strip, : tile_cols.shape[1]].astype(jnp.int32)
     half = width // 2
     sent = call(
         functools.partial(combine_kernel, n_y=n_y, strip=strip),
@@ -349,8 +385,15 @@
         return call(
             kernel,
             shape((leaf_rows, width), F32),
-            lead + [VMEM(), VMEM(), VMEM(), VMEM()],
-            [pltpu.VMEM((2 * kmax, width), BF16)] + scratch,
+            lead + [VMEM(), VMEM(), ANY(), VMEM()],
+            [
+                pltpu.VMEM((2 * kmax, width), BF16),
+                pltpu.VMEM((leaf_rows, width), F32),
+                pltpu.SemaphoreType.DMA((PIECES,)),
+                pltpu.SemaphoreType.DMA((PIECES,)),
+            ]
+            + scratch,
+            ANY(),
         )
 
     def by_slots():

time: 113 us -> 116 us (1.027)
  blocking collectives: 64.3 us -> 47.4 us
  starting transfers between devices: 12.6 us -> 23.5 us
  waiting for transfers between devices: 15.5 us -> 23 us
  Pallas kernels: 16.1 us -> 18.1 us
    all_to_all x3 -> x2, blocking collectives: 64.3 us -> 47.4 us  [exchange(): return lax.all_to_all(value, axes, split_axis=0, concat_axis=0, tiled=True)]
    all_to_all x2 -> x3, starting transfers between devices: 10.1 us -> 20.7 us  [exchange(): return lax.all_to_all(value, axes, split_axis=0, concat_axis=0, tiled=True)]
    all_to_all x2 -> x3, waiting for transfers between devices: 8.98 us -> 15.9 us  [exchange(): return lax.all_to_all(value, axes, split_axis=0, concat_axis=0, tiled=True)]
  transfers between devices with their start and end apart: 3 -> 4, of which waited for: 3 -> 3; matrix products, arithmetic and copies ran while one was open for 1% -> 1% of each run, Pallas kernels for 3% -> 3%
where the time goes in v5:
time: 116 us
  blocking collectives  47.4 us (41%)
  starting transfers between devices  23.5 us (20%)
  waiting for transfers between devices  23 us (20%)
  Pallas kernels  18.1 us (16%)
  between operations  2.02 us (2%)
    all_to_all x2, blocking collectives, exchange(): return lax.all_to_all(value, axes, split_axis=0, concat_axis=0, tiled=True)  47.4 us
    all_to_all x3, starting transfers between devices, exchange(): return lax.all_to_all(value, axes, split_axis=0, concat_axis=0, tiled=True)  20.7 us
    all_to_all x3, waiting for transfers between devices, exchange(): return lax.all_to_all(value, axes, split_axis=0, concat_axis=0, tiled=True)  15.9 us
    ppermute x1, waiting for transfers between devices, body(): near_bundle = lax.ppermute(bundle, 'zl', [(0, 1), (1, 0)])  7.14 us
    pallas_call x1, Pallas kernels, body(): call(functools.partial(forward_kernel, strip=strip), (shape((leaf_rows, w...  4.82 us
    pallas_call x1, Pallas kernels, by_slots(): finished(slot_finish_kernel, [SMEM(), SMEM(), VMEM()], [pltpu.VMEM((n_lea...  4.02 us
    pallas_call x1, Pallas kernels, body(): call(transposed_kernel, (shape((leaf_rows, width), F32), shape((leaf_rows...  3.44 us
    ppermute x1, starting transfers between devices, body(): near_bundle = lax.ppermute(bundle, 'zl', [(0, 1), (1, 0)])  2.71 us
  transfers between devices with their start and end apart: 4, of which 3 were waited for; matrix products, arithmetic and copies ran while one was open for 1% of the time, Pallas kernels for 3%

profile of v5, /device:TPU:8, one launch (start us, length us, event | category | flops | bytes accessed | tf_op | source)
XLA Modules:
  0.0 115.6 jit_solution(12691432371220058057)
XLA Ops:
  1.3 0.0 copy-start.1
  1.3 4.8 %shard_map.104 = (bf16[1536,256]{1,0:T(8,128)(2,1)}, bf16[8,72,256]{2,1,0:T(8,128)(2,1)}, f32[64,256]{1,0:T(8,128)S(1)}, s32[1,64]{1,0:T(1,128)S(1)}) custom-call(s32[4,12]{1,0:T(4,128)} %bitcast.29, s32[1,64]{1,0:T(1,128)} %bitcast.35, s32[1,64]{1,0:T(1,128)} %bitcast.33, s32[1,1]{1,0:T(1,128)S(6)} %copy.17.count, f32[1536,256]{1,0:T(8,128)} %bitcast.23, ...), custom_call_target="tpu_custom_call" | custom-call | tf_op jit(solution)/shard_map/pallas_call | solution.py:330
  6.1 9.1 %all-to-all-start.3 = ((bf16[8,72,256]{2,1,0:T(8,128)(2,1)}), bf16[8,72,256]{2,1,0:T(8,128)(2,1)S(1)}, u32[]{:S(2)}, u32[]{:S(2)}) async-start(bf16[8,72,256]{2,1,0:T(8,128)(2,1)} %get-tuple-element.60), calls=%async_computation.3 | async-start | bytes 589824 | tf_op jit(solution)/shard_map/all_to_all | solution.py:42
  15.3 0.1 copy.13
  15.4 0.0 copy-done
  15.4 0.1 reshape_squeeze.3
  15.5 2.7 %collective-permute-start = (bf16[8,40,512]{2,1,0:T(8,128)(2,1)S(1)}, bf16[8,40,512]{2,1,0:T(8,128)(2,1)S(1)}, u32[]{:S(2)}, u32[]{:S(2)}) collective-permute-start(bf16[8,40,512]{2,1,0:T(8,128)(2,1)S(1)} %fusion.1.strips), channel_id=1, source_target_pairs={{0,64},{64,0},{1,65},{65,1},{2,66},{66,2},{3,67},{67,3},{4,68},{68... | collective-permute-start | bytes 983048 | tf_op jit(solution)/shard_map/ppermute | solution.py:329
  18.2 7.1 %collective-permute-done.near_strips = bf16[8,40,512]{2,1,0:T(8,128)(2,1)S(1)} collective-permute-done((bf16[8,40,512]{2,1,0:T(8,128)(2,1)S(1)}, bf16[8,40,512]{2,1,0:T(8,128)(2,1)S(1)}, u32[]{:S(2)}, u32[]{:S(2)}) %collective-permute-start) | collective-permute-done | bytes 327712 | tf_op jit(solution)/shard_map/ppermute | solution.py:329
  25.4 0.0 all-to-all-done.3.got
  25.4 2.2 %shard_map.105 = bf16[8,288,128]{2,1,0:T(8,128)(2,1)} custom-call(bf16[8,72,256]{2,1,0:T(8,128)(2,1)S(1)} %all-to-all-done.3.got, f32[32,256]{1,0:T(8,128)} %bitcast.27), custom_call_target="tpu_custom_call" | custom-call | tf_op jit(solution)/shard_map/pallas_call | solution.py:355
  27.6 27.2 %all_to_all.35.got.asked = bf16[8,288,128]{2,1,0:T(8,128)(2,1)S(1)} all-to-all(bf16[8,288,128]{2,1,0:T(8,128)(2,1)} %shard_map.105), channel_id=1, replica_groups=mesh['zh'=4,'zl'=2,'y'=8,'sep'=8] {'zh','zl'}, dimensions={0} | all-to-all | bytes 1179648 | tf_op jit(solution)/shard_map/all_to_all | solution.py:42
  54.7 0.9 shard_map.106
  55.6 7.2 %all-to-all-start.5 = ((bf16[8,256,128]{2,1,0:T(8,128)(2,1)}), bf16[8,256,128]{2,1,0:T(8,128)(2,1)S(1)}, u32[]{:S(2)}, u32[]{:S(2)}) async-start(bf16[8,256,128]{2,1,0:T(8,128)(2,1)} %shard_map.106), calls=%async_computation.5 | async-start | bytes 1048576 | tf_op jit(solution)/shard_map/all_to_all | solution.py:42
  62.8 0.7 copy.14
  63.5 11.2 %all-to-all-done.5.residual = bf16[8,256,128]{2,1,0:T(8,128)(2,1)S(1)} async-done(((bf16[8,256,128]{2,1,0:T(8,128)(2,1)}), bf16[8,256,128]{2,1,0:T(8,128)(2,1)S(1)}, u32[]{:S(2)}, u32[]{:S(2)}) %all-to-all-start.5) | async-done | bytes 524320 | tf_op jit(solution)/shard_map/all_to_all | solution.py:42
  74.6 2.1 %shard_map.107 = f32[16,40,128]{2,1,0:T(8,128)} custom-call(s32[4,8]{1,0:T(4,128)} %bitcast.32, s32[4,8]{1,0:T(4,128)} %bitcast.31, bf16[8,40,512]{2,1,0:T(8,128)(2,1)S(1)} %fusion.1.strips, bf16[8,40,512]{2,1,0:T(8,128)(2,1)S(1)} %collective-permute-done.near_strips, bf16[8,256,128]{2,1,0:T(8,128)(2,1)S(1)} %all-to-all-done.5.residual, ...), custom_call_target="tpu_custom_call" | custom-call | tf_op jit(solution)/shard_map/pallas_call | solution.py:371
  76.7 4.4 %all-to-all-start.6 = ((f32[16,40,128]{2,1,0:T(8,128)}), f32[16,40,128]{2,1,0:T(8,128)S(1)}, u32[]{:S(2)}, u32[]{:S(2)}) async-start(f32[16,40,128]{2,1,0:T(8,128)} %shard_map.107), calls=%async_computation.6 | async-start | bytes 655360 | tf_op jit(solution)/shard_map/all_to_all | solution.py:42
  81.1 0.6 pad_add_fusion.row_lanes
  81.7 3.4 %shard_map.109 = (f32[1536,256]{1,0:T(8,128)S(1)}, bf16[1536,128]{1,0:T(8,128)(2,1)S(1)}, f32[64,128]{1,0:T(8,128)S(1)}) custom-call(s32[4,12]{1,0:T(4,128)} %bitcast.30, s32[1,1]{1,0:T(1,128)S(6)} %copy.17.count, bf16[1536,256]{1,0:T(8,128)(2,1)} %get-tuple-element.67.forward, bf16[12,4,128,128]{3,2,1,0:T(8,128)(2,1)} %bitcast.22, ...), custom_call_target="tpu_custom_call" | custom-call | tf_op jit(solution)/shard_map/pallas_call | solution.py:365
  85.2 4.7 %all-to-all-done.6.got = f32[16,40,128]{2,1,0:T(8,128)S(1)} async-done(((f32[16,40,128]{2,1,0:T(8,128)}), f32[16,40,128]{2,1,0:T(8,128)S(1)}, u32[]{:S(2)}, u32[]{:S(2)}) %all-to-all-start.6) | async-done | bytes 327712 | tf_op jit(solution)/shard_map/all_to_all | solution.py:42
  89.8 0.8 shard_map.108
  91.2 24.3 %conditional.1 = (f32[1,1,1536,256]{3,2,1,0:T(8,128)}) conditional(s32[]{:T(128)} %bitcast.15, (bf16[64,8,256]{2,1,0:T(8,128)(2,1)S(1)}, s32[1,64]{1,0:T(1,128)S(1)}, s32[1,1]{1,0:T(1,128)}, f32[64,256]{1,0:T(8,128)S(1)}, f32[64,128]{1,0:T(8,128)S(1)}, /*index=5*/f32[1536,256]{1,0:T(8,128)S(1)}, bf16[1536,128]{1,0:T(8,128)(2,1)S(1)}) %tuple.19, ...), branch_computations={%region_0.1_spmd, %region_1.2_spmd} | conditional | flops 8192 | bytes 983048 | solution.py:420
  91.2 20.3 %all_to_all.32.got = bf16[64,8,256]{2,1,0:T(8,128)(2,1)S(1)} all-to-all(bf16[64,8,256]{2,1,0:T(8,128)(2,1)S(1)} %get-tuple-element.34), channel_id=1, replica_groups=mesh['zh'=4,'zl'=2,'y'=8,'sep'=8] {'zh','zl','y'}, dimensions={0} | all-to-all | bytes 524288 | tf_op jit(solution)/shard_map/cond/branch_0_fun/all_to_all | solution.py:42
  111.5 4.0 %branch_0_fun.1 = f32[1536,256]{1,0:T(8,128)} custom-call(s32[1,64]{1,0:T(1,128)S(1)} %get-tuple-element.32.slots, s32[1,1]{1,0:T(1,128)} %get-tuple-element.33.count, bf16[64,8,256]{2,1,0:T(8,128)(2,1)S(1)} %all_to_all.32.got, f32[64,256]{1,0:T(8,128)S(1)} %get-tuple-element.35.taken, f32[64,128]{1,0:T(8,128)S(1)} %get-tuple-element.36.same, ...), custom_call_target="tpu_custom_call" | custom-call | tf_op jit(solution)/shard_map/cond/branch_0_fun/pallas_call | solution.py:401
  (7 shorter events, 0.0 us)
Async XLA Ops:
  1.3 14.0 %copy-start.1 = (s32[8,1,1,4]{0,3,2,1:T(4,128)S(1)}, s32[8,1,1,4]{0,3,2,1:T(4,128)}, u32[]{:S(2)}) copy-start(s32[8,1,1,4]{0,3,2,1:T(4,128)} %param.19) | copy-start | bytes 388
  1.3 14.1 %copy-start = (bf16[8,32,1,4,128]{4,3,2,1,0:T(4,128)(2,1)S(1)}, bf16[8,32,1,4,128]{4,3,2,1,0:T(4,128)(2,1)}, u32[]{:S(2)}) copy-start(bf16[8,32,1,4,128]{4,3,2,1,0:T(4,128)(2,1)} %param.18) | copy-start | bytes 786436
  6.1 19.2 %all-to-all-start.3 = ((bf16[8,72,256]{2,1,0:T(8,128)(2,1)}), bf16[8,72,256]{2,1,0:T(8,128)(2,1)S(1)}, u32[]{:S(2)}, u32[]{:S(2)}) async-start(bf16[8,72,256]{2,1,0:T(8,128)(2,1)} %get-tuple-element.60), calls=%async_computation.3 | async-start | bytes 589824 | tf_op jit(solution)/shard_map/all_to_all | solution.py:42
  15.5 9.9 %collective-permute-start = (bf16[8,40,512]{2,1,0:T(8,128)(2,1)S(1)}, bf16[8,40,512]{2,1,0:T(8,128)(2,1)S(1)}, u32[]{:S(2)}, u32[]{:S(2)}) collective-permute-start(bf16[8,40,512]{2,1,0:T(8,128)(2,1)S(1)} %fusion.1.strips), channel_id=1, source_target_pairs={{0,64},{64,0},{1,65},{65,1},{2,66},{66,2},{3,67},{67,3},{4,68},{68... | collective-permute-start | bytes 983048 | tf_op jit(solution)/shard_map/ppermute | solution.py:329
  55.6 19.1 %all-to-all-start.5 = ((bf16[8,256,128]{2,1,0:T(8,128)(2,1)}), bf16[8,256,128]{2,1,0:T(8,128)(2,1)S(1)}, u32[]{:S(2)}, u32[]{:S(2)}) async-start(bf16[8,256,128]{2,1,0:T(8,128)(2,1)} %shard_map.106), calls=%async_computation.5 | async-start | bytes 1048576 | tf_op jit(solution)/shard_map/all_to_all | solution.py:42
  62.8 18.3 %copy-start.2 = (s32[1,1,64]{2,1,0:T(1,128)S(1)}, s32[1,1,64]{2,1,0:T(1,128)}, u32[]{:S(2)}) copy-start(s32[1,1,64]{2,1,0:T(1,128)} %param.14) | copy-start | bytes 772
  76.7 13.1 %all-to-all-start.6 = ((f32[16,40,128]{2,1,0:T(8,128)}), f32[16,40,128]{2,1,0:T(8,128)S(1)}, u32[]{:S(2)}, u32[]{:S(2)}) async-start(f32[16,40,128]{2,1,0:T(8,128)} %shard_map.107), calls=%async_computation.6 | async-start | bytes 655360 | tf_op jit(solution)/shard_map/all_to_all | solution.py:42

commit v6 on v4

--- a/solution.py
+++ b/solution.py
@@ -110,7 +110,7 @@
         yield p, info, jnp.where(row_id == target, 1.0, 0.0).astype(BF16)
 
 
-def combine_kernel(got, load, sent, summed, *, n_y, strip):
+def combine_kernel(got, load, cols, sent, summed, notes, *, n_y, strip):
     peers, _, width = got.shape
     n_z, _, half = sent.shape
     n_rows = n_z * strip
@@ -127,8 +127,10 @@
         asked = wanted if asked is None else asked + wanted
         flag = info[3:4, :TILE]
         over = flag if over is None else jnp.maximum(over, flag)
-    lane = lax.broadcasted_iota(jnp.int32, asked.shape, 1)
-    asked = jnp.where(lane < peers * SLOTS, asked, jnp.broadcast_to(over, asked.shape)).astype(BF16)
+    rank = lax.broadcasted_iota(jnp.int32, (strip, TILE), 0).astype(F32) + 1.0
+    lane = lax.broadcasted_iota(jnp.int32, over.shape, 1)
+    notes[...] = jnp.zeros_like(notes)
+    notes[pl.ds(EXTRA // 2, cols.shape[0]), pl.ds(0, cols.shape[1])] = cols[...].astype(F32)
     summed[...] = -total
     z = lax.axis_index("zh") * 2 + lax.axis_index("zl")
     own = pl.ds(pl.multiple_of(z * strip, strip), strip)
@@ -136,7 +138,9 @@
     halves = [summed[:, pl.ds(h * half, half)].astype(BF16) for h in range(2)]
     for p in range(n_z):
         sent[p, pl.ds(0, n_rows), :] = halves[p % 2]
-        sent[p, pl.ds(n_rows, strip), :] = asked[p * strip : (p + 1) * strip]
+        row = jnp.sum(asked[p * strip : (p + 1) * strip] * rank, axis=0, keepdims=True)
+        notes[pl.ds(0, 1), :] = jnp.where(lane < peers * SLOTS, row, over)
+        sent[p, pl.ds(n_rows, EXTRA), :] = notes[...].astype(BF16)
 
 
 def residual_kernel(got, sent):
@@ -195,8 +199,11 @@
     value = own[...].astype(BF16)
     n_z, held, _ = asked.shape
     per = sent.shape[0] // n_z
+    rank = lax.broadcasted_iota(jnp.int32, (strip, TILE), 0).astype(F32) + 1.0
     for p in range(n_z):
-        rows = over_rows(asked[p, pl.ds(held - strip, strip), :], value)[: per * SLOTS]
+        row = asked[p, pl.ds(held - EXTRA, EXTRA), :].astype(F32)[0:1]
+        hot = jnp.where(rank == row, 1.0, 0.0).astype(BF16)
+        rows = over_rows(hot, value)[: per * SLOTS]
         sent[pl.ds(p * per, per)] = rows.astype(BF16).reshape(per, SLOTS, width)
 
 
@@ -244,7 +251,7 @@
     out[...] = base[...] + jnp.dot(reach[...], change[...], preferred_element_type=F32)
 
 
-def slot_finish_kernel(slots, count, got, taken, same, base, reach, out, change, plain, rows):
+def finish_kernel(slots, count, over, got, other, taken, same, base, reach, out, change, plain, rows):
     kmax = taken.shape[0]
 
     def needed():
@@ -253,17 +260,7 @@
             at = slots[0, k]
             row = plain[pl.ds(jnp.maximum(at, 0), 1), :]
             rows[pl.ds(k, 1), :] = jnp.where(at >= 0, row, 0.0)
-        return rows[...]
-
-    finish(needed, count, taken, same, base, reach, out, change)
-
-
-def ring_finish_kernel(count, got, taken, same, base, reach, out, change):
-    def needed():
-        total = got[0].astype(F32)
-        for p in range(1, got.shape[0]):
-            total = total + got[p].astype(F32)
-        return total
+        return jnp.where(over[0, 0] > 0, other[...].astype(F32), rows[...])
 
     finish(needed, count, taken, same, base, reach, out, change)
 
@@ -288,15 +285,9 @@
     kmax = rows.shape[1]
     strip = load.shape[0]
     shape = jax.ShapeDtypeStruct
-    tile_cols = inverse_cols[:, 0, 0]
+    tile_cols = inverse_cols[:, 0, 0].T
     strips = inverse_tiles[:, :, 0].reshape(n_sep, strip, -1)
-    noted = jnp.pad(
-        tile_cols.astype(BF16)[:, None],
-        ((0, 0), (0, EXTRA - 1), (0, strips.shape[2] - tile_cols.shape[1])),
-    )
-    bundle = jnp.concatenate([strips, noted], axis=1)
-    near_bundle = lax.ppermute(bundle, "zl", [(0, 1), (1, 0)])
-    near_cols = near_bundle[:, strip, : tile_cols.shape[1]].astype(jnp.int32)
+    near_strips = lax.ppermute(strips, "zl", [(0, 1), (1, 0)])
     forward, sent, taken, slots = call(
         functools.partial(forward_kernel, strip=strip),
         (
@@ -318,17 +309,25 @@
     half = width // 2
     sent = call(
         functools.partial(combine_kernel, n_y=n_y, strip=strip),
-        shape((n_z, n_z * strip + strip, half), BF16),
-        [VMEM(), VMEM()],
-        [pltpu.VMEM((n_z * strip, width), F32)],
-    )(near(ring), load)
+        shape((n_z, n_z * strip + EXTRA, half), BF16),
+        [VMEM(), VMEM(), VMEM()],
+        [pltpu.VMEM((n_z * strip, width), F32), pltpu.VMEM((EXTRA, half), F32)],
+    )(near(ring), load, tile_cols)
     asked = exchange(sent, z_axes)
+    beside = lax.axis_index("zh") * 2 + 1 - lax.axis_index("zl")
+    near_cols = lax.dynamic_slice(
+        asked, (beside, n_z * strip + EXTRA // 2, 0), (1,) + tile_cols.shape
+    )[0].astype(jnp.int32)
     sent = call(residual_kernel, shape((n_y, n_z * strip, half), BF16), [VMEM()])(near(asked))
     residual = exchange(sent, "y")
     held_rows, _ = lax.optimization_barrier((rows, asked[0, 0, 0]))
     base, reach, same = call(
         transposed_kernel,
-        (shape((leaf_rows, width), F32), shape((leaf_rows, TILE), BF16), shape((kmax, TILE), F32)),
+        (
+            pltpu.VMEM((leaf_rows, width), F32),
+            pltpu.VMEM((leaf_rows, TILE), BF16),
+            shape((kmax, TILE), F32),
+        ),
         [SMEM(), SMEM(), VMEM(), VMEM(), VMEM()],
         [pltpu.VMEM((leaf_rows, width + TILE), F32)],
     )(cols, boundary_count, forward, tiles, jnp.concatenate([held_rows, held_rows], axis=1))
@@ -336,7 +335,7 @@
         separator_kernel,
         shape((2 * n_sep, strip + EXTRA, half), F32),
         [SMEM(), SMEM(), VMEM(), VMEM(), VMEM(), VMEM()],
-    )(tile_cols.T, near_cols.T, near(bundle), near(near_bundle), near(residual), near(asked))
+    )(tile_cols, near_cols, near(strips), near(near_strips), near(residual), near(asked))
     got = exchange(product, ("zl", "sep"))
     own, sent, over = call(
         solution_kernel,
@@ -345,21 +344,8 @@
         out_specs=(VMEM(), VMEM(), SMEM()),
     )(near(got), near(asked))
 
-    def finished(kernel, lead, scratch):
-        return call(
-            kernel,
-            shape((leaf_rows, width), F32),
-            lead + [VMEM(), VMEM(), VMEM(), VMEM()],
-            [pltpu.VMEM((2 * kmax, width), BF16)] + scratch,
-        )
-
     def by_slots():
-        got = exchange(sent, z_axes + ("y",))
-        return finished(
-            slot_finish_kernel,
-            [SMEM(), SMEM(), VMEM()],
-            [pltpu.VMEM((n_leaf * SLOTS, width), F32), pltpu.VMEM((kmax, width), F32)],
-        )(slots, boundary_count, near(got), taken, same, base, reach)
+        return exchange(sent, z_axes + ("y",)), jnp.zeros((kmax, width), BF16)
 
     def by_rings():
         value = jnp.broadcast_to(own.astype(BF16)[None], (n_z, strip, width))
@@ -370,11 +356,19 @@
             [VMEM(), VMEM()],
         )(ring, solved)
         got = exchange(picked, "y")
-        return finished(ring_finish_kernel, [SMEM(), VMEM()], [])(
-            boundary_count, near(got), taken, same, base, reach
-        )
-
-    leaf_solution = lax.cond(over[0, 0] > 0, by_rings, by_slots)
+        return jnp.zeros_like(sent), jnp.sum(got.astype(F32), axis=0).astype(BF16)
+
+    got, other = lax.cond(over[0, 0] > 0, by_rings, by_slots)
+    leaf_solution = call(
+        finish_kernel,
+        shape((leaf_rows, width), F32),
+        [SMEM()] * 3 + [VMEM()] * 6,
+        [
+            pltpu.VMEM((2 * kmax, width), BF16),
+            pltpu.VMEM((n_leaf * SLOTS, width), F32),
+            pltpu.VMEM((kmax, width), F32),
+        ],
+    )(slots, boundary_count, over, near(got), other, taken, same, near(base), near(reach))
     return leaf_solution[None, None], own[None]
 
 

time: 113 us -> 113 us (level)
  waiting for transfers between devices: 15.5 us -> 13.9 us
    ppermute x1, waiting for transfers between devices: 6.49 us -> 5.19 us  [body(): near_strips = lax.ppermute(strips, 'zl', [(0, 1), (1, 0)])]
    unnamed x6 -> x8, local copies, waits for them, and re-layouts: 0.01 us -> 1.16 us
where the time goes in v6:
time: 113 us; the launch traced here: 112 us
  blocking collectives  63.9 us (57%)
  Pallas kernels  17.1 us (15%)
  waiting for transfers between devices  13.9 us (12%)
  starting transfers between devices  12.6 us (11%)
  between operations  2.14 us (2%)
  local copies, waits for them, and re-layouts  1.26 us (1%)
  other arithmetic  1.17 us (1%)
    all_to_all x3, blocking collectives, exchange(): return lax.all_to_all(value, axes, split_axis=0, concat_axis=0, tiled=True)  63.9 us
    all_to_all x2, starting transfers between devices, exchange(): return lax.all_to_all(value, axes, split_axis=0, concat_axis=0, tiled=True)  10.1 us
    all_to_all x2, waiting for transfers between devices, exchange(): return lax.all_to_all(value, axes, split_axis=0, concat_axis=0, tiled=True)  8.67 us
    ppermute x1, waiting for transfers between devices, body(): near_strips = lax.ppermute(strips, 'zl', [(0, 1), (1, 0)])  5.19 us
    pallas_call x1, Pallas kernels, body(): call(functools.partial(forward_kernel, strip=strip), (shape((leaf_rows, w...  3.98 us
    pallas_call x1, Pallas kernels, body(): call(transposed_kernel, (pltpu.VMEM((leaf_rows, width), F32), pltpu.VMEM(...  3.89 us
    pallas_call x1, Pallas kernels, body(): call(finish_kernel, shape((leaf_rows, width), F32), [SMEM()] * 3 + [VMEM(...  3.36 us
    ppermute x1, starting transfers between devices, body(): near_strips = lax.ppermute(strips, 'zl', [(0, 1), (1, 0)])  2.47 us
  transfers between devices with their start and end apart: 3, of which 3 were waited for; matrix products, arithmetic and copies ran while one was open for 1% of the time, Pallas kernels for 3%

profile of v6, /device:TPU:8, one launch (start us, length us, event | category | flops | bytes accessed | tf_op | source)
XLA Modules:
  0.0 112.1 jit_solution(16121128247918084380)
XLA Ops:
  1.3 4.0 %shard_map.104 = (bf16[1536,256]{1,0:T(8,128)(2,1)}, bf16[8,72,256]{2,1,0:T(8,128)(2,1)}, f32[64,256]{1,0:T(8,128)}, s32[1,64]{1,0:T(1,128)}) custom-call(s32[4,12]{1,0:T(4,128)} %bitcast.24, s32[1,64]{1,0:T(1,128)} %bitcast.30, s32[1,64]{1,0:T(1,128)} %bitcast.28, s32[1,1]{1,0:T(1,128)S(6)} %copy.15.count, f32[1536,256]{1,0:T(8,128)} %bitcast.20, ...), custom_call_target="tpu_custom_call" | custom-call | tf_op jit(solution)/shard_map/pallas_call | solution.py:291
  5.3 18.7 %all_to_all.35.got = bf16[8,72,256]{2,1,0:T(8,128)(2,1)S(1)} all-to-all(bf16[8,72,256]{2,1,0:T(8,128)(2,1)} %get-tuple-element.22), channel_id=1, replica_groups=mesh['zh'=4,'zl'=2,'y'=8,'sep'=8] {'y'}, dimensions={0} | all-to-all | bytes 589824 | tf_op jit(solution)/shard_map/all_to_all | solution.py:40
  23.9 2.2 %shard_map.105 = bf16[8,264,128]{2,1,0:T(8,128)(2,1)} custom-call(bf16[8,72,256]{2,1,0:T(8,128)(2,1)S(1)} %all_to_all.35.got, f32[32,256]{1,0:T(8,128)} %bitcast.23, s32[4,8]{1,0:T(4,128)} %bitcast.26), custom_call_target="tpu_custom_call" | custom-call | tf_op jit(solution)/shard_map/pallas_call | solution.py:310
  26.1 25.5 %all_to_all.36.got.asked = bf16[8,264,128]{2,1,0:T(8,128)(2,1)S(1)} all-to-all(bf16[8,264,128]{2,1,0:T(8,128)(2,1)} %shard_map.105), channel_id=1, replica_groups=mesh['zh'=4,'zl'=2,'y'=8,'sep'=8] {'zh','zl'}, dimensions={0} | all-to-all | bytes 1081344 | tf_op jit(solution)/shard_map/all_to_all | solution.py:40
  51.6 0.9 shard_map.106
  52.5 5.7 %all-to-all-start.5 = ((bf16[8,256,128]{2,1,0:T(8,128)(2,1)}), bf16[8,256,128]{2,1,0:T(8,128)(2,1)S(1)}, u32[]{:S(2)}, u32[]{:S(2)}) async-start(bf16[8,256,128]{2,1,0:T(8,128)(2,1)} %shard_map.106), calls=%async_computation.5 | async-start | bytes 1048576 | tf_op jit(solution)/shard_map/all_to_all | solution.py:40
  58.3 0.0 copy-done.2
  58.3 0.1 reshape_squeeze.3.strips
  58.4 2.5 %collective-permute-start = (bf16[8,32,512]{2,1,0:T(8,128)(2,1)S(1)}, bf16[8,32,512]{2,1,0:T(8,128)(2,1)S(1)}, u32[]{:S(2)}, u32[]{:S(2)}) collective-permute-start(bf16[8,32,512]{2,1,0:T(8,128)(2,1)S(1)} %reshape_squeeze.3.strips), channel_id=1, source_target_pairs={{0,64},{64,0},{1,65},{65,1},{2,66},{66,2},{3,67},{67,3},{4,68},{68... | collective-permute-start | bytes 786440 | tf_op jit(solution)/shard_map/ppermute | solution.py:290
  60.9 0.6 bitcast_convert_fusion.near_cols
  61.4 5.2 %collective-permute-done.near_strips = bf16[8,32,512]{2,1,0:T(8,128)(2,1)S(1)} collective-permute-done((bf16[8,32,512]{2,1,0:T(8,128)(2,1)S(1)}, bf16[8,32,512]{2,1,0:T(8,128)(2,1)S(1)}, u32[]{:S(2)}, u32[]{:S(2)}) %collective-permute-start) | collective-permute-done | bytes 262176 | tf_op jit(solution)/shard_map/ppermute | solution.py:290
  66.6 5.6 %all-to-all-done.5.residual = bf16[8,256,128]{2,1,0:T(8,128)(2,1)S(1)} async-done(((bf16[8,256,128]{2,1,0:T(8,128)(2,1)}), bf16[8,256,128]{2,1,0:T(8,128)(2,1)S(1)}, u32[]{:S(2)}, u32[]{:S(2)}) %all-to-all-start.5) | async-done | bytes 524320 | tf_op jit(solution)/shard_map/all_to_all | solution.py:40
  72.2 2.1 %shard_map.107 = f32[16,40,128]{2,1,0:T(8,128)} custom-call(s32[4,8]{1,0:T(4,128)} %bitcast.27, s32[4,8]{1,0:T(4,128)} %bitcast_convert_fusion.near_cols, bf16[8,32,512]{2,1,0:T(8,128)(2,1)S(1)} %reshape_squeeze.3.strips, bf16[8,32,512]{2,1,0:T(8,128)(2,1)S(1)} %collective-permute-done.near_strips, bf16[8,256,128]{2,1,0:T(8,128)(2,1)S(1)} %all-to-all-done.5.residual, ...), custom_call_target="tpu_custom_call" | custom-call | tf_op jit(solution)/shard_map/pallas_call | solution.py:334
  74.3 4.4 %all-to-all-start.6 = ((f32[16,40,128]{2,1,0:T(8,128)}), f32[16,40,128]{2,1,0:T(8,128)S(1)}, u32[]{:S(2)}, u32[]{:S(2)}) async-start(f32[16,40,128]{2,1,0:T(8,128)} %shard_map.107), calls=%async_computation.6 | async-start | bytes 655360 | tf_op jit(solution)/shard_map/all_to_all | solution.py:40
  78.7 0.0 copy-done.3
  78.7 0.6 pad_add_fusion.row_lanes
  79.3 3.9 %shard_map.109 = (f32[1536,256]{1,0:T(8,128)S(1)}, bf16[1536,128]{1,0:T(8,128)(2,1)S(1)}, f32[64,128]{1,0:T(8,128)}) custom-call(s32[4,12]{1,0:T(4,128)} %bitcast.25, s32[1,1]{1,0:T(1,128)S(6)} %copy.15.count, bf16[1536,256]{1,0:T(8,128)(2,1)} %get-tuple-element.29.forward, bf16[12,4,128,128]{3,2,1,0:T(8,128)(2,1)} %bitcast.19, s32[1,128]{1,0:T(1,128)} %pad_add_fusion.row_lanes), custom_call_target="tpu_custom_call" | custom-call | tf_op jit(solution)/shard_map/pallas_call | solution.py:324
  83.2 1.1 %copy-done = f32[1536,256]{1,0:T(8,128)} copy-done((f32[1536,256]{1,0:T(8,128)}, f32[1536,256]{1,0:T(8,128)S(1)}, u32[]{:S(2)}) %copy-start) | copy-done | bytes 1572888
  84.3 3.1 %all-to-all-done.6.got = f32[16,40,128]{2,1,0:T(8,128)S(1)} async-done(((f32[16,40,128]{2,1,0:T(8,128)}), f32[16,40,128]{2,1,0:T(8,128)S(1)}, u32[]{:S(2)}, u32[]{:S(2)}) %all-to-all-start.6) | async-done | bytes 327712 | tf_op jit(solution)/shard_map/all_to_all | solution.py:40
  87.4 0.8 shard_map.108
  88.2 0.0 copy-start.1
  89.0 19.8 %conditional.1 = (bf16[64,8,256]{2,1,0:T(8,128)(2,1)S(1)}, bf16[64,256]{1,0:T(8,128)(2,1)S(1)}) conditional(s32[]{:T(128)} %bitcast.12, bf16[64,8,256]{2,1,0:T(8,128)(2,1)S(1)} %get-tuple-element.24, (f32[32,256]{1,0:T(8,128)}, bf16[8,72,256]{2,1,0:T(8,128)(2,1)S(1)}) %tuple.17), branch_computations={%region_0.0_spmd, %region_1.0_spmd} | conditional | flops 122880 | bytes 1540116 | solution.py:361
  89.0 19.8 %all_to_all.32 = bf16[64,8,256]{2,1,0:T(8,128)(2,1)S(1)} all-to-all(bf16[64,8,256]{2,1,0:T(8,128)(2,1)S(1)} %param), channel_id=1, replica_groups=mesh['zh'=4,'zl'=2,'y'=8,'sep'=8] {'zh','zl','y'}, dimensions={0} | all-to-all | bytes 524288 | tf_op jit(solution)/shard_map/cond/branch_0_fun/all_to_all | solution.py:40
  108.8 3.4 %shard_map.110 = f32[1536,256]{1,0:T(8,128)} custom-call(s32[1,64]{1,0:T(1,128)} %get-tuple-element.21.slots, s32[1,1]{1,0:T(1,128)S(6)} %copy.15.count, s32[1,1]{1,0:T(1,128)} %get-tuple-element.23.over, bf16[64,8,256]{2,1,0:T(8,128)(2,1)S(1)} %get-tuple-element.26.got, bf16[64,256]{1,0:T(8,128)(2,1)S(1)} %get-tuple-element.27.other, ...), custom_call_target="tpu_custom_call" | custom-call | tf_op jit(solution)/shard_map/pallas_call | solution.py:362
  (5 shorter events, 0.0 us)
Async XLA Ops:
  26.1 32.1 %copy-start.2 = (bf16[8,32,1,4,128]{4,3,2,1,0:T(4,128)(2,1)S(1)}, bf16[8,32,1,4,128]{4,3,2,1,0:T(4,128)(2,1)}, u32[]{:S(2)}) copy-start(bf16[8,32,1,4,128]{4,3,2,1,0:T(4,128)(2,1)} %param.18) | copy-start | bytes 786436
  52.5 19.7 %all-to-all-start.5 = ((bf16[8,256,128]{2,1,0:T(8,128)(2,1)}), bf16[8,256,128]{2,1,0:T(8,128)(2,1)S(1)}, u32[]{:S(2)}, u32[]{:S(2)}) async-start(bf16[8,256,128]{2,1,0:T(8,128)(2,1)} %shard_map.106), calls=%async_computation.5 | async-start | bytes 1048576 | tf_op jit(solution)/shard_map/all_to_all | solution.py:40
  58.3 20.4 %copy-start.3 = (s32[1,1,64]{2,1,0:T(1,128)S(1)}, s32[1,1,64]{2,1,0:T(1,128)}, u32[]{:S(2)}) copy-start(s32[1,1,64]{2,1,0:T(1,128)} %param.14) | copy-start | bytes 772
  58.4 8.3 %collective-permute-start = (bf16[8,32,512]{2,1,0:T(8,128)(2,1)S(1)}, bf16[8,32,512]{2,1,0:T(8,128)(2,1)S(1)}, u32[]{:S(2)}, u32[]{:S(2)}) collective-permute-start(bf16[8,32,512]{2,1,0:T(8,128)(2,1)S(1)} %reshape_squeeze.3.strips), channel_id=1, source_target_pairs={{0,64},{64,0},{1,65},{65,1},{2,66},{66,2},{3,67},{67,3},{4,68},{68... | collective-permute-start | bytes 786440 | tf_op jit(solution)/shard_map/ppermute | solution.py:290
  74.3 13.1 %all-to-all-start.6 = ((f32[16,40,128]{2,1,0:T(8,128)}), f32[16,40,128]{2,1,0:T(8,128)S(1)}, u32[]{:S(2)}, u32[]{:S(2)}) async-start(f32[16,40,128]{2,1,0:T(8,128)} %shard_map.107), calls=%async_computation.6 | async-start | bytes 655360 | tf_op jit(solution)/shard_map/all_to_all | solution.py:40
  83.2 1.1 %copy-start = (f32[1536,256]{1,0:T(8,128)}, f32[1536,256]{1,0:T(8,128)S(1)}, u32[]{:S(2)}) copy-start(f32[1536,256]{1,0:T(8,128)S(1)} %get-tuple-element.31.base) | copy-start | bytes 4718596
  88.2 20.6 %copy-start.1 = (f32[1536,256]{1,0:T(8,128)S(1)}, f32[1536,256]{1,0:T(8,128)}, u32[]{:S(2)}) copy-start(f32[1536,256]{1,0:T(8,128)} %copy-done) | copy-start | bytes 4718596

commit v7 on v6

--- a/solution.py
+++ b/solution.py
@@ -83,8 +83,8 @@
         filled[owner] = slot + alive
         most = jnp.maximum(most, alive * (slot + 1))
         place = jnp.where(lane == k, slot, place)
-        slots[0, k] = jnp.where(k < live, owner * SLOTS + jnp.minimum(slot, SLOTS - 1), -1)
     target = own_map[...]
+    slots[...] = jnp.where(lane < live, (target // strip) * SLOTS + jnp.minimum(place, SLOTS - 1), -1)
     high = jnp.where(lane < live, target >> SHIFT, DEAD).astype(F32)
     low = (target & (TILE - 1)).astype(F32)
     picked[pl.ds(kmax, EXTRA), :] = jnp.zeros((EXTRA, width), F32)
@@ -251,16 +251,13 @@
     out[...] = base[...] + jnp.dot(reach[...], change[...], preferred_element_type=F32)
 
 
-def finish_kernel(slots, count, over, got, other, taken, same, base, reach, out, change, plain, rows):
-    kmax = taken.shape[0]
-
+def finish_kernel(count, over, slots, got, other, taken, same, base, reach, out, change):
     def needed():
-        plain[...] = got[...].reshape(plain.shape).astype(F32)
-        for k in range(kmax):
-            at = slots[0, k]
-            row = plain[pl.ds(jnp.maximum(at, 0), 1), :]
-            rows[pl.ds(k, 1), :] = jnp.where(at >= 0, row, 0.0)
-        return jnp.where(over[0, 0] > 0, other[...].astype(F32), rows[...])
+        n_leaf, per, width = got.shape
+        rows = got[...].reshape(n_leaf * per, width)
+        at = lax.broadcasted_iota(jnp.int32, (n_leaf * per, slots.shape[1]), 0)
+        hot = jnp.where(at == slots[...], 1.0, 0.0).astype(BF16)
+        return jnp.where(over[0, 0] > 0, other[...].astype(F32), over_rows(hot, rows))
 
     finish(needed, count, taken, same, base, reach, out, change)
 
@@ -303,7 +300,6 @@
             pltpu.VMEM((kmax + EXTRA, width), F32),
             pltpu.SMEM((n_leaf,), jnp.int32),
         ],
-        (VMEM(), VMEM(), VMEM(), SMEM()),
     )(cols, rows, own_map, boundary_count, shots, tiles, own_map)
     ring = exchange(sent, "y")
     half = width // 2
@@ -312,7 +308,7 @@
         shape((n_z, n_z * strip + EXTRA, half), BF16),
         [VMEM(), VMEM(), VMEM()],
         [pltpu.VMEM((n_z * strip, width), F32), pltpu.VMEM((EXTRA, half), F32)],
-    )(near(ring), load, tile_cols)
+    )(near(ring), near(load), near(tile_cols))
     asked = exchange(sent, z_axes)
     beside = lax.axis_index("zh") * 2 + 1 - lax.axis_index("zl")
     near_cols = lax.dynamic_slice(
@@ -362,13 +358,19 @@
     leaf_solution = call(
         finish_kernel,
         shape((leaf_rows, width), F32),
-        [SMEM()] * 3 + [VMEM()] * 6,
-        [
-            pltpu.VMEM((2 * kmax, width), BF16),
-            pltpu.VMEM((n_leaf * SLOTS, width), F32),
-            pltpu.VMEM((kmax, width), F32),
-        ],
-    )(slots, boundary_count, over, near(got), other, taken, same, near(base), near(reach))
+        [SMEM()] * 2 + [VMEM()] * 7,
+        [pltpu.VMEM((2 * kmax, width), BF16)],
+    )(
+        boundary_count,
+        over,
+        near(slots),
+        near(got),
+        near(other),
+        near(taken),
+        near(same),
+        near(base),
+        near(reach),
+    )
     return leaf_solution[None, None], own[None]
 
 

time: 113 us -> 111 us (0.982)
  Pallas kernels: 17.1 us -> 15.4 us
  transfers between devices with their start and end apart: 3 -> 3, of which waited for: 3 -> 3; matrix products, arithmetic and copies ran while one was open for 1% -> 1% of each run, Pallas kernels for 3% -> 4%
where the time goes in v7:
time: 111 us; the launch traced here: 110 us
  blocking collectives  63.9 us (58%)
  Pallas kernels  15.4 us (14%)
  waiting for transfers between devices  13.8 us (12%)
  starting transfers between devices  12.6 us (11%)
  between operations  2.1 us (2%)
  local copies, waits for them, and re-layouts  1.29 us (1%)
  other arithmetic  1.17 us (1%)
    all_to_all x3, blocking collectives, exchange(): return lax.all_to_all(value, axes, split_axis=0, concat_axis=0, tiled=True)  63.9 us
    all_to_all x2, starting transfers between devices, exchange(): return lax.all_to_all(value, axes, split_axis=0, concat_axis=0, tiled=True)  10.2 us
    all_to_all x2, waiting for transfers between devices, exchange(): return lax.all_to_all(value, axes, split_axis=0, concat_axis=0, tiled=True)  8.64 us
    ppermute x1, waiting for transfers between devices, body(): near_strips = lax.ppermute(strips, 'zl', [(0, 1), (1, 0)])  5.19 us
    pallas_call x1, Pallas kernels, body(): call(functools.partial(forward_kernel, strip=strip), (shape((leaf_rows, w...  3.96 us
    pallas_call x1, Pallas kernels, body(): call(transposed_kernel, (pltpu.VMEM((leaf_rows, width), F32), pltpu.VMEM(...  3.89 us
    ppermute x1, starting transfers between devices, body(): near_strips = lax.ppermute(strips, 'zl', [(0, 1), (1, 0)])  2.47 us
    pallas_call x1, Pallas kernels, body(): call(finish_kernel, shape((leaf_rows, width), F32), [SMEM()] * 2 + [VMEM(...  2.45 us
  transfers between devices with their start and end apart: 3, of which 3 were waited for; matrix products, arithmetic and copies ran while one was open for 1% of the time, Pallas kernels for 4%

profile of v7, /device:TPU:8, one launch (start us, length us, event | category | flops | bytes accessed | tf_op | source)
XLA Modules:
  0.0 110.4 jit_solution(7164799501147621974)
XLA Ops:
  1.3 0.0 copy-start.5
  1.3 4.0 %shard_map.104 = (bf16[1536,256]{1,0:T(8,128)(2,1)}, bf16[8,72,256]{2,1,0:T(8,128)(2,1)}, f32[64,256]{1,0:T(8,128)}, s32[1,64]{1,0:T(1,128)}) custom-call(s32[4,12]{1,0:T(4,128)} %bitcast.26, s32[1,64]{1,0:T(1,128)} %bitcast.30, s32[1,64]{1,0:T(1,128)} %bitcast.28, s32[1,1]{1,0:T(1,128)S(6)} %copy.15.count, f32[1536,256]{1,0:T(8,128)} %bitcast.23, ...), custom_call_target="tpu_custom_call" | custom-call | tf_op jit(solution)/shard_map/pallas_call | solution.py:288
  5.3 18.7 %all_to_all.35.got = bf16[8,72,256]{2,1,0:T(8,128)(2,1)S(1)} all-to-all(bf16[8,72,256]{2,1,0:T(8,128)(2,1)} %get-tuple-element.21), channel_id=1, replica_groups=mesh['zh'=4,'zl'=2,'y'=8,'sep'=8] {'y'}, dimensions={0} | all-to-all | bytes 589824 | tf_op jit(solution)/shard_map/all_to_all | solution.py:40
  23.9 1.4 %shard_map.105 = bf16[8,264,128]{2,1,0:T(8,128)(2,1)} custom-call(bf16[8,72,256]{2,1,0:T(8,128)(2,1)S(1)} %all_to_all.35.got, f32[32,256]{1,0:T(8,128)S(1)} %bitcast.18, s32[4,8]{1,0:T(4,128)S(1)} %bitcast.20), custom_call_target="tpu_custom_call" | custom-call | tf_op jit(solution)/shard_map/pallas_call | solution.py:306
  25.3 25.5 %all_to_all.36.got.asked = bf16[8,264,128]{2,1,0:T(8,128)(2,1)S(1)} all-to-all(bf16[8,264,128]{2,1,0:T(8,128)(2,1)} %shard_map.105), channel_id=1, replica_groups=mesh['zh'=4,'zl'=2,'y'=8,'sep'=8] {'zh','zl'}, dimensions={0} | all-to-all | bytes 1081344 | tf_op jit(solution)/shard_map/all_to_all | solution.py:40
  50.9 0.9 shard_map.106
  51.7 5.8 %all-to-all-start.5 = ((bf16[8,256,128]{2,1,0:T(8,128)(2,1)}), bf16[8,256,128]{2,1,0:T(8,128)(2,1)S(1)}, u32[]{:S(2)}, u32[]{:S(2)}) async-start(bf16[8,256,128]{2,1,0:T(8,128)(2,1)} %shard_map.106), calls=%async_computation.5 | async-start | bytes 1048576 | tf_op jit(solution)/shard_map/all_to_all | solution.py:40
  57.5 0.0 copy-done.7
  57.5 0.1 reshape_squeeze.3.strips
  57.6 2.5 %collective-permute-start = (bf16[8,32,512]{2,1,0:T(8,128)(2,1)S(1)}, bf16[8,32,512]{2,1,0:T(8,128)(2,1)S(1)}, u32[]{:S(2)}, u32[]{:S(2)}) collective-permute-start(bf16[8,32,512]{2,1,0:T(8,128)(2,1)S(1)} %reshape_squeeze.3.strips), channel_id=1, source_target_pairs={{0,64},{64,0},{1,65},{65,1},{2,66},{66,2},{3,67},{67,3},{4,68},{68... | collective-permute-start | bytes 786440 | tf_op jit(solution)/shard_map/ppermute | solution.py:287
  60.1 0.6 bitcast_convert_fusion.near_cols
  60.7 5.2 %collective-permute-done.near_strips = bf16[8,32,512]{2,1,0:T(8,128)(2,1)S(1)} collective-permute-done((bf16[8,32,512]{2,1,0:T(8,128)(2,1)S(1)}, bf16[8,32,512]{2,1,0:T(8,128)(2,1)S(1)}, u32[]{:S(2)}, u32[]{:S(2)}) %collective-permute-start) | collective-permute-done | bytes 262176 | tf_op jit(solution)/shard_map/ppermute | solution.py:287
  65.9 5.6 %all-to-all-done.5.residual = bf16[8,256,128]{2,1,0:T(8,128)(2,1)S(1)} async-done(((bf16[8,256,128]{2,1,0:T(8,128)(2,1)}), bf16[8,256,128]{2,1,0:T(8,128)(2,1)S(1)}, u32[]{:S(2)}, u32[]{:S(2)}) %all-to-all-start.5) | async-done | bytes 524320 | tf_op jit(solution)/shard_map/all_to_all | solution.py:40
  71.4 2.1 %shard_map.107 = f32[16,40,128]{2,1,0:T(8,128)} custom-call(s32[4,8]{1,0:T(4,128)} %bitcast.19, s32[4,8]{1,0:T(4,128)} %bitcast_convert_fusion.near_cols, bf16[8,32,512]{2,1,0:T(8,128)(2,1)S(1)} %reshape_squeeze.3.strips, bf16[8,32,512]{2,1,0:T(8,128)(2,1)S(1)} %collective-permute-done.near_strips, bf16[8,256,128]{2,1,0:T(8,128)(2,1)S(1)} %all-to-all-done.5.residual, ...), custom_call_target="tpu_custom_call" | custom-call | tf_op jit(solution)/shard_map/pallas_call | solution.py:330
  73.5 4.4 %all-to-all-start.6 = ((f32[16,40,128]{2,1,0:T(8,128)}), f32[16,40,128]{2,1,0:T(8,128)S(1)}, u32[]{:S(2)}, u32[]{:S(2)}) async-start(f32[16,40,128]{2,1,0:T(8,128)} %shard_map.107), calls=%async_computation.6 | async-start | bytes 655360 | tf_op jit(solution)/shard_map/all_to_all | solution.py:40
  77.9 0.6 pad_add_fusion.row_lanes
  78.5 3.9 %shard_map.109 = (f32[1536,256]{1,0:T(8,128)S(1)}, bf16[1536,128]{1,0:T(8,128)(2,1)S(1)}, f32[64,128]{1,0:T(8,128)}) custom-call(s32[4,12]{1,0:T(4,128)} %bitcast.27, s32[1,1]{1,0:T(1,128)S(6)} %copy.15.count, bf16[1536,256]{1,0:T(8,128)(2,1)} %get-tuple-element.29.forward, bf16[12,4,128,128]{3,2,1,0:T(8,128)(2,1)} %bitcast.22, s32[1,128]{1,0:T(1,128)} %pad_add_fusion.row_lanes), custom_call_target="tpu_custom_call" | custom-call | tf_op jit(solution)/shard_map/pallas_call | solution.py:320
  82.4 1.1 %copy-done = f32[1536,256]{1,0:T(8,128)} copy-done((f32[1536,256]{1,0:T(8,128)}, f32[1536,256]{1,0:T(8,128)S(1)}, u32[]{:S(2)}) %copy-start) | copy-done | bytes 1572888
  83.5 3.1 %all-to-all-done.6.got = f32[16,40,128]{2,1,0:T(8,128)S(1)} async-done(((f32[16,40,128]{2,1,0:T(8,128)}), f32[16,40,128]{2,1,0:T(8,128)S(1)}, u32[]{:S(2)}, u32[]{:S(2)}) %all-to-all-start.6) | async-done | bytes 327712 | tf_op jit(solution)/shard_map/all_to_all | solution.py:40
  86.6 0.8 shard_map.108
  87.4 0.0 copy-start.1
  88.1 19.8 %conditional.1 = (bf16[64,8,256]{2,1,0:T(8,128)(2,1)S(1)}, bf16[64,256]{1,0:T(8,128)(2,1)S(1)}) conditional(s32[]{:T(128)} %bitcast.12, bf16[64,8,256]{2,1,0:T(8,128)(2,1)S(1)} %get-tuple-element.24, (f32[32,256]{1,0:T(8,128)}, bf16[8,72,256]{2,1,0:T(8,128)(2,1)S(1)}) %tuple.17), branch_computations={%region_0.0_spmd, %region_1.0_spmd} | conditional | flops 122880 | bytes 1540116 | solution.py:357
  88.1 19.8 %all_to_all.32 = bf16[64,8,256]{2,1,0:T(8,128)(2,1)S(1)} all-to-all(bf16[64,8,256]{2,1,0:T(8,128)(2,1)S(1)} %param), channel_id=1, replica_groups=mesh['zh'=4,'zl'=2,'y'=8,'sep'=8] {'zh','zl','y'}, dimensions={0} | all-to-all | bytes 524288 | tf_op jit(solution)/shard_map/cond/branch_0_fun/all_to_all | solution.py:40
  107.9 2.5 %shard_map.110 = f32[1536,256]{1,0:T(8,128)} custom-call(s32[1,1]{1,0:T(1,128)S(6)} %copy.15.count, s32[1,1]{1,0:T(1,128)} %get-tuple-element.22.over, s32[1,64]{1,0:T(1,128)S(1)} %copy-done.6, bf16[64,8,256]{2,1,0:T(8,128)(2,1)S(1)} %get-tuple-element.26.got, bf16[64,256]{1,0:T(8,128)(2,1)S(1)} %get-tuple-element.27.other, f32[64,256]{1,0:T(8,128)S(1)} %copy-done.2, ...), custom_call_target="tpu_custom_call" | custom-call | tf_op jit(solution)/shard_map/pallas_call | solution.py:358
  (15 shorter events, 0.0 us)
Async XLA Ops:
  1.3 22.6 %copy-start.4 = (f32[1,32,256]{2,1,0:T(8,128)S(1)}, f32[1,32,256]{2,1,0:T(8,128)}, u32[]{:S(2)}) copy-start(f32[1,32,256]{2,1,0:T(8,128)} %param.17) | copy-start | bytes 98308
  1.3 22.6 %copy-start.5 = (s32[8,1,1,4]{0,3,2,1:T(4,128)S(1)}, s32[8,1,1,4]{0,3,2,1:T(4,128)}, u32[]{:S(2)}) copy-start(s32[8,1,1,4]{0,3,2,1:T(4,128)} %param.19) | copy-start | bytes 388
  25.3 32.1 %copy-start.7 = (bf16[8,32,1,4,128]{4,3,2,1,0:T(4,128)(2,1)S(1)}, bf16[8,32,1,4,128]{4,3,2,1,0:T(4,128)(2,1)}, u32[]{:S(2)}) copy-start(bf16[8,32,1,4,128]{4,3,2,1,0:T(4,128)(2,1)} %param.18) | copy-start | bytes 786436
  51.7 19.7 %all-to-all-start.5 = ((bf16[8,256,128]{2,1,0:T(8,128)(2,1)}), bf16[8,256,128]{2,1,0:T(8,128)(2,1)S(1)}, u32[]{:S(2)}, u32[]{:S(2)}) async-start(bf16[8,256,128]{2,1,0:T(8,128)(2,1)} %shard_map.106), calls=%async_computation.5 | async-start | bytes 1048576 | tf_op jit(solution)/shard_map/all_to_all | solution.py:40
  57.5 20.4 %copy-start.8 = (s32[1,1,64]{2,1,0:T(1,128)S(1)}, s32[1,1,64]{2,1,0:T(1,128)}, u32[]{:S(2)}) copy-start(s32[1,1,64]{2,1,0:T(1,128)} %param.14) | copy-start | bytes 772
  57.6 8.3 %collective-permute-start = (bf16[8,32,512]{2,1,0:T(8,128)(2,1)S(1)}, bf16[8,32,512]{2,1,0:T(8,128)(2,1)S(1)}, u32[]{:S(2)}, u32[]{:S(2)}) collective-permute-start(bf16[8,32,512]{2,1,0:T(8,128)(2,1)S(1)} %reshape_squeeze.3.strips), channel_id=1, source_target_pairs={{0,64},{64,0},{1,65},{65,1},{2,66},{66,2},{3,67},{67,3},{4,68},{68... | collective-permute-start | bytes 786440 | tf_op jit(solution)/shard_map/ppermute | solution.py:287
  73.5 13.1 %all-to-all-start.6 = ((f32[16,40,128]{2,1,0:T(8,128)}), f32[16,40,128]{2,1,0:T(8,128)S(1)}, u32[]{:S(2)}, u32[]{:S(2)}) async-start(f32[16,40,128]{2,1,0:T(8,128)} %shard_map.107), calls=%async_computation.6 | async-start | bytes 655360 | tf_op jit(solution)/shard_map/all_to_all | solution.py:40
  82.4 1.1 %copy-start = (f32[1536,256]{1,0:T(8,128)}, f32[1536,256]{1,0:T(8,128)S(1)}, u32[]{:S(2)}) copy-start(f32[1536,256]{1,0:T(8,128)S(1)} %get-tuple-element.31.base) | copy-start | bytes 4718596
  87.4 20.5 %copy-start.1 = (f32[1536,256]{1,0:T(8,128)S(1)}, f32[1536,256]{1,0:T(8,128)}, u32[]{:S(2)}) copy-start(f32[1536,256]{1,0:T(8,128)} %copy-done) | copy-start | bytes 4718596
  87.4 20.5 %copy-start.2 = (f32[64,256]{1,0:T(8,128)S(1)}, f32[64,256]{1,0:T(8,128)}, u32[]{:S(2)}) copy-start(f32[64,256]{1,0:T(8,128)} %get-tuple-element.28.taken) | copy-start | bytes 196612
  87.4 20.5 %copy-start.3 = (f32[64,128]{1,0:T(8,128)S(1)}, f32[64,128]{1,0:T(8,128)}, u32[]{:S(2)}) copy-start(f32[64,128]{1,0:T(8,128)} %get-tuple-element.30.same) | copy-start | bytes 98308
  87.4 20.5 %copy-start.6 = (s32[1,64]{1,0:T(1,128)S(1)}, s32[1,64]{1,0:T(1,128)}, u32[]{:S(2)}) copy-start(s32[1,64]{1,0:T(1,128)} %get-tuple-element.23.slots) | copy-start | bytes 772

commit v8 on v7

--- a/solution.py
+++ b/solution.py
@@ -160,6 +160,8 @@
     per_tile = TILE // strip
     zl = lax.axis_index("zl")
 
+    own_cols, other_cols = cols[...], near_cols[...]
+
     def tile(c):
         parts = n_y // per_tile
         y = (c % parts) * per_tile
@@ -169,7 +171,7 @@
     over = got[0, pl.ds(n_rows, EXTRA), :].astype(F32)
     for p in range(1, got.shape[0]):
         over = jnp.maximum(over, got[p, pl.ds(n_rows, EXTRA), :].astype(F32))
-    for which, wanted, rows in ((zl, cols, strips), (1 - zl, near_cols, near_strips)):
+    for which, wanted, rows in ((zl, own_cols, strips), (1 - zl, other_cols, near_strips)):
         for q in range(sections):
             total = None
             for k in range(0, per_row, 2):
@@ -310,13 +312,7 @@
         [pltpu.VMEM((n_z * strip, width), F32), pltpu.VMEM((EXTRA, half), F32)],
     )(near(ring), near(load), near(tile_cols))
     asked = exchange(sent, z_axes)
-    beside = lax.axis_index("zh") * 2 + 1 - lax.axis_index("zl")
-    near_cols = lax.dynamic_slice(
-        asked, (beside, n_z * strip + EXTRA // 2, 0), (1,) + tile_cols.shape
-    )[0].astype(jnp.int32)
-    sent = call(residual_kernel, shape((n_y, n_z * strip, half), BF16), [VMEM()])(near(asked))
-    residual = exchange(sent, "y")
-    held_rows, _ = lax.optimization_barrier((rows, asked[0, 0, 0]))
+    held_rows, _ = lax.optimization_barrier((rows, ring[0, 0, :TILE]))
     base, reach, same = call(
         transposed_kernel,
         (
@@ -327,11 +323,18 @@
         [SMEM(), SMEM(), VMEM(), VMEM(), VMEM()],
         [pltpu.VMEM((leaf_rows, width + TILE), F32)],
     )(cols, boundary_count, forward, tiles, jnp.concatenate([held_rows, held_rows], axis=1))
+    asked, same = lax.optimization_barrier((asked, same))
+    beside = lax.axis_index("zh") * 2 + 1 - lax.axis_index("zl")
+    near_cols = lax.dynamic_slice(
+        asked, (beside, n_z * strip + EXTRA // 2, 0), (1,) + tile_cols.shape
+    )[0].astype(jnp.int32)
+    sent = call(residual_kernel, shape((n_y, n_z * strip, half), BF16), [VMEM()])(near(asked))
+    residual = exchange(sent, "y")
     product = call(
         separator_kernel,
         shape((2 * n_sep, strip + EXTRA, half), F32),
-        [SMEM(), SMEM(), VMEM(), VMEM(), VMEM(), VMEM()],
-    )(tile_cols, near_cols, near(strips), near(near_strips), near(residual), near(asked))
+        [VMEM()] * 6,
+    )(near(tile_cols), near(near_cols), near(strips), near(near_strips), near(residual), near(asked))
     got = exchange(product, ("zl", "sep"))
     own, sent, over = call(
         solution_kernel,

time: 111 us -> 112 us (level)
  blocking collectives: 63.9 us -> 50.8 us
  waiting for transfers between devices: 13.8 us -> 22.9 us
  starting transfers between devices: 12.6 us -> 18.5 us
    all_to_all x3, blocking collectives: 63.9 us -> 50.8 us  [exchange(): return lax.all_to_all(value, axes, split_axis=0, concat_axis=0, tiled=True)]
    all_to_all x2, waiting for transfers between devices: 8.64 us -> 16 us  [exchange(): return lax.all_to_all(value, axes, split_axis=0, concat_axis=0, tiled=True)]
    all_to_all x2, starting transfers between devices: 10.2 us -> 16.1 us  [exchange(): return lax.all_to_all(value, axes, split_axis=0, concat_axis=0, tiled=True)]
    ppermute x1, waiting for transfers between devices: 5.19 us -> 6.91 us  [body(): near_strips = lax.ppermute(strips, 'zl', [(0, 1), (1, 0)])]
where the time goes in v8:
time: 112 us; the launch traced here: 111 us
  blocking collectives  50.8 us (45%)
  waiting for transfers between devices  22.9 us (20%)
  starting transfers between devices  18.5 us (17%)
  Pallas kernels  14.8 us (13%)
  between operations  2.13 us (2%)
  local copies, waits for them, and re-layouts  1.29 us (1%)
    all_to_all x3, blocking collectives, exchange(): return lax.all_to_all(value, axes, split_axis=0, concat_axis=0, tiled=True)  50.8 us
    all_to_all x2, starting transfers between devices, exchange(): return lax.all_to_all(value, axes, split_axis=0, concat_axis=0, tiled=True)  16.1 us
    all_to_all x2, waiting for transfers between devices, exchange(): return lax.all_to_all(value, axes, split_axis=0, concat_axis=0, tiled=True)  16 us
    ppermute x1, waiting for transfers between devices, body(): near_strips = lax.ppermute(strips, 'zl', [(0, 1), (1, 0)])  6.91 us
    pallas_call x1, Pallas kernels, body(): call(functools.partial(forward_kernel, strip=strip), (shape((leaf_rows, w...  3.95 us
    pallas_call x1, Pallas kernels, body(): call(transposed_kernel, (pltpu.VMEM((leaf_rows, width), F32), pltpu.VMEM(...  3.89 us
    pallas_call x1, Pallas kernels, body(): call(finish_kernel, shape((leaf_rows, width), F32), [SMEM()] * 2 + [VMEM(...  2.5 us
    ppermute x1, starting transfers between devices, body(): near_strips = lax.ppermute(strips, 'zl', [(0, 1), (1, 0)])  2.47 us
  transfers between devices with their start and end apart: 3, of which 3 were waited for; matrix products, arithmetic and copies ran while one was open for 1% of the time, Pallas kernels for 4%

profile of v8, /device:TPU:8, one launch (start us, length us, event | category | flops | bytes accessed | tf_op | source)
XLA Modules:
  0.0 111.1 jit_solution(12534397613758146902)
XLA Ops:
  1.3 4.0 %shard_map.104 = (bf16[1536,256]{1,0:T(8,128)(2,1)}, bf16[8,72,256]{2,1,0:T(8,128)(2,1)}, f32[64,256]{1,0:T(8,128)}, s32[1,64]{1,0:T(1,128)}) custom-call(s32[4,12]{1,0:T(4,128)} %bitcast.26, s32[1,64]{1,0:T(1,128)} %bitcast.30, s32[1,64]{1,0:T(1,128)} %bitcast.28, s32[1,1]{1,0:T(1,128)S(6)} %copy.15.count, f32[1536,256]{1,0:T(8,128)} %bitcast.23, ...), custom_call_target="tpu_custom_call" | custom-call | tf_op jit(solution)/shard_map/pallas_call | solution.py:290
  5.2 18.8 %all_to_all.35.got = bf16[8,72,256]{2,1,0:T(8,128)(2,1)S(1)} all-to-all(bf16[8,72,256]{2,1,0:T(8,128)(2,1)} %get-tuple-element.23), channel_id=1, replica_groups=mesh['zh'=4,'zl'=2,'y'=8,'sep'=8] {'y'}, dimensions={0} | all-to-all | bytes 589824 | tf_op jit(solution)/shard_map/all_to_all | solution.py:40
  24.0 0.0 copy-done.4
  24.1 1.4 %shard_map.105 = bf16[8,264,128]{2,1,0:T(8,128)(2,1)} custom-call(bf16[8,72,256]{2,1,0:T(8,128)(2,1)S(1)} %all_to_all.35.got, f32[32,256]{1,0:T(8,128)S(1)} %bitcast.18, s32[4,8]{1,0:T(4,128)S(1)} %bitcast.19), custom_call_target="tpu_custom_call" | custom-call | tf_op jit(solution)/shard_map/pallas_call | solution.py:308
  25.5 10.3 %all-to-all-start.4 = ((bf16[8,264,128]{2,1,0:T(8,128)(2,1)}), bf16[8,264,128]{2,1,0:T(8,128)(2,1)S(1)}, u32[]{:S(2)}, u32[]{:S(2)}) async-start(bf16[8,264,128]{2,1,0:T(8,128)(2,1)} %shard_map.105), calls=%async_computation.4 | async-start | bytes 1081344 | tf_op jit(solution)/shard_map/all_to_all | solution.py:40
  35.8 0.6 pad_add_fusion.row_lanes
  36.4 3.9 %shard_map.106 = (f32[1536,256]{1,0:T(8,128)S(1)}, bf16[1536,128]{1,0:T(8,128)(2,1)S(1)}, f32[64,128]{1,0:T(8,128)}) custom-call(s32[4,12]{1,0:T(4,128)} %bitcast.27, s32[1,1]{1,0:T(1,128)S(6)} %copy.15.count, bf16[1536,256]{1,0:T(8,128)(2,1)} %get-tuple-element.24.forward, bf16[12,4,128,128]{3,2,1,0:T(8,128)(2,1)} %bitcast.22, s32[1,128]{1,0:T(1,128)} %pad_add_fusion.row_lanes), custom_call_target="tpu_custom_call" | custom-call | tf_op jit(solution)/shard_map/pallas_call | solution.py:316
  40.3 1.1 %copy-done = f32[1536,256]{1,0:T(8,128)} copy-done((f32[1536,256]{1,0:T(8,128)}, f32[1536,256]{1,0:T(8,128)S(1)}, u32[]{:S(2)}) %copy-start) | copy-done | bytes 1572888
  41.4 9.4 %all-to-all-done.4.got.asked = bf16[8,264,128]{2,1,0:T(8,128)(2,1)S(1)} async-done(((bf16[8,264,128]{2,1,0:T(8,128)(2,1)}), bf16[8,264,128]{2,1,0:T(8,128)(2,1)S(1)}, u32[]{:S(2)}, u32[]{:S(2)}) %all-to-all-start.4) | async-done | bytes 540704 | tf_op jit(solution)/shard_map/all_to_all | solution.py:40
  50.9 0.9 shard_map.107
  51.7 5.7 %all-to-all-start.5 = ((bf16[8,256,128]{2,1,0:T(8,128)(2,1)}), bf16[8,256,128]{2,1,0:T(8,128)(2,1)S(1)}, u32[]{:S(2)}, u32[]{:S(2)}) async-start(bf16[8,256,128]{2,1,0:T(8,128)(2,1)} %shard_map.107), calls=%async_computation.5 | async-start | bytes 1048576 | tf_op jit(solution)/shard_map/all_to_all | solution.py:40
  57.5 0.1 reshape_squeeze.3.strips
  57.6 2.5 %collective-permute-start = (bf16[8,32,512]{2,1,0:T(8,128)(2,1)S(1)}, bf16[8,32,512]{2,1,0:T(8,128)(2,1)S(1)}, u32[]{:S(2)}, u32[]{:S(2)}) collective-permute-start(bf16[8,32,512]{2,1,0:T(8,128)(2,1)S(1)} %reshape_squeeze.3.strips), channel_id=1, source_target_pairs={{0,64},{64,0},{1,65},{65,1},{2,66},{66,2},{3,67},{67,3},{4,68},{68... | collective-permute-start | bytes 786440 | tf_op jit(solution)/shard_map/ppermute | solution.py:289
  60.1 6.9 %collective-permute-done.near_strips = bf16[8,32,512]{2,1,0:T(8,128)(2,1)S(1)} collective-permute-done((bf16[8,32,512]{2,1,0:T(8,128)(2,1)S(1)}, bf16[8,32,512]{2,1,0:T(8,128)(2,1)S(1)}, u32[]{:S(2)}, u32[]{:S(2)}) %collective-permute-start) | collective-permute-done | bytes 262176 | tf_op jit(solution)/shard_map/ppermute | solution.py:289
  67.0 6.5 %all-to-all-done.5.residual = bf16[8,256,128]{2,1,0:T(8,128)(2,1)S(1)} async-done(((bf16[8,256,128]{2,1,0:T(8,128)(2,1)}), bf16[8,256,128]{2,1,0:T(8,128)(2,1)S(1)}, u32[]{:S(2)}, u32[]{:S(2)}) %all-to-all-start.5) | async-done | bytes 524320 | tf_op jit(solution)/shard_map/all_to_all | solution.py:40
  73.5 1.4 %shard_map.108 = f32[16,40,128]{2,1,0:T(8,128)} custom-call(s32[4,8]{1,0:T(4,128)S(1)} %bitcast.20, s32[4,8]{1,0:T(4,128)S(1)} %bitcast_convert_fusion.near_cols, bf16[8,32,512]{2,1,0:T(8,128)(2,1)S(1)} %reshape_squeeze.3.strips, bf16[8,32,512]{2,1,0:T(8,128)(2,1)S(1)} %collective-permute-done.near_strips, bf16[8,256,128]{2,1,0:T(8,128)(2,1)S(1)} %all-to-all-done.5.residual, ...), custom_call_target="tpu_custom_call" | custom-call | tf_op jit(solution)/shard_map/pallas_call | solution.py:333
  74.9 13.1 %all_to_all.36.got = f32[16,40,128]{2,1,0:T(8,128)S(1)} all-to-all(f32[16,40,128]{2,1,0:T(8,128)} %shard_map.108), channel_id=1, replica_groups=mesh['zh'=4,'zl'=2,'y'=8,'sep'=8] {'zl','sep'}, dimensions={0} | all-to-all | bytes 655360 | tf_op jit(solution)/shard_map/all_to_all | solution.py:40
  88.1 0.8 shard_map.109
  88.8 0.0 copy-start.1
  89.6 18.9 %conditional.1 = (bf16[64,8,256]{2,1,0:T(8,128)(2,1)S(1)}, bf16[64,256]{1,0:T(8,128)(2,1)S(1)}) conditional(s32[]{:T(128)} %bitcast.13, bf16[64,8,256]{2,1,0:T(8,128)(2,1)S(1)} %get-tuple-element.29, (f32[32,256]{1,0:T(8,128)}, bf16[8,72,256]{2,1,0:T(8,128)(2,1)S(1)}) %tuple.19), branch_computations={%region_0.0_spmd, %region_1.0_spmd} | conditional | flops 122880 | bytes 1540116 | solution.py:360
  89.6 18.9 %all_to_all.32 = bf16[64,8,256]{2,1,0:T(8,128)(2,1)S(1)} all-to-all(bf16[64,8,256]{2,1,0:T(8,128)(2,1)S(1)} %param), channel_id=1, replica_groups=mesh['zh'=4,'zl'=2,'y'=8,'sep'=8] {'zh','zl','y'}, dimensions={0} | all-to-all | bytes 524288 | tf_op jit(solution)/shard_map/cond/branch_0_fun/all_to_all | solution.py:40
  108.5 0.0 copy-done.2
  108.6 0.0 copy-done.3
  108.6 2.5 %shard_map.110 = f32[1536,256]{1,0:T(8,128)} custom-call(s32[1,1]{1,0:T(1,128)S(6)} %copy.15.count, s32[1,1]{1,0:T(1,128)} %get-tuple-element.27.over, s32[1,64]{1,0:T(1,128)S(1)} %copy-done.6, bf16[64,8,256]{2,1,0:T(8,128)(2,1)S(1)} %get-tuple-element.31.got, bf16[64,256]{1,0:T(8,128)(2,1)S(1)} %get-tuple-element.32.other, f32[64,256]{1,0:T(8,128)S(1)} %copy-done.2, ...), custom_call_target="tpu_custom_call" | custom-call | tf_op jit(solution)/shard_map/pallas_call | solution.py:361
  (15 shorter events, 0.0 us)
Async XLA Ops:
  1.3 22.8 %copy-start.4 = (f32[1,32,256]{2,1,0:T(8,128)S(1)}, f32[1,32,256]{2,1,0:T(8,128)}, u32[]{:S(2)}) copy-start(f32[1,32,256]{2,1,0:T(8,128)} %param.17) | copy-start | bytes 98308
  1.3 22.8 %copy-start.5 = (s32[8,1,1,4]{0,3,2,1:T(4,128)S(1)}, s32[8,1,1,4]{0,3,2,1:T(4,128)}, u32[]{:S(2)}) copy-start(s32[8,1,1,4]{0,3,2,1:T(4,128)} %param.19) | copy-start | bytes 388
  5.2 30.5 %copy-start.8 = (s32[1,1,64]{2,1,0:T(1,128)S(1)}, s32[1,1,64]{2,1,0:T(1,128)}, u32[]{:S(2)}) copy-start(s32[1,1,64]{2,1,0:T(1,128)} %param.14) | copy-start | bytes 772
  25.5 25.4 %all-to-all-start.4 = ((bf16[8,264,128]{2,1,0:T(8,128)(2,1)}), bf16[8,264,128]{2,1,0:T(8,128)(2,1)S(1)}, u32[]{:S(2)}, u32[]{:S(2)}) async-start(bf16[8,264,128]{2,1,0:T(8,128)(2,1)} %shard_map.105), calls=%async_computation.4 | async-start | bytes 1081344 | tf_op jit(solution)/shard_map/all_to_all | solution.py:40
  40.3 1.1 %copy-start = (f32[1536,256]{1,0:T(8,128)}, f32[1536,256]{1,0:T(8,128)S(1)}, u32[]{:S(2)}) copy-start(f32[1536,256]{1,0:T(8,128)S(1)} %get-tuple-element.35.base) | copy-start | bytes 4718596
  41.4 16.1 %copy-start.7 = (bf16[8,32,1,4,128]{4,3,2,1,0:T(4,128)(2,1)S(1)}, bf16[8,32,1,4,128]{4,3,2,1,0:T(4,128)(2,1)}, u32[]{:S(2)}) copy-start(bf16[8,32,1,4,128]{4,3,2,1,0:T(4,128)(2,1)} %param.18) | copy-start | bytes 786436
  51.7 21.8 %all-to-all-start.5 = ((bf16[8,256,128]{2,1,0:T(8,128)(2,1)}), bf16[8,256,128]{2,1,0:T(8,128)(2,1)S(1)}, u32[]{:S(2)}, u32[]{:S(2)}) async-start(bf16[8,256,128]{2,1,0:T(8,128)(2,1)} %shard_map.107), calls=%async_computation.5 | async-start | bytes 1048576 | tf_op jit(solution)/shard_map/all_to_all | solution.py:40
  57.6 9.4 %collective-permute-start = (bf16[8,32,512]{2,1,0:T(8,128)(2,1)S(1)}, bf16[8,32,512]{2,1,0:T(8,128)(2,1)S(1)}, u32[]{:S(2)}, u32[]{:S(2)}) collective-permute-start(bf16[8,32,512]{2,1,0:T(8,128)(2,1)S(1)} %reshape_squeeze.3.strips), channel_id=1, source_target_pairs={{0,64},{64,0},{1,65},{65,1},{2,66},{66,2},{3,67},{67,3},{4,68},{68... | collective-permute-start | bytes 786440 | tf_op jit(solution)/shard_map/ppermute | solution.py:289
  88.8 19.7 %copy-start.1 = (f32[1536,256]{1,0:T(8,128)S(1)}, f32[1536,256]{1,0:T(8,128)}, u32[]{:S(2)}) copy-start(f32[1536,256]{1,0:T(8,128)} %copy-done) | copy-start | bytes 4718596
  88.8 19.7 %copy-start.2 = (f32[64,256]{1,0:T(8,128)S(1)}, f32[64,256]{1,0:T(8,128)}, u32[]{:S(2)}) copy-start(f32[64,256]{1,0:T(8,128)} %get-tuple-element.33.taken) | copy-start | bytes 196612
  88.8 19.7 %copy-start.3 = (f32[64,128]{1,0:T(8,128)S(1)}, f32[64,128]{1,0:T(8,128)}, u32[]{:S(2)}) copy-start(f32[64,128]{1,0:T(8,128)} %get-tuple-element.34.same) | copy-start | bytes 98308
  88.9 19.7 %copy-start.6 = (s32[1,64]{1,0:T(1,128)S(1)}, s32[1,64]{1,0:T(1,128)}, u32[]{:S(2)}) copy-start(s32[1,64]{1,0:T(1,128)} %get-tuple-element.28.slots) | copy-start | bytes 772

commit v9 on v7

--- a/solution.py
+++ b/solution.py
@@ -160,6 +160,8 @@
     per_tile = TILE // strip
     zl = lax.axis_index("zl")
 
+    own_cols, other_cols = cols[...], near_cols[...]
+
     def tile(c):
         parts = n_y // per_tile
         y = (c % parts) * per_tile
@@ -169,7 +171,7 @@
     over = got[0, pl.ds(n_rows, EXTRA), :].astype(F32)
     for p in range(1, got.shape[0]):
         over = jnp.maximum(over, got[p, pl.ds(n_rows, EXTRA), :].astype(F32))
-    for which, wanted, rows in ((zl, cols, strips), (1 - zl, near_cols, near_strips)):
+    for which, wanted, rows in ((zl, own_cols, strips), (1 - zl, other_cols, near_strips)):
         for q in range(sections):
             total = None
             for k in range(0, per_row, 2):
@@ -330,8 +332,8 @@
     product = call(
         separator_kernel,
         shape((2 * n_sep, strip + EXTRA, half), F32),
-        [SMEM(), SMEM(), VMEM(), VMEM(), VMEM(), VMEM()],
-    )(tile_cols, near_cols, near(strips), near(near_strips), near(residual), near(asked))
+        [VMEM()] * 6,
+    )(near(tile_cols), near(near_cols), near(strips), near(near_strips), near(residual), near(asked))
     got = exchange(product, ("zl", "sep"))
     own, sent, over = call(
         solution_kernel,

time: 111 us -> 110 us (level)
  no operation moved by 1% of the time
where the time goes in v9:
time: 110 us
  blocking collectives  64 us (58%)
  Pallas kernels  14.7 us (13%)
  waiting for transfers between devices  14.4 us (13%)
  starting transfers between devices  12.6 us (11%)
  between operations  2.1 us (2%)
  local copies, waits for them, and re-layouts  1.28 us (1%)
    all_to_all x3, blocking collectives, exchange(): return lax.all_to_all(value, axes, split_axis=0, concat_axis=0, tiled=True)  64 us
    all_to_all x2, starting transfers between devices, exchange(): return lax.all_to_all(value, axes, split_axis=0, concat_axis=0, tiled=True)  10.1 us
    all_to_all x2, waiting for transfers between devices, exchange(): return lax.all_to_all(value, axes, split_axis=0, concat_axis=0, tiled=True)  8.66 us
    ppermute x1, waiting for transfers between devices, body(): near_strips = lax.ppermute(strips, 'zl', [(0, 1), (1, 0)])  5.76 us
    pallas_call x1, Pallas kernels, body(): call(functools.partial(forward_kernel, strip=strip), (shape((leaf_rows, w...  3.95 us
    pallas_call x1, Pallas kernels, body(): call(transposed_kernel, (pltpu.VMEM((leaf_rows, width), F32), pltpu.VMEM(...  3.89 us
    ppermute x1, starting transfers between devices, body(): near_strips = lax.ppermute(strips, 'zl', [(0, 1), (1, 0)])  2.47 us
    pallas_call x1, Pallas kernels, body(): call(finish_kernel, shape((leaf_rows, width), F32), [SMEM()] * 2 + [VMEM(...  2.45 us
  transfers between devices with their start and end apart: 3, of which 3 were waited for; matrix products, arithmetic and copies ran while one was open for 1% of the time, Pallas kernels for 4%

profile of v9, /device:TPU:8, one launch (start us, length us, event | category | flops | bytes accessed | tf_op | source)
XLA Modules:
  0.0 109.7 jit_solution(11973808775150558883)
XLA Ops:
  1.3 4.0 %shard_map.104 = (bf16[1536,256]{1,0:T(8,128)(2,1)}, bf16[8,72,256]{2,1,0:T(8,128)(2,1)}, f32[64,256]{1,0:T(8,128)}, s32[1,64]{1,0:T(1,128)}) custom-call(s32[4,12]{1,0:T(4,128)} %bitcast.26, s32[1,64]{1,0:T(1,128)} %bitcast.30, s32[1,64]{1,0:T(1,128)} %bitcast.28, s32[1,1]{1,0:T(1,128)S(6)} %copy.15.count, f32[1536,256]{1,0:T(8,128)} %bitcast.23, ...), custom_call_target="tpu_custom_call" | custom-call | tf_op jit(solution)/shard_map/pallas_call | solution.py:290
  5.2 18.7 %all_to_all.35.got = bf16[8,72,256]{2,1,0:T(8,128)(2,1)S(1)} all-to-all(bf16[8,72,256]{2,1,0:T(8,128)(2,1)} %get-tuple-element.21), channel_id=1, replica_groups=mesh['zh'=4,'zl'=2,'y'=8,'sep'=8] {'y'}, dimensions={0} | all-to-all | bytes 589824 | tf_op jit(solution)/shard_map/all_to_all | solution.py:40
  23.9 1.4 %shard_map.105 = bf16[8,264,128]{2,1,0:T(8,128)(2,1)} custom-call(bf16[8,72,256]{2,1,0:T(8,128)(2,1)S(1)} %all_to_all.35.got, f32[32,256]{1,0:T(8,128)S(1)} %bitcast.18, s32[4,8]{1,0:T(4,128)S(1)} %bitcast.19), custom_call_target="tpu_custom_call" | custom-call | tf_op jit(solution)/shard_map/pallas_call | solution.py:308
  25.3 25.5 %all_to_all.36.got.asked = bf16[8,264,128]{2,1,0:T(8,128)(2,1)S(1)} all-to-all(bf16[8,264,128]{2,1,0:T(8,128)(2,1)} %shard_map.105), channel_id=1, replica_groups=mesh['zh'=4,'zl'=2,'y'=8,'sep'=8] {'zh','zl'}, dimensions={0} | all-to-all | bytes 1081344 | tf_op jit(solution)/shard_map/all_to_all | solution.py:40
  50.9 0.9 shard_map.106
  51.7 5.7 %all-to-all-start.5 = ((bf16[8,256,128]{2,1,0:T(8,128)(2,1)}), bf16[8,256,128]{2,1,0:T(8,128)(2,1)S(1)}, u32[]{:S(2)}, u32[]{:S(2)}) async-start(bf16[8,256,128]{2,1,0:T(8,128)(2,1)} %shard_map.106), calls=%async_computation.5 | async-start | bytes 1048576 | tf_op jit(solution)/shard_map/all_to_all | solution.py:40
  57.5 0.1 reshape_squeeze.3.strips
  57.6 2.5 %collective-permute-start = (bf16[8,32,512]{2,1,0:T(8,128)(2,1)S(1)}, bf16[8,32,512]{2,1,0:T(8,128)(2,1)S(1)}, u32[]{:S(2)}, u32[]{:S(2)}) collective-permute-start(bf16[8,32,512]{2,1,0:T(8,128)(2,1)S(1)} %reshape_squeeze.3.strips), channel_id=1, source_target_pairs={{0,64},{64,0},{1,65},{65,1},{2,66},{66,2},{3,67},{67,3},{4,68},{68... | collective-permute-start | bytes 786440 | tf_op jit(solution)/shard_map/ppermute | solution.py:289
  60.1 5.8 %collective-permute-done.near_strips = bf16[8,32,512]{2,1,0:T(8,128)(2,1)S(1)} collective-permute-done((bf16[8,32,512]{2,1,0:T(8,128)(2,1)S(1)}, bf16[8,32,512]{2,1,0:T(8,128)(2,1)S(1)}, u32[]{:S(2)}, u32[]{:S(2)}) %collective-permute-start) | collective-permute-done | bytes 262176 | tf_op jit(solution)/shard_map/ppermute | solution.py:289
  65.8 5.6 %all-to-all-done.5.residual = bf16[8,256,128]{2,1,0:T(8,128)(2,1)S(1)} async-done(((bf16[8,256,128]{2,1,0:T(8,128)(2,1)}), bf16[8,256,128]{2,1,0:T(8,128)(2,1)S(1)}, u32[]{:S(2)}, u32[]{:S(2)}) %all-to-all-start.5) | async-done | bytes 524320 | tf_op jit(solution)/shard_map/all_to_all | solution.py:40
  71.4 1.4 %shard_map.107 = f32[16,40,128]{2,1,0:T(8,128)} custom-call(s32[4,8]{1,0:T(4,128)S(1)} %bitcast.20, s32[4,8]{1,0:T(4,128)S(1)} %bitcast_convert_fusion.near_cols, bf16[8,32,512]{2,1,0:T(8,128)(2,1)S(1)} %reshape_squeeze.3.strips, bf16[8,32,512]{2,1,0:T(8,128)(2,1)S(1)} %collective-permute-done.near_strips, bf16[8,256,128]{2,1,0:T(8,128)(2,1)S(1)} %all-to-all-done.5.residual, ...), custom_call_target="tpu_custom_call" | custom-call | tf_op jit(solution)/shard_map/pallas_call | solution.py:332
  72.8 4.4 %all-to-all-start.6 = ((f32[16,40,128]{2,1,0:T(8,128)}), f32[16,40,128]{2,1,0:T(8,128)S(1)}, u32[]{:S(2)}, u32[]{:S(2)}) async-start(f32[16,40,128]{2,1,0:T(8,128)} %shard_map.107), calls=%async_computation.6 | async-start | bytes 655360 | tf_op jit(solution)/shard_map/all_to_all | solution.py:40
  77.2 0.0 copy-done.8
  77.2 0.6 pad_add_fusion.row_lanes
  77.8 3.9 %shard_map.109 = (f32[1536,256]{1,0:T(8,128)S(1)}, bf16[1536,128]{1,0:T(8,128)(2,1)S(1)}, f32[64,128]{1,0:T(8,128)}) custom-call(s32[4,12]{1,0:T(4,128)} %bitcast.27, s32[1,1]{1,0:T(1,128)S(6)} %copy.15.count, bf16[1536,256]{1,0:T(8,128)(2,1)} %get-tuple-element.29.forward, bf16[12,4,128,128]{3,2,1,0:T(8,128)(2,1)} %bitcast.22, s32[1,128]{1,0:T(1,128)} %pad_add_fusion.row_lanes), custom_call_target="tpu_custom_call" | custom-call | tf_op jit(solution)/shard_map/pallas_call | solution.py:322
  81.7 1.1 %copy-done = f32[1536,256]{1,0:T(8,128)} copy-done((f32[1536,256]{1,0:T(8,128)}, f32[1536,256]{1,0:T(8,128)S(1)}, u32[]{:S(2)}) %copy-start) | copy-done | bytes 1572888
  82.8 3.1 %all-to-all-done.6.got = f32[16,40,128]{2,1,0:T(8,128)S(1)} async-done(((f32[16,40,128]{2,1,0:T(8,128)}), f32[16,40,128]{2,1,0:T(8,128)S(1)}, u32[]{:S(2)}, u32[]{:S(2)}) %all-to-all-start.6) | async-done | bytes 327712 | tf_op jit(solution)/shard_map/all_to_all | solution.py:40
  85.9 0.8 shard_map.108
  86.7 0.0 copy-start.1
  87.4 19.8 %conditional.1 = (bf16[64,8,256]{2,1,0:T(8,128)(2,1)S(1)}, bf16[64,256]{1,0:T(8,128)(2,1)S(1)}) conditional(s32[]{:T(128)} %bitcast.12, bf16[64,8,256]{2,1,0:T(8,128)(2,1)S(1)} %get-tuple-element.24, (f32[32,256]{1,0:T(8,128)}, bf16[8,72,256]{2,1,0:T(8,128)(2,1)S(1)}) %tuple.17), branch_computations={%region_0.0_spmd, %region_1.0_spmd} | conditional | flops 122880 | bytes 1540116 | solution.py:359
  87.4 19.8 %all_to_all.32 = bf16[64,8,256]{2,1,0:T(8,128)(2,1)S(1)} all-to-all(bf16[64,8,256]{2,1,0:T(8,128)(2,1)S(1)} %param), channel_id=1, replica_groups=mesh['zh'=4,'zl'=2,'y'=8,'sep'=8] {'zh','zl','y'}, dimensions={0} | all-to-all | bytes 524288 | tf_op jit(solution)/shard_map/cond/branch_0_fun/all_to_all | solution.py:40
  107.2 0.0 copy-done.2
  107.2 0.0 copy-done.3
  107.3 2.4 %shard_map.110 = f32[1536,256]{1,0:T(8,128)} custom-call(s32[1,1]{1,0:T(1,128)S(6)} %copy.15.count, s32[1,1]{1,0:T(1,128)} %get-tuple-element.22.over, s32[1,64]{1,0:T(1,128)S(1)} %copy-done.6, bf16[64,8,256]{2,1,0:T(8,128)(2,1)S(1)} %get-tuple-element.26.got, bf16[64,256]{1,0:T(8,128)(2,1)S(1)} %get-tuple-element.27.other, f32[64,256]{1,0:T(8,128)S(1)} %copy-done.2, ...), custom_call_target="tpu_custom_call" | custom-call | tf_op jit(solution)/shard_map/pallas_call | solution.py:360
  (15 shorter events, 0.0 us)
Async XLA Ops:
  1.3 22.6 %copy-start.4 = (f32[1,32,256]{2,1,0:T(8,128)S(1)}, f32[1,32,256]{2,1,0:T(8,128)}, u32[]{:S(2)}) copy-start(f32[1,32,256]{2,1,0:T(8,128)} %param.17) | copy-start | bytes 98308
  1.3 22.6 %copy-start.5 = (s32[8,1,1,4]{0,3,2,1:T(4,128)S(1)}, s32[8,1,1,4]{0,3,2,1:T(4,128)}, u32[]{:S(2)}) copy-start(s32[8,1,1,4]{0,3,2,1:T(4,128)} %param.19) | copy-start | bytes 388
  25.3 32.1 %copy-start.7 = (bf16[8,32,1,4,128]{4,3,2,1,0:T(4,128)(2,1)S(1)}, bf16[8,32,1,4,128]{4,3,2,1,0:T(4,128)(2,1)}, u32[]{:S(2)}) copy-start(bf16[8,32,1,4,128]{4,3,2,1,0:T(4,128)(2,1)} %param.18) | copy-start | bytes 786436
  51.7 19.7 %all-to-all-start.5 = ((bf16[8,256,128]{2,1,0:T(8,128)(2,1)}), bf16[8,256,128]{2,1,0:T(8,128)(2,1)S(1)}, u32[]{:S(2)}, u32[]{:S(2)}) async-start(bf16[8,256,128]{2,1,0:T(8,128)(2,1)} %shard_map.106), calls=%async_computation.5 | async-start | bytes 1048576 | tf_op jit(solution)/shard_map/all_to_all | solution.py:40
  57.5 19.7 %copy-start.8 = (s32[1,1,64]{2,1,0:T(1,128)S(1)}, s32[1,1,64]{2,1,0:T(1,128)}, u32[]{:S(2)}) copy-start(s32[1,1,64]{2,1,0:T(1,128)} %param.14) | copy-start | bytes 772
  57.6 8.3 %collective-permute-start = (bf16[8,32,512]{2,1,0:T(8,128)(2,1)S(1)}, bf16[8,32,512]{2,1,0:T(8,128)(2,1)S(1)}, u32[]{:S(2)}, u32[]{:S(2)}) collective-permute-start(bf16[8,32,512]{2,1,0:T(8,128)(2,1)S(1)} %reshape_squeeze.3.strips), channel_id=1, source_target_pairs={{0,64},{64,0},{1,65},{65,1},{2,66},{66,2},{3,67},{67,3},{4,68},{68... | collective-permute-start | bytes 786440 | tf_op jit(solution)/shard_map/ppermute | solution.py:289
  72.8 13.1 %all-to-all-start.6 = ((f32[16,40,128]{2,1,0:T(8,128)}), f32[16,40,128]{2,1,0:T(8,128)S(1)}, u32[]{:S(2)}, u32[]{:S(2)}) async-start(f32[16,40,128]{2,1,0:T(8,128)} %shard_map.107), calls=%async_computation.6 | async-start | bytes 655360 | tf_op jit(solution)/shard_map/all_to_all | solution.py:40
  81.7 1.1 %copy-start = (f32[1536,256]{1,0:T(8,128)}, f32[1536,256]{1,0:T(8,128)S(1)}, u32[]{:S(2)}) copy-start(f32[1536,256]{1,0:T(8,128)S(1)} %get-tuple-element.31.base) | copy-start | bytes 4718596
  86.7 20.5 %copy-start.1 = (f32[1536,256]{1,0:T(8,128)S(1)}, f32[1536,256]{1,0:T(8,128)}, u32[]{:S(2)}) copy-start(f32[1536,256]{1,0:T(8,128)} %copy-done) | copy-start | bytes 4718596
  86.7 20.5 %copy-start.2 = (f32[64,256]{1,0:T(8,128)S(1)}, f32[64,256]{1,0:T(8,128)}, u32[]{:S(2)}) copy-start(f32[64,256]{1,0:T(8,128)} %get-tuple-element.28.taken) | copy-start | bytes 196612
  86.7 20.5 %copy-start.3 = (f32[64,128]{1,0:T(8,128)S(1)}, f32[64,128]{1,0:T(8,128)}, u32[]{:S(2)}) copy-start(f32[64,128]{1,0:T(8,128)} %get-tuple-element.30.same) | copy-start | bytes 98308
  86.7 20.5 %copy-start.6 = (s32[1,64]{1,0:T(1,128)S(1)}, s32[1,64]{1,0:T(1,128)}, u32[]{:S(2)}) copy-start(s32[1,64]{1,0:T(1,128)} %get-tuple-element.23.slots) | copy-start | bytes 772
